TPU v7x, 32 devices: a whole 2x2x4 slice. The times are simulated.
32 devices in a mesh: dp: 4 (over y, x), sp: 8 (over z, core).
Axes of the slice: x: 2, y: 2, z: 4, core: 2. Of those that a mesh axis runs over, the one named last changes fastest.
Arguments:
- inputs: bfloat16 [3, 8, 8, 200, 768], P(None, 'dp', None, 'sp'), may hold values from -6 to 6
- cotangent: bfloat16 [3, 8, 8, 200, 768], P(None, 'dp', None, 'sp'), may hold values from -6 to 6
- params: bfloat16 [10043392], P(('dp', 'sp'))
- clip_counts: int32 [3, 4], P(None, 'dp'), may hold values from 1 to 2, as said below
- slot_live: int32 [3, 8, 200], P(None, 'dp', 'sp'), may hold values from 0 to 1, as said below
Outputs:
- layer_out: bfloat16 [3, 8, 8, 200, 768], P(None, 'dp', None, 'sp')
- input_grad: bfloat16 [3, 8, 8, 200, 768], P(None, 'dp', None, 'sp')
- param_grad: float32 [10043392], P(('dp', 'sp'))
Inputs may be any that keep to these rules, and one draw needn't show every extreme that they name: `slot_live`: each clip slot has exactly 196 place slots with value 1. In each micro-batch, group g uses its clip slots 0 to clip_counts[m, g] - 1; some group of some micro-batch uses all 2.
All inputs are finite; a program needn't handle non-finite values.
Results may differ from a plain program's by a relative error of at most 0.018.
Values may be sent and summed in bfloat16 or wider, within the bound.
No kernel may reach another device: no remote copies, remote signals or barrier semaphores. Data moves between devices by JAX's collectives and lax.ppermute only.
A program may use at most 384 MiB of HBM per device.

v0:
```python
import math

import jax
import jax.numpy as jnp
from jax import lax
from jax.sharding import PartitionSpec as P

H = 12
FF = 3072


EPS = 1e-06
MASKED = -1000000000.0


def segment_shapes(model_width, hidden_width):
    return [
        (model_width,),
        (model_width,),
        (model_width, 3 * model_width),
        (model_width,),
        (model_width,),
        (model_width, model_width),
        (model_width,),
        (model_width, model_width),
        (model_width,),
        (model_width,),
        (model_width,),
        (model_width, 3 * model_width),
        (model_width,),
        (model_width,),
        (model_width, model_width),
        (model_width,),
        (model_width,),
        (model_width,),
        (model_width, hidden_width),
        (hidden_width,),
        (hidden_width, model_width),
        (model_width,),
    ]


def unpack(flat_params, model_width, hidden_width):
    pieces = []
    offset = 0
    for layout in segment_shapes(model_width, hidden_width):
        length = math.prod(layout)
        pieces.append(flat_params[offset : offset + length].reshape(layout))
        offset = offset + length
    return pieces


def pack_grads(pieces, full_length):
    flat_grads = jnp.concatenate([piece.reshape(-1) for piece in pieces])
    padding = jnp.zeros((full_length - flat_grads.shape[0],), jnp.float32)
    return jnp.concatenate([flat_grads, padding])


def layer_norm(values, norm_gain, norm_shift):
    center = values - jnp.mean(values, axis=-1, keepdims=True)
    spread = jnp.mean(center * center, axis=-1, keepdims=True)
    return center * lax.rsqrt(spread + EPS) * norm_gain + norm_shift


def gelu_exact(values):
    return jax.nn.gelu(values, approximate=False)


def product(left_side, right_side):
    return jnp.dot(left_side, right_side, preferred_element_type=jnp.float32)


def product_back(grad_rows, weight):
    return jnp.einsum("...n,kn->...k", grad_rows, weight, preferred_element_type=jnp.float32)


def weight_grad(left_side, grad_rows):
    left_flat = left_side.reshape(-1, left_side.shape[-1])
    grad_flat = grad_rows.reshape(-1, grad_rows.shape[-1])
    return jnp.einsum("rk,rn->kn", left_flat, grad_flat, preferred_element_type=jnp.float32)


def row_sum(grad_rows):
    return jnp.sum(grad_rows.astype(jnp.float32).reshape(-1, grad_rows.shape[-1]), axis=0)


def split_heads(packed, head_count):
    model_width = packed.shape[-1] // 3
    leading = packed.shape[:-1]
    head_size = model_width // head_count
    return [
        packed[..., portion * model_width : (portion + 1) * model_width].reshape(
            leading + (head_count, head_size)
        )
        for portion in range(3)
    ]


def masked_scores(query_rows, key_rows, key_live):
    score_scale = query_rows.shape[-1] ** (-0.5)
    scores = (
        jnp.einsum("bqhd,bkhd->bhqk", query_rows, key_rows, preferred_element_type=jnp.float32)
        * score_scale
    )
    if key_live is not None:
        scores = jnp.where(key_live[:, None, None, :], scores, MASKED)
    return scores


def attention_forward(query_rows, key_rows, value_rows, key_live):
    scores = masked_scores(query_rows, key_rows, key_live)
    row_max = jnp.max(scores, axis=-1, keepdims=True)
    row_total = jnp.sum(jnp.exp(scores - row_max), axis=-1, keepdims=True)
    log_total = row_max + jnp.log(row_total)
    softmax_rows = jnp.exp(scores - log_total)
    mixed_rows = jnp.einsum(
        "bhqk,bkhd->bqhd",
        softmax_rows.astype(jnp.bfloat16),
        value_rows,
        preferred_element_type=jnp.float32,
    )
    return (mixed_rows, log_total)


def attention_backward(query_rows, key_rows, value_rows, log_total, key_live, grad_out):
    score_scale = query_rows.shape[-1] ** (-0.5)
    scores = masked_scores(query_rows, key_rows, key_live)
    softmax_rows = jnp.exp(scores - log_total)
    grad_soft = jnp.einsum(
        "bqhd,bkhd->bhqk", grad_out, value_rows, preferred_element_type=jnp.float32
    )
    grad_value = jnp.einsum(
        "bhqk,bqhd->bkhd",
        softmax_rows.astype(jnp.bfloat16),
        grad_out,
        preferred_element_type=jnp.float32,
    )
    grad_scores = softmax_rows * (
        grad_soft - jnp.sum(softmax_rows * grad_soft, axis=-1, keepdims=True)
    )
    grad_scores = grad_scores.astype(jnp.bfloat16)
    grad_query = (
        jnp.einsum("bhqk,bkhd->bqhd", grad_scores, key_rows, preferred_element_type=jnp.float32)
        * score_scale
    )
    grad_key = (
        jnp.einsum("bhqk,bqhd->bkhd", grad_scores, query_rows, preferred_element_type=jnp.float32)
        * score_scale
    )
    return (grad_query, grad_key, grad_value)


def attend_forward(normed, weight, query_bias, value_bias, key_live, head_count):
    bias_all = jnp.concatenate([query_bias, jnp.zeros_like(query_bias), value_bias])
    packed = (product(normed, weight) + bias_all).astype(jnp.bfloat16)
    query_rows, key_rows, value_rows = split_heads(packed, head_count)
    mixed_rows, log_total = attention_forward(query_rows, key_rows, value_rows, key_live)
    merged = mixed_rows.reshape(normed.shape).astype(jnp.bfloat16)
    return (merged, (packed, log_total))


def attend_backward(normed, weight, kept_rows, key_live, grad_merged, head_count):
    packed, log_total = kept_rows
    query_rows, key_rows, value_rows = split_heads(packed, head_count)
    grad_heads = grad_merged.reshape(query_rows.shape)
    grad_query, grad_key, grad_value = attention_backward(
        query_rows, key_rows, value_rows, log_total, key_live, grad_heads
    )
    flat_shape = normed.shape
    grad_packed = jnp.concatenate(
        [
            grad_query.reshape(flat_shape),
            grad_key.reshape(flat_shape),
            grad_value.reshape(flat_shape),
        ],
        axis=-1,
    ).astype(jnp.bfloat16)
    model_width = normed.shape[-1]
    grad_weight = weight_grad(normed, grad_packed)
    column_sums = row_sum(grad_packed)
    grad_normed = product_back(grad_packed, weight)
    return (grad_normed, grad_weight, column_sums[:model_width], column_sums[2 * model_width :])


def temporal_forward(token_rows, pieces, head_count):
    (
        norm_gain,
        norm_shift,
        qkv_weight,
        query_bias,
        value_bias,
        out_weight,
        out_bias,
        fc_weight,
        fc_bias,
    ) = pieces
    normed = layer_norm(token_rows, norm_gain, norm_shift).astype(jnp.bfloat16)
    merged, kept_rows = attend_forward(normed, qkv_weight, query_bias, value_bias, None, head_count)
    mixed_rows = (product(merged, out_weight) + out_bias).astype(jnp.bfloat16)
    result = token_rows + product(mixed_rows, fc_weight) + fc_bias
    return (result, (normed, merged, mixed_rows, kept_rows))


def temporal_backward(token_rows, pieces, saved, grad_result, head_count):
    (
        norm_gain,
        norm_shift,
        qkv_weight,
        query_bias,
        value_bias,
        out_weight,
        out_bias,
        fc_weight,
        fc_bias,
    ) = pieces
    normed, merged, mixed_rows, kept_rows = saved
    grad_fc = weight_grad(mixed_rows, grad_result)
    grad_fc_bias = row_sum(grad_result)
    grad_mixed = product_back(grad_result, fc_weight).astype(jnp.bfloat16)
    grad_out = weight_grad(merged, grad_mixed)
    grad_out_bias = row_sum(grad_mixed)
    grad_merged = product_back(grad_mixed, out_weight).astype(jnp.bfloat16)
    grad_normed, grad_qkv, grad_query_bias, grad_value_bias = attend_backward(
        normed, qkv_weight, kept_rows, None, grad_merged, head_count
    )
    unused, norm_pull = jax.vjp(layer_norm, token_rows, norm_gain, norm_shift)
    grad_tokens, grad_gain, grad_shift = norm_pull(grad_normed)
    grads = [
        grad_gain,
        grad_shift,
        grad_qkv,
        grad_query_bias,
        grad_value_bias,
        grad_out,
        grad_out_bias,
        grad_fc,
        grad_fc_bias,
    ]
    return (grad_result.astype(jnp.float32) + grad_tokens, grads)


def frame_forward(frame_rows, key_live, pieces, head_count):
    (
        norm_gain,
        norm_shift,
        qkv_weight,
        query_bias,
        value_bias,
        out_weight,
        out_bias,
        mlp_gain,
        mlp_shift,
        up_weight,
        up_bias,
        down_weight,
        down_bias,
    ) = pieces
    start_rows = frame_rows.astype(jnp.float32)
    normed = layer_norm(start_rows, norm_gain, norm_shift).astype(jnp.bfloat16)
    merged, kept_rows = attend_forward(
        normed, qkv_weight, query_bias, value_bias, key_live, head_count
    )
    middle = start_rows + product(merged, out_weight) + out_bias
    normed_mlp = layer_norm(middle, mlp_gain, mlp_shift).astype(jnp.bfloat16)
    upper = product(normed_mlp, up_weight) + up_bias
    active = gelu_exact(upper).astype(jnp.bfloat16)
    result = middle + product(active, down_weight) + down_bias
    return (
        result.astype(jnp.bfloat16),
        (start_rows, normed, merged, kept_rows, middle, normed_mlp, upper, active),
    )


def frame_backward(key_live, pieces, saved, grad_result, head_count):
    (
        norm_gain,
        norm_shift,
        qkv_weight,
        query_bias,
        value_bias,
        out_weight,
        out_bias,
        mlp_gain,
        mlp_shift,
        up_weight,
        up_bias,
        down_weight,
        down_bias,
    ) = pieces
    start_rows, normed, merged, kept_rows, middle, normed_mlp, upper, active = saved
    grad_down = weight_grad(active, grad_result)
    grad_down_bias = row_sum(grad_result)
    grad_active = product_back(grad_result, down_weight)
    unused, gelu_pull = jax.vjp(gelu_exact, upper)
    grad_upper = gelu_pull(grad_active)[0].astype(jnp.bfloat16)
    grad_up = weight_grad(normed_mlp, grad_upper)
    grad_up_bias = row_sum(grad_upper)
    grad_normed_mlp = product_back(grad_upper, up_weight)
    unused, mlp_pull = jax.vjp(layer_norm, middle, mlp_gain, mlp_shift)
    grad_middle_norm, grad_mlp_gain, grad_mlp_shift = mlp_pull(grad_normed_mlp)
    grad_middle = grad_result.astype(jnp.float32) + grad_middle_norm
    grad_branch = grad_middle.astype(jnp.bfloat16)
    grad_out = weight_grad(merged, grad_branch)
    grad_out_bias = row_sum(grad_branch)
    grad_merged = product_back(grad_branch, out_weight).astype(jnp.bfloat16)
    grad_normed, grad_qkv, grad_query_bias, grad_value_bias = attend_backward(
        normed, qkv_weight, kept_rows, key_live, grad_merged, head_count
    )
    unused, first_pull = jax.vjp(layer_norm, start_rows, norm_gain, norm_shift)
    grad_start_norm, grad_gain, grad_shift = first_pull(grad_normed)
    grads = [
        grad_gain,
        grad_shift,
        grad_qkv,
        grad_query_bias,
        grad_value_bias,
        grad_out,
        grad_out_bias,
        grad_mlp_gain,
        grad_mlp_shift,
        grad_up,
        grad_up_bias,
        grad_down,
        grad_down_bias,
    ]
    return ((grad_middle + grad_start_norm).astype(jnp.bfloat16), grads)


def shards(inputs, cotangent, params, clip_counts, slot_live):
    micro_count, clip_slots, frame_count, place_slots, model_width = inputs.shape
    full_length = params.shape[0] * lax.axis_size(("dp", "sp"))
    totals = None
    outputs = []
    input_grads = []
    for micro_step in range(micro_count):
        gathered = lax.all_gather(params, ("dp", "sp"), axis=0, tiled=True)
        raw_pieces = unpack(gathered, model_width, FF)
        pieces = [piece.astype(jnp.float32) if piece.ndim == 1 else piece for piece in raw_pieces]
        time_pieces = pieces[:9]
        frame_pieces = pieces[9:]
        in_use = (jnp.arange(clip_slots, dtype=jnp.int32) < clip_counts[micro_step, 0]).astype(
            jnp.float32
        )
        live_mask = slot_live[micro_step].astype(jnp.float32) * in_use[:, None]
        live_low = live_mask.astype(jnp.bfloat16)
        token_rows = jnp.swapaxes(inputs[micro_step].astype(jnp.float32), 1, 2).reshape(
            clip_slots * place_slots, frame_count, model_width
        )
        first_rows, time_saved = temporal_forward(token_rows, time_pieces, H)
        sent_rows = jnp.swapaxes(
            first_rows.reshape(clip_slots, place_slots, frame_count, model_width), 1, 2
        )
        sent_rows = sent_rows.astype(jnp.bfloat16).reshape(
            clip_slots * frame_count, place_slots, model_width
        )
        live_sent = jnp.broadcast_to(
            live_low[:, None, :], (clip_slots, frame_count, place_slots)
        ).reshape(clip_slots * frame_count, place_slots)
        masked_cot = (cotangent[micro_step] * live_low[:, None, :, None]).reshape(
            clip_slots * frame_count, place_slots, model_width
        )
        frame_rows, frame_live = (
            lax.all_to_all(sent_rows, "sp", split_axis=0, concat_axis=1, tiled=True),
            lax.all_to_all(live_sent, "sp", split_axis=0, concat_axis=1, tiled=True),
        )
        key_live = frame_live > 0.5
        frame_out, frame_saved = frame_forward(frame_rows, key_live, frame_pieces, H)
        returned = lax.all_to_all(frame_out, "sp", split_axis=1, concat_axis=0, tiled=True)
        outputs.append(
            returned.reshape(clip_slots, frame_count, place_slots, model_width)
            * live_low[:, None, :, None]
        )
        frame_cot = lax.all_to_all(masked_cot, "sp", split_axis=0, concat_axis=1, tiled=True)
        grad_frame, frame_grads = frame_backward(key_live, frame_pieces, frame_saved, frame_cot, H)
        grad_first = lax.all_to_all(grad_frame, "sp", split_axis=1, concat_axis=0, tiled=True)
        grad_time = jnp.swapaxes(
            grad_first.reshape(clip_slots, frame_count, place_slots, model_width), 1, 2
        ).reshape(clip_slots * place_slots, frame_count, model_width)
        grad_tokens, time_grads = temporal_backward(
            token_rows, time_pieces, time_saved, grad_time, H
        )
        input_grads.append(
            jnp.swapaxes(
                grad_tokens.reshape(clip_slots, place_slots, frame_count, model_width), 1, 2
            ).astype(jnp.bfloat16)
        )
        step_grads = time_grads + frame_grads
        if totals is None:
            totals = step_grads
        else:
            totals = [older + newer for older, newer in zip(totals, step_grads)]
    flat_grads = pack_grads(totals, full_length)
    param_grad = lax.psum_scatter(flat_grads, ("dp", "sp"), scatter_dimension=0, tiled=True)
    return (jnp.stack(outputs), jnp.stack(input_grads), param_grad)


def solution(mesh):
    placed = (
        P(None, "dp", None, "sp", None),
        P(None, "dp", None, "sp", None),
        P(("dp", "sp")),
        P(None, "dp"),
        P(None, "dp", "sp"),
    )
    return jax.shard_map(
        shards,
        mesh=mesh,
        in_specs=placed,
        out_specs=(
            P(None, "dp", None, "sp", None),
            P(None, "dp", None, "sp", None),
            P(("dp", "sp")),
        ),
        check_vma=False,
    )
```

profile of v0, /device:TPU:0, one launch (start us, length us, event | category | flops | bytes accessed | tf_op | source)
XLA Modules:
  0.0 2345.1 jit_solution(2083524142388841629)
XLA Ops:
  7.2 7.6 reshape.1244
  55.8 32.1 %all-to-all-done.11 = bf16[16,25,768]{2,1,0:T(8,128)(2,1)S(1)} async-done(((bf16[16,25,768]{2,1,0:T(8,128)(2,1)}), bf16[16,25,768]{2,1,0:T(8,128)(2,1)S(1)}, u32[]{:S(2)}, u32[]{:S(2)}) %all-to-all-start.11) | async-done | bytes 614432 | tf_op jit(solution)/shard_map/all_to_all | solution.py:373
  100.4 32.8 %all-to-all-done.13 = bf16[16,25,768]{2,1,0:T(8,128)(2,1)S(1)} async-done(((bf16[16,25,768]{2,1,0:T(8,128)(2,1)}), bf16[16,25,768]{2,1,0:T(8,128)(2,1)S(1)}, u32[]{:S(2)}, u32[]{:S(2)}) %all-to-all-start.13) | async-done | bytes 614432 | tf_op jit(solution)/shard_map/all_to_all | solution.py:373
  177.3 103.2 %all-gather.3.cloned.1.call-done = bf16[32,1,313856]{2,1,0:T(2,128)(2,1)} async-done(((bf16[1,1,313856]{2,1,0:T(2,128)(2,1)}), bf16[32,1,313856]{2,1,0:T(2,128)(2,1)}) %all-gather.3.cloned.1.call-update) | async-done | bytes 20086800 | tf_op jit(solution)/shard_map/all_gather | solution.py:336
  280.5 348.8 %reduce.27 = bf16[32,313856]{1,0:T(8,128)(2,1)} reduce(bf16[32,1,313856]{2,1,0:T(2,128)(2,1)} %all-gather.3.cloned.1.call-done, bf16[]{:T(256)} %constant.128), dimensions={1}, to_apply=%all-gather.reduce_sub_computation | reduce | bytes 40173568 | tf_op jit(solution)/shard_map/all_gather | solution.py:336
  629.3 48.6 %reshape.1245 = bf16[10043392]{0:T(1024)(128)(2,1)} reshape(bf16[32,313856]{1,0:T(8,128)(2,1)} %reduce.27) | data formatting | bytes 40173568
  688.4 9.2 fusion.216
  702.8 7.8 reshape.1246
  787.2 9.3 reshape.1252
  811.7 8.2 reshape.1251
  836.3 9.6 all-to-all-done
  924.6 14.8 fusion.67
  939.4 38.4 %multiply_convert_fusion.5 = (bf16[2,200,3072]{2,1,0:T(8,128)(2,1)}, f32[2,200,3072]{2,1,0:T(8,128)S(1)}, bf16[2,200,3072]{2,1,0:T(8,128)(2,1)}, f32[2,200,3072]...) fusion(f32[2,200,3072]{2,1,0:T(8,128)} %get-tuple-element.213, f32[3072]{0:T(1024)S(1)} %copy-done.229, ...), kind=kLoop, calls=%fused_computation.71 | loop fusion | flops 259276800 | bytes 40562688 | tf_op jit(solution)/shard_map/convert_element_type | solution.py:266
  977.9 7.9 convert_reduce_fusion
  989.1 9.0 convert_reduce_fusion.1
  1002.1 8.3 convert_reduce_fusion.2
  1178.5 10.4 fusion
  1200.2 11.3 add_add_fusion
  1217.8 7.9 reshape.1222
  1225.8 9.5 copy.1328
  1235.3 11.2 reshape.1231
  1264.2 8.1 all-to-all-done.12
  1403.3 8.0 reshape.1216
  1423.2 60.8 %dynamic-update-slice.2 = f32[10043392]{0:T(1024)} dynamic-update-slice(f32[10043392]{0:T(1024)} %constant_dynamic-update-slice_fusion.10, f32[1769472]{0:T(1024)} %reshape.1216, s32[]{} %constant.131) | dynamic-update-slice | bytes 14155780
  1491.2 21.3 dynamic-update-slice.7
  1524.2 21.3 dynamic-update-slice.14
  1549.4 80.6 %dynamic-update-slice.18 = f32[10043392]{0:T(1024)} dynamic-update-slice(f32[10043392]{0:T(1024)} %constant_dynamic-update-slice_fusion.12, f32[2359296]{0:T(1024)} %bitcast.569, s32[]{} %constant.147) | dynamic-update-slice | bytes 18874372
  1631.3 80.0 %dynamic-update-slice.20 = f32[10043392]{0:T(1024)} dynamic-update-slice(f32[10043392]{0:T(1024)} %add_dynamic-update-slice_fusion, f32[2359296]{0:T(1024)} %reshape.1231, s32[]{} %constant.149) | dynamic-update-slice | bytes 18874372
  1733.4 16.9 all-to-all-done.2
  1761.3 16.9 all-to-all-done.8
  1791.4 14.5 all-to-all-done.5
  1824.1 511.2 %all-reduce.3.cloned.1.call-done = f32[10043392]{0:T(1024)} async-done(((f32[10043392]{0:T(1024)}), f32[10043392]{0:T(1024)}) %all-reduce.3.cloned.1.call-update) | async-done | bytes 40173584
  (1144 shorter events, 741.3 us)
Async XLA Ops:
  7.2 273.3 %all-gather.3.cloned.1.call-start = ((), (), s32[]{:S(2)}) async-start(), calls=%async_computation.15 | async-start | bytes 41428992 | tf_op jit(solution)/shard_map/all_gather | solution.py:336
  18.1 11.9 all-to-all-start.7
  30.6 8.9 all-to-all-start.1
  40.2 8.9 all-to-all-start.4
  49.7 38.2 %all-to-all-start.11 = ((bf16[16,25,768]{2,1,0:T(8,128)(2,1)}), bf16[16,25,768]{2,1,0:T(8,128)(2,1)S(1)}, u32[]{:S(2)}, u32[]{:S(2)}) async-start(bf16[16,25,768]{2,1,0:T(8,128)(2,1)} %copy.1199), calls=%async_computation.11 | async-start | bytes 1572864 | tf_op jit(solution)/shard_map/all_to_all | solution.py:373
  87.9 45.3 %all-to-all-start.13 = ((bf16[16,25,768]{2,1,0:T(8,128)(2,1)}), bf16[16,25,768]{2,1,0:T(8,128)(2,1)S(1)}, u32[]{:S(2)}, u32[]{:S(2)}) async-start(bf16[16,25,768]{2,1,0:T(8,128)(2,1)} %copy.1234), calls=%async_computation.13 | async-start | bytes 1572864 | tf_op jit(solution)/shard_map/all_to_all | solution.py:373
  98.4 39.3 %copy-start.244 = (f32[2,25,8]{1,2,0:T(8,128)S(1)}, f32[2,25,8]{1,2,0:T(8,128)}, u32[]{:S(2)}) copy-start(f32[2,25,8]{1,2,0:T(8,128)} %copy.1074) | copy-start | bytes 4804
  98.4 39.9 %copy-start.224 = (f32[2,25,8]{1,2,0:T(8,128)S(1)}, f32[2,25,8]{1,2,0:T(8,128)}, u32[]{:S(2)}) copy-start(f32[2,25,8]{1,2,0:T(8,128)} %copy-done.223) | copy-start | bytes 4804
  98.4 39.9 %copy-start.222 = (f32[2,25,8]{1,2,0:T(8,128)S(1)}, f32[2,25,8]{1,2,0:T(8,128)}, u32[]{:S(2)}) copy-start(f32[2,25,8]{1,2,0:T(8,128)} %copy-done.221) | copy-start | bytes 4804
  133.2 29.8 %all-to-all-start.9 = ((bf16[16,25,768]{2,1,0:T(8,128)(2,1)}), bf16[16,25,768]{2,1,0:T(8,128)(2,1)}, u32[]{:S(2)}, u32[]{:S(2)}) async-start(bf16[16,25,768]{2,1,0:T(8,128)(2,1)} %copy.1164), calls=%async_computation.9 | async-start | bytes 1572864 | tf_op jit(solution)/shard_map/all_to_all | solution.py:373
  679.3 187.9 %copy-start.166 = (f32[768]{0:T(1024)}, f32[768]{0:T(1024)S(1)}, u32[]{:S(2)}) copy-start(f32[768]{0:T(1024)S(1)} %get-tuple-element.98) | copy-start | bytes 9220
  679.3 187.9 %copy-start.168 = (f32[768]{0:T(1024)}, f32[768]{0:T(1024)S(1)}, u32[]{:S(2)}) copy-start(f32[768]{0:T(1024)S(1)} %get-tuple-element.97) | copy-start | bytes 9220
  752.5 25.8 %all-to-all-start.6 = ((bf16[16,25,768]{2,1,0:T(8,128)(2,1)}), bf16[16,25,768]{2,1,0:T(8,128)(2,1)}, u32[]{:S(2)}, u32[]{:S(2)}) async-start(bf16[16,25,768]{2,1,0:T(8,128)(2,1)} %copy.1142), calls=%async_computation.6 | async-start | bytes 1572864 | tf_op jit(solution)/shard_map/all_to_all | solution.py:363
  778.2 41.7 %all-to-all-start.3 = ((bf16[16,25,768]{2,1,0:T(8,128)(2,1)}), bf16[16,25,768]{2,1,0:T(8,128)(2,1)}, u32[]{:S(2)}, u32[]{:S(2)}) async-start(bf16[16,25,768]{2,1,0:T(8,128)(2,1)} %copy.1112), calls=%async_computation.3 | async-start | bytes 1572864 | tf_op jit(solution)/shard_map/all_to_all | solution.py:363
  819.9 26.0 %all-to-all-start = ((bf16[16,25,768]{2,1,0:T(8,128)(2,1)}), bf16[16,25,768]{2,1,0:T(8,128)(2,1)S(1)}, u32[]{:S(2)}, u32[]{:S(2)}) async-start(bf16[16,25,768]{2,1,0:T(8,128)(2,1)} %copy.1082), calls=%async_computation | async-start | bytes 1572864 | tf_op jit(solution)/shard_map/all_to_all | solution.py:363
  939.4 38.4 %copy-start.19 = (f32[2,200,3072]{2,1,0:T(8,128)S(1)}, f32[2,200,3072]{2,1,0:T(8,128)}, u32[]{:S(2)}) copy-start(f32[2,200,3072]{2,1,0:T(8,128)} %fusion.160) | copy-start | bytes 14745604
  939.4 38.4 %copy-start.90 = (bf16[8,2,25,768]{3,1,2,0:T(2,128)(2,1)S(1)}, bf16[8,2,25,768]{3,1,2,0:T(2,128)(2,1)}, u32[]{:S(2)}) copy-start(bf16[8,2,25,768]{3,1,2,0:T(2,128)(2,1)} %copy.1324) | copy-start | bytes 1843204
  939.4 49.6 %slice-start.12 = ((s8[4915200]{0:T(1024)(128)(4,1)}), s8[4194304]{0:T(1024)(128)(4,1)S(1)}, s32[]{:S(2)}) async-start(s8[4915200]{0:T(1024)(128)(4,1)} %bitcast.570), calls=%async_computation.29 | async-start | bytes 8388608
  1169.2 80.9 %all-to-all-start.10 = ((bf16[2,200,768]{2,0,1:T(2,128)(2,1)}), bf16[2,200,768]{2,0,1:T(2,128)(2,1)}, u32[]{:S(2)}, u32[]{:S(2)}) async-start(bf16[2,200,768]{2,0,1:T(2,128)(2,1)} %copy.1177), calls=%async_computation.10 | async-start | bytes 1228800 | tf_op jit(solution)/shard_map/all_to_all | solution.py:375
  1250.0 22.3 all-to-all-start.12
  1257.6 127.3 %copy-start.85 = (bf16[2,25,8,768]{3,2,1,0:T(8,128)(2,1)}, bf16[2,25,8,768]{3,2,1,0:T(8,128)(2,1)S(1)}, u32[]{:S(2)}) copy-start(bf16[2,25,8,768]{3,2,1,0:T(8,128)(2,1)S(1)} %copy.1179) | copy-start | bytes 1843204
  1272.3 37.5 %all-to-all-start.14 = ((bf16[2,200,768]{2,0,1:T(2,128)(2,1)}), bf16[2,200,768]{2,0,1:T(2,128)(2,1)}, u32[]{:S(2)}, u32[]{:S(2)}) async-start(bf16[2,200,768]{2,0,1:T(2,128)(2,1)} %copy.1247), calls=%async_computation.14 | async-start | bytes 1228800 | tf_op jit(solution)/shard_map/all_to_all | solution.py:375
  1276.5 1058.8 %all-reduce.3.cloned.1.call-start = ((), (), s32[]{:S(2)}) async-start(), calls=%async_computation.16 | async-start | bytes 80347136
  1549.4 80.6 %copy-start.263 = (f32[3072]{0:T(1024)S(1)}, f32[3072]{0:T(1024)}, u32[]{:S(2)}) copy-start(f32[3072]{0:T(1024)} %get-tuple-element.237) | copy-start | bytes 36868
  1549.4 80.6 %copy-start.264 = (f32[3072]{0:T(1024)S(1)}, f32[3072]{0:T(1024)}, u32[]{:S(2)}) copy-start(f32[3072]{0:T(1024)} %get-tuple-element.241) | copy-start | bytes 36868
  1549.4 80.6 %copy-start.265 = (f32[3072]{0:T(1024)S(1)}, f32[3072]{0:T(1024)}, u32[]{:S(2)}) copy-start(f32[3072]{0:T(1024)} %get-tuple-element.239) | copy-start | bytes 36868
  1631.3 80.0 %copy-start.245 = (f32[768]{0:T(1024)S(1)}, f32[768]{0:T(1024)}, u32[]{:S(2)}) copy-start(f32[768]{0:T(1024)} %get-tuple-element.69) | copy-start | bytes 9220
  1631.3 80.0 %copy-start.246 = (f32[768]{0:T(1024)S(1)}, f32[768]{0:T(1024)}, u32[]{:S(2)}) copy-start(f32[768]{0:T(1024)} %get-tuple-element.67) | copy-start | bytes 9220
  1631.3 80.0 %copy-start.247 = (f32[768]{0:T(1024)S(1)}, f32[768]{0:T(1024)}, u32[]{:S(2)}) copy-start(f32[768]{0:T(1024)} %get-tuple-element.71) | copy-start | bytes 9220
  1721.7 28.5 %all-to-all-start.2 = ((bf16[2,200,768]{2,0,1:T(2,128)(2,1)}), bf16[2,200,768]{2,0,1:T(2,128)(2,1)}, u32[]{:S(2)}, u32[]{:S(2)}) async-start(bf16[2,200,768]{2,0,1:T(2,128)(2,1)} %copy.1099), calls=%async_computation.2 | async-start | bytes 1228800 | tf_op jit(solution)/shard_map/all_to_all | solution.py:368
  1750.3 27.9 %all-to-all-start.8 = ((bf16[2,200,768]{2,0,1:T(2,128)(2,1)}), bf16[2,200,768]{2,0,1:T(2,128)(2,1)}, u32[]{:S(2)}, u32[]{:S(2)}) async-start(bf16[2,200,768]{2,0,1:T(2,128)(2,1)} %copy.1159), calls=%async_computation.8 | async-start | bytes 1228800 | tf_op jit(solution)/shard_map/all_to_all | solution.py:368
  1778.2 27.8 %all-to-all-start.5 = ((bf16[2,200,768]{2,0,1:T(2,128)(2,1)}), bf16[2,200,768]{2,0,1:T(2,128)(2,1)S(1)}, u32[]{:S(2)}, u32[]{:S(2)}) async-start(bf16[2,200,768]{2,0,1:T(2,128)(2,1)} %copy.1129), calls=%async_computation.5 | async-start | bytes 1228800 | tf_op jit(solution)/shard_map/all_to_all | solution.py:368
  (303 other events, 1955.4 us)
Sparse Core Ops, SparseCore 0:
  14.9 265.5 all-gather.2
  1714.1 621.1 all-reduce.2
where the time goes:
time: 2370 us; the launch traced here: 2350 us
  waiting for transfers between devices  770 us (32%)
  local copies, waits for them, and re-layouts  704 us (30%)
  other arithmetic  480 us (20%)
  matrix products  308 us (13%)
  starting transfers between devices  65.5 us (3%)
    unnamed x3, waiting for transfers between devices  511 us
    unnamed x654, local copies, waits for them, and re-layouts  372 us
    all_gather x1, other arithmetic, shards(): gathered = lax.all_gather(params, ('dp', 'sp'), axis=0, tiled=True)  349 us
    all_gather x1, waiting for transfers between devices, shards(): gathered = lax.all_gather(params, ('dp', 'sp'), axis=0, tiled=True)  103 us
    dot_general x21, matrix products, weight_grad(): jnp.einsum('rk,rn->kn', left_flat, grad_flat, preferred_element_type=jnp....  90 us
    dot_general x21, matrix products, product_back(): jnp.einsum('...n,kn->...k', grad_rows, weight, preferred_element_type=jnp...  78.9 us
    all_to_all x3, waiting for transfers between devices, shards(): lax.all_to_all(masked_cot, 'sp', split_axis=0, concat_axis=1, tiled=True)  71.2 us
    dot_general x21, matrix products, product(): return jnp.dot(left_side, right_side, preferred_element_type=jnp.float32)  66.6 us
  transfers between devices with their start and end apart: 17, of which 14 were waited for; matrix products, arithmetic and copies ran while one was open for 12% of the time, Pallas kernels for 0%

commit v1 on v0

v1 whole, which is shorter than its diff:
```python
import math

import jax
import jax.numpy as jnp
from jax import lax
from jax.experimental import pallas as pl
from jax.experimental.pallas import tpu as pltpu
from jax.sharding import PartitionSpec as P

H = 12
FF = 3072
EPS = 1e-06
MASKED = -1000000000.0
LANES = 128
BOTH = ("dp", "sp")
BF = jnp.bfloat16
F32 = jnp.float32


def segment_shapes(d, ff):
    return [
        (d,), (d,), (d, 3 * d), (d,), (d,), (d, d), (d,), (d, d), (d,),
        (d,), (d,), (d, 3 * d), (d,), (d,), (d, d), (d,),
        (d,), (d,), (d, ff), (ff,), (ff, d), (d,),
    ]


def pair_masks(rows):
    lane = lax.broadcasted_iota(jnp.int32, (rows, LANES), 1)
    return lane < LANES // 2


def dot_t(a, b):
    return lax.dot_general(a, b, (((1,), (1,)), ((), ())), preferred_element_type=F32)


def dot_l(a, b):
    return lax.dot_general(a, b, (((0,), (0,)), ((), ())), preferred_element_type=F32)


def dot(a, b):
    return jnp.dot(a, b, preferred_element_type=F32)


def softmax_of(q, k, keep):
    s = jnp.where(keep, dot_t(q, k), MASKED)
    top = jnp.max(s, axis=-1, keepdims=True)
    e = jnp.exp(s - top)
    return e * (1.0 / jnp.sum(e, axis=-1, keepdims=True))


def attend_kernel(q_ref, k_ref, v_ref, m_ref, o_ref):
    keep = m_ref[0] > 0.5
    rows, width = q_ref.shape[1], q_ref.shape[2]
    first = pair_masks(rows)
    for at in range(0, width, LANES):
        q = q_ref[0, :, at : at + LANES] * jnp.asarray(0.125, BF)
        k = k_ref[0, :, at : at + LANES]
        v = v_ref[0, :, at : at + LANES]
        zero = jnp.zeros_like(q)
        pa = softmax_of(jnp.where(first, q, zero), k, keep).astype(BF)
        pb = softmax_of(jnp.where(first, zero, q), k, keep).astype(BF)
        o_ref[0, :, at : at + LANES] = jnp.where(first, dot(pa, v), dot(pb, v)).astype(BF)


def attend_back_kernel(q_ref, k_ref, v_ref, m_ref, d_ref, dq_ref, dk_ref, dv_ref):
    keep = m_ref[0] > 0.5
    rows, width = q_ref.shape[1], q_ref.shape[2]
    first = pair_masks(rows)
    for at in range(0, width, LANES):
        q = q_ref[0, :, at : at + LANES] * jnp.asarray(0.125, BF)
        k = k_ref[0, :, at : at + LANES]
        v = v_ref[0, :, at : at + LANES]
        d = d_ref[0, :, at : at + LANES]
        zero = jnp.zeros_like(q)
        parts = []
        for here in (True, False):
            pick = (lambda t: jnp.where(first, t, zero)) if here else (lambda t: jnp.where(first, zero, t))
            p = softmax_of(pick(q), k, keep)
            dp = dot_t(pick(d), v)
            ds = (p * (dp - jnp.sum(p * dp, axis=-1, keepdims=True))).astype(BF)
            parts.append((dot(ds, k) * 0.125, dot_l(ds, q), dot_l(p.astype(BF), d)))
        for ref, a, b in zip((dq_ref, dk_ref, dv_ref), *parts):
            ref[0, :, at : at + LANES] = jnp.where(first, a, b).astype(BF)


def head_split(width):
    for parts in (2, 3, 1):
        if width % (parts * LANES) == 0:
            return parts
    return 1


def attention_specs(packed, keep, d):
    parts = head_split(d)
    w = d // parts
    rows = packed.shape[1]
    own = lambda third: pl.BlockSpec((1, rows, w), lambda i, j: (i, 0, third * parts + j))
    one = keep.shape[0] == 1
    mask = pl.BlockSpec((1,) + keep.shape[1:], lambda i, j: (0 if one else i, 0, 0))
    flat = pl.BlockSpec((1, rows, w), lambda i, j: (i, 0, j))
    return parts, own, mask, flat


def attend(packed, keep, d):
    n, rows, _ = packed.shape
    parts, own, mask, flat = attention_specs(packed, keep, d)
    return pl.pallas_call(
        attend_kernel,
        grid=(n, parts),
        in_specs=[own(0), own(1), own(2), mask],
        out_specs=flat,
        out_shape=jax.ShapeDtypeStruct((n, rows, d), BF),
        cost_estimate=pl.CostEstimate(
            flops=4 * n * rows * rows * d * 2,
            bytes_accessed=n * rows * d * 8,
            transcendentals=n * rows * rows * (d // 64),
        ),
        name="attend",
    )(packed, packed, packed, keep)


def attend_back(packed, keep, grad, d):
    n, rows, _ = packed.shape
    parts, own, mask, flat = attention_specs(packed, keep, d)
    shape = jax.ShapeDtypeStruct((n, rows, d), BF)
    return pl.pallas_call(
        attend_back_kernel,
        grid=(n, parts),
        in_specs=[own(0), own(1), own(2), mask, flat],
        out_specs=[flat, flat, flat],
        out_shape=[shape, shape, shape],
        cost_estimate=pl.CostEstimate(
            flops=10 * n * rows * rows * d * 2,
            bytes_accessed=n * rows * d * 14,
            transcendentals=n * rows * rows * (d // 64),
        ),
        name="attend_back",
    )(packed, packed, packed, keep, grad)


def flip_perm(dp_bits=0, sp_bits=0):
    return [(d * 8 + s, (d ^ dp_bits) * 8 + (s ^ sp_bits)) for d in range(4) for s in range(8)]


def send(value, dp_bits=0, sp_bits=0):
    return lax.ppermute(value, BOTH, flip_perm(dp_bits, sp_bits))


def pick(stack, at):
    return lax.dynamic_index_in_dim(stack, at, 0, keepdims=False)


def place_of():
    dp, sp = lax.axis_index("dp"), lax.axis_index("sp")
    return jnp.stack([dp, sp >> 1, sp & 1]).astype(jnp.int32)


def round_up(value, step):
    return -(-value // step) * step


class Plan:
    def __init__(self, rows):
        self.rows = rows
        self.part = round_up(-(-rows // 4), 16)
        self.gap = 4 * self.part - rows
        self.block = 32 * self.part

    def padded(self, row):
        return row + self.gap * (row // self.rows)


def assemble_kernel(pos_ref, *refs):
    ins, out, buf, sem_in, sem_out = refs[:8], refs[8], refs[9], refs[10], refs[11]
    dp, z, core = pos_ref[0], pos_ref[1], pos_ref[2]
    loads = []
    for j in range(8):
        for k in range(4):
            at = j * 4 + k
            load = pltpu.make_async_copy(ins[j].at[k], buf.at[at], sem_in.at[at])
            load.start()
            loads.append(load)
    stores = []
    for j in range(8):
        for k in range(4):
            at = j * 4 + k
            loads[at].wait()
            to = ((z ^ k) * 2 + (core ^ (j // 4))) * 4 + (dp ^ (j % 4))
            store = pltpu.make_async_copy(buf.at[at], out.at[to], sem_out.at[at])
            store.start()
            stores.append(store)
    for store in stores:
        store.wait()


def assemble(pos, pieces):
    part = pieces[0].shape[1]
    any_spec = pl.BlockSpec(memory_space=pl.ANY)
    out = pl.pallas_call(
        assemble_kernel,
        grid_spec=pltpu.PrefetchScalarGridSpec(
            num_scalar_prefetch=1,
            grid=(1,),
            in_specs=[any_spec] * 8,
            out_specs=any_spec,
            scratch_shapes=[
                pltpu.VMEM((32, part, LANES), BF),
                pltpu.SemaphoreType.DMA((32,)),
                pltpu.SemaphoreType.DMA((32,)),
            ],
        ),
        out_shape=jax.ShapeDtypeStruct((32, part, LANES), BF),
        cost_estimate=pl.CostEstimate(flops=0, bytes_accessed=32 * part * LANES * 4, transcendentals=0),
        name="assemble",
    )(pos, *pieces)
    return out.reshape(32 * part, LANES)


def gather_blocks(shard, plan, pos):
    dp = pos[0]
    mine = jnp.pad(shard.reshape(plan.rows, LANES), ((0, plan.gap), (0, 0)))
    mine = mine.reshape(4, plan.part, LANES)
    spread = jnp.zeros_like(mine)
    for k in range(4):
        piece = pick(mine, dp ^ k)
        got = piece if k == 0 else send(piece, k)
        spread = lax.dynamic_update_slice(spread, got[None], (dp ^ k, 0, 0))
    blocks = []
    for b in range(4):
        piece = spread[b]
        line = jnp.stack([piece] + [send(piece, 0, 2 * k) for k in range(1, 4)])
        own = [line] + [send(line, k) for k in range(1, 4)]
        other = [send(part, 0, 1) for part in own]
        blocks.append(assemble(pos, own + other))
    return blocks


CHUNK = 1152


def unflatten(src, base, off, rows, width, plan):
    lanes = width // LANES
    step_rows = CHUNK // lanes
    size = src.shape[0]
    window = round_up(CHUNK + plan.gap + 16, 16)

    def where_from(i):
        first = off + CHUNK * i
        at = first + plan.gap * (first // plan.rows) - base
        return first, at, jnp.minimum(at // 16 * 16, size - window)

    def kernel(in_ref, out_ref, wide):
        first, at, start = where_from(pl.program_id(0))
        delta = at - start
        left = plan.rows - first % plan.rows
        wide[...] = in_ref[...].astype(F32)

        @pl.when(left >= CHUNK)
        def _():
            for b in range(lanes):
                got = wide[pl.ds(delta + b, step_rows, stride=lanes), :]
                out_ref[:, b * LANES : (b + 1) * LANES] = got.astype(BF)

        @pl.when(left < CHUNK)
        def _():
            row = lax.broadcasted_iota(jnp.int32, (step_rows, LANES), 0) * lanes
            for b in range(lanes):
                near = wide[pl.ds(delta + b, step_rows, stride=lanes), :]
                far = wide[pl.ds(delta + b + plan.gap, step_rows, stride=lanes), :]
                got = jnp.where(row + b < left, near, far)
                out_ref[:, b * LANES : (b + 1) * LANES] = got.astype(BF)

    return pl.pallas_call(
        kernel,
        grid=(rows // step_rows,),
        in_specs=[
            pl.BlockSpec(
                (pl.Element(window), pl.Element(LANES)),
                lambda i: (pl.multiple_of(where_from(i)[2], 16), 0),
            )
        ],
        out_specs=pl.BlockSpec((step_rows, width), lambda i: (i, 0)),
        out_shape=jax.ShapeDtypeStruct((rows, width), BF),
        scratch_shapes=[pltpu.VMEM((window, LANES), F32)],
        cost_estimate=pl.CostEstimate(flops=0, bytes_accessed=rows * width * 4, transcendentals=0),
        name="unflatten",
    )(src)


def flatten(pos, b, mats, vecs, plan):
    part = plan.part
    shapes = []
    for off, mat in mats:
        lanes = mat.shape[1] // LANES
        shapes.append((off, mat.shape[0], lanes, round_up(-(-part // lanes) + 8, 8)))
    pad = round_up(max([w * c for _, _, c, w in shapes] + [v.shape[0] for _, v in vecs]), 8) + 8

    def first_row(t, pos_ref):
        z = pos_ref[1] ^ (t % 4)
        core = jnp.where(t < 16, 1 - pos_ref[2], pos_ref[2])
        quarter = pos_ref[0] ^ (t // 4 % 4)
        return (8 * b + z * 2 + core) * plan.rows + quarter * part

    def start_row(p0, off, rows, lanes, w):
        return jnp.minimum(jnp.maximum(p0 - off, 0) // lanes // 8 * 8, rows - w)

    def kernel(pos_ref, *refs):
        ins = refs[: len(mats)]
        vins = refs[len(mats) : len(mats) + len(vecs)]
        theirs, ours, wide = refs[len(mats) + len(vecs) :]
        t = pl.program_id(0)
        p0 = first_row(t, pos_ref)
        for (off, rows, lanes, w), ref in zip(shapes, ins):

            @pl.when((p0 + part > off) & (p0 < off + rows * lanes))
            def _():
                at = off + lanes * start_row(p0, off, rows, lanes, w) - p0 + pad
                for c in range(lanes):
                    wide[pl.ds(at + c, w, stride=lanes), :] = ref[:, c * LANES : (c + 1) * LANES]

        for (off, vec), ref in zip(vecs, vins):
            n = vec.shape[0]

            @pl.when((p0 + part > off) & (p0 < off + n))
            def _():
                at = off - p0 + pad
                for r in range(n):
                    wide[pl.ds(at + r, 1), :] = ref[r : r + 1, :]

        got = wide[pad : pad + part, :].astype(BF)

        @pl.when(t < 16)
        def _():
            theirs[0] = got

        @pl.when(t >= 16)
        def _():
            ours[0] = got

    in_specs = [
        pl.BlockSpec(
            (pl.Element(w), pl.Element(lanes * LANES)),
            lambda t, p, off=off, rows=rows, lanes=lanes, w=w: (
                pl.multiple_of(start_row(first_row(t, p), off, rows, lanes, w), 8),
                0,
            ),
        )
        for off, rows, lanes, w in shapes
    ] + [pl.BlockSpec(v.shape, lambda t, p: (0, 0)) for _, v in vecs]
    shape = jax.ShapeDtypeStruct((16, part, LANES), BF)
    theirs, ours = pl.pallas_call(
        kernel,
        grid_spec=pltpu.PrefetchScalarGridSpec(
            num_scalar_prefetch=1,
            grid=(32,),
            in_specs=in_specs,
            out_specs=[
                pl.BlockSpec((1, part, LANES), lambda t, p: (jnp.minimum(t, 15), 0, 0)),
                pl.BlockSpec((1, part, LANES), lambda t, p: (jnp.maximum(t - 16, 0), 0, 0)),
            ],
            scratch_shapes=[pltpu.VMEM((2 * pad + part, LANES), F32)],
        ),
        out_shape=[shape, shape],
        cost_estimate=pl.CostEstimate(flops=0, bytes_accessed=plan.block * LANES * 6, transcendentals=0),
        name="flatten",
    )(pos, *[m for _, m in mats], *[v for _, v in vecs])
    return theirs.reshape(4, 4, part, LANES), ours.reshape(4, 4, part, LANES)


def reduce_block(theirs, ours):
    ours = (ours.astype(F32) + send(theirs, 0, 1).astype(F32)).astype(BF)
    total = ours[0].astype(F32)
    for k in range(1, 4):
        total = total + send(ours[k], k).astype(F32)
    line = total.astype(BF)
    total = line[0].astype(F32)
    for k in range(1, 4):
        total = total + send(line[k], 0, 2 * k).astype(F32)
    return total


def return_quarters(quarters, plan, pos):
    stack = jnp.stack(quarters)
    dp = pos[0]
    out = jnp.zeros_like(stack)
    for k in range(4):
        piece = pick(stack, dp ^ k)
        got = piece if k == 0 else send(piece, k)
        out = lax.dynamic_update_slice(out, got[None], (dp ^ k, 0, 0))
    return out.reshape(4 * plan.part, LANES)[: plan.rows].reshape(-1)


def segment_rows(d, ff):
    spans, at = [], 0
    for shape in segment_shapes(d, ff):
        length = math.prod(shape)
        spans.append((at, at + length, shape))
        at += length
    return spans, at


def cut(blocks, lo, hi):
    size = blocks[0].shape[0]
    pieces = []
    for i, block in enumerate(blocks):
        a, b = max(lo, i * size), min(hi, (i + 1) * size)
        if a < b:
            pieces.append(block[a - i * size : b - i * size])
    return pieces[0] if len(pieces) == 1 else jnp.concatenate(pieces)


def cut_padded(blocks, lo, hi, plan):
    pieces = []
    while lo < hi:
        end = min(hi, (lo // plan.rows + 1) * plan.rows)
        pieces.append(cut(blocks, plan.padded(lo), plan.padded(lo) + end - lo))
        lo = end
    return pieces[0] if len(pieces) == 1 else jnp.concatenate(pieces)


def matrix_of(blocks, lo, shape, plan):
    rows, width = shape
    first = plan.padded(lo)
    last = plan.padded(lo + rows * (width // LANES) - 1) + 1
    a, b = first // plan.block, (last - 1) // plan.block
    if a == b:
        return unflatten(blocks[a], a * plan.block, lo, rows, width, plan)
    base = first // 16 * 16
    return unflatten(cut(blocks, base, round_up(last, 16)), base, lo, rows, width, plan)


def stats(v):
    center = v - jnp.mean(v, axis=-1, keepdims=True)
    scale = lax.rsqrt(jnp.mean(center * center, axis=-1, keepdims=True) + EPS)
    return center * scale, scale


def norm_back(hat, scale, gain, grad):
    inner = grad * gain
    back = scale * (
        inner
        - jnp.mean(inner, axis=-1, keepdims=True)
        - hat * jnp.mean(inner * hat, axis=-1, keepdims=True)
    )
    return back, jnp.sum(grad * hat, axis=0), jnp.sum(grad, axis=0)


def product_back(grad_rows, weight):
    return lax.dot_general(grad_rows, weight, (((1,), (1,)), ((), ())), preferred_element_type=F32)


def weight_grad(lefts, grads):
    return dot_l(jnp.concatenate(lefts), jnp.concatenate(grads))


def row_sum(grads):
    return sum(jnp.sum(g.astype(F32), axis=0) for g in grads)


def add_up(parts):
    total = parts[0]
    for part in parts[1:]:
        total = total + part
    return total


def gelu_pair(u):
    half = 0.5 * (1.0 + lax.erf(u * (2.0 ** -0.5)))
    slope = half + u * jnp.exp(-0.5 * u * u) * ((2.0 * math.pi) ** -0.5)
    return (u * half).astype(BF), slope


def bias_row(q_bias, v_bias):
    return jnp.concatenate([q_bias, jnp.zeros_like(q_bias), v_bias])


def shards(inputs, cotangent, params, clip_counts, slot_live):
    micro, clips, frames, places, d = inputs.shape
    n_sp = lax.axis_size("sp")
    n_dev = lax.axis_size("dp") * n_sp
    full_length = params.shape[0] * n_dev
    tokens = clips * frames * places
    seqs = clips * frames // n_sp
    length = places * n_sp
    rows = params.shape[0] // LANES
    fast = n_sp == 8 and n_dev == 32 and params.shape[0] % (2 * LANES) == 0

    spans, used = segment_rows(d, FF)
    pieces = []
    if fast:
        plan, pos = Plan(rows), place_of()
        blocks = gather_blocks(params, plan, pos)
        for lo, hi, shape in spans:
            lo, hi = lo // LANES, hi // LANES
            if len(shape) == 1:
                pieces.append(cut_padded(blocks, lo, hi, plan).reshape(shape).astype(F32))
            else:
                pieces.append(matrix_of(blocks, lo, shape, plan))
    else:
        blocks = [lax.all_gather(params, BOTH, axis=0, tiled=True).reshape(-1, LANES)]
        for lo, hi, shape in spans:
            piece = cut(blocks, lo // LANES, hi // LANES).reshape(shape)
            pieces.append(piece.astype(F32) if len(shape) == 1 else piece)
    (tg, tb, w_qkv_t, bq_t, bv_t, w_out_t, bo_t, w_fc, b_fc,
     sg, sb, w_qkv_s, bq_s, bv_s, w_out_s, bo_s,
     mg, mb_, w_up, b_up, w_down, b_down) = pieces

    in_use = (jnp.arange(clips, dtype=jnp.int32)[None] < clip_counts).astype(F32)
    live = slot_live.astype(F32) * in_use[:, :, None]
    live_low = live.astype(BF)

    def to_frames(rows):
        return lax.all_to_all(
            rows.reshape(clips * frames, places, d), "sp", split_axis=0, concat_axis=1, tiled=True
        )

    def to_places(rows):
        return lax.all_to_all(
            rows.reshape(seqs, length, d), "sp", split_axis=1, concat_axis=0, tiled=True
        ).reshape(clips, frames, places, d)

    place = jnp.arange(frames * places, dtype=jnp.int32) % places
    same = (place[:, None] == place[None]).astype(F32)[None]
    bias_t = bias_row(bq_t, bv_t)
    bias_s = bias_row(bq_s, bv_s)
    span_t = frames * places

    live_sent = jnp.broadcast_to(live_low[:, :, None], (micro, clips, frames, places)).reshape(
        micro, clips * frames, places
    )
    live_frames = lax.all_to_all(live_sent, "sp", split_axis=1, concat_axis=2, tiled=True)
    keep_s = live_frames.astype(F32).reshape(micro, seqs, 1, length)
    cots = [
        to_frames(cotangent[m] * live_low[m, :, None, :, None]).reshape(seqs * length, d)
        for m in range(micro)
    ]

    time_kept, sent = [], []
    for m in range(micro):
        x = inputs[m].reshape(tokens, d).astype(F32)
        hat, scale = stats(x)
        h1 = (hat * tg + tb).astype(BF)
        qkv = (dot(h1, w_qkv_t) + bias_t).astype(BF)
        o = attend(qkv.reshape(clips, span_t, 3 * d), same, d).reshape(tokens, d)
        a = (dot(o, w_out_t) + bo_t).astype(BF)
        x1 = (x + dot(a, w_fc) + b_fc).astype(BF)
        sent.append(to_frames(x1).reshape(seqs * length, d))
        time_kept.append((h1, qkv, o, a))

    outs, returned, space_kept = [], [], []
    for m in range(micro):
        xb = sent[m].astype(F32)
        hat2, scale2 = stats(xb)
        h2 = (hat2 * sg + sb).astype(BF)
        qkv = (dot(h2, w_qkv_s) + bias_s).astype(BF)
        qkv3 = qkv.reshape(seqs, length, 3 * d)
        o = attend(qkv3, keep_s[m], d).reshape(-1, d)
        x2 = xb + dot(o, w_out_s) + bo_s
        hat3, scale3 = stats(x2)
        h3 = (hat3 * mg + mb_).astype(BF)
        g, slope = gelu_pair(dot(h3, w_up) + b_up)
        x3 = (x2 + dot(g, w_down) + b_down).astype(BF)
        outs.append(to_places(x3) * live_low[m, :, None, :, None])
        dx3 = cots[m]
        du = (product_back(dx3, w_down) * slope).astype(BF)
        back3, d_mg, d_mb = norm_back(hat3, scale3, mg, product_back(du, w_up))
        dx2 = dx3.astype(F32) + back3
        da = dx2.astype(BF)
        do = product_back(da, w_out_s).astype(BF)
        dqkv = [t.reshape(-1, d) for t in attend_back(qkv3, keep_s[m], do.reshape(seqs, length, d), d)]
        dqkv = jnp.concatenate(dqkv, axis=-1)
        back2, d_sg, d_sb = norm_back(hat2, scale2, sg, product_back(dqkv, w_qkv_s))
        dx1 = (dx2 + back2).astype(BF)
        returned.append(to_places(dx1).reshape(tokens, d))
        space_kept.append((h2, dqkv, o, da, h3, du, g, dx3, d_mg, d_mb, d_sg, d_sb))
    (h2s, dqkvs, os_, das, h3s, dus, gs, dx3s, d_mg, d_mb, d_sg, d_sb) = zip(*space_kept)
    grad_down, grad_b_down = weight_grad(gs, dx3s), row_sum(dx3s)
    grad_up, grad_b_up = weight_grad(h3s, dus), row_sum(dus)
    grad_out_s, grad_bo_s = weight_grad(os_, das), row_sum(das)
    grad_qkv_s, sums_s = weight_grad(h2s, dqkvs), row_sum(dqkvs)
    late = [add_up(d_sg), add_up(d_sb), grad_qkv_s, sums_s[:d], sums_s[2 * d :], grad_out_s, grad_bo_s,
            add_up(d_mg), add_up(d_mb), grad_up, grad_b_up, grad_down, grad_b_down]

    input_grads, back_kept = [], []
    for m in range(micro):
        h1, qkv, o, a = time_kept[m]
        dx1 = returned[m]
        da = product_back(dx1, w_fc).astype(BF)
        do = product_back(da, w_out_t).astype(BF)
        dqkv = attend_back(qkv.reshape(clips, span_t, 3 * d), same, do.reshape(clips, span_t, d), d)
        dqkv = jnp.concatenate([t.reshape(tokens, d) for t in dqkv], axis=-1)
        hat, scale = stats(inputs[m].reshape(tokens, d).astype(F32))
        back1, d_tg, d_tb = norm_back(hat, scale, tg, product_back(dqkv, w_qkv_t))
        input_grads.append((dx1.astype(F32) + back1).astype(BF).reshape(clips, frames, places, d))
        back_kept.append((h1, dqkv, o, da, a, dx1, d_tg, d_tb))
    h1s, dqkvs, os_, das, as_, dx1s, d_tg, d_tb = zip(*back_kept)
    grad_fc, grad_b_fc = weight_grad(as_, dx1s), row_sum(dx1s)
    grad_out_t, grad_bo_t = weight_grad(os_, das), row_sum(das)
    grad_qkv_t, sums_t = weight_grad(h1s, dqkvs), row_sum(dqkvs)
    early = [add_up(d_tg), add_up(d_tb), grad_qkv_t, sums_t[:d], sums_t[2 * d :], grad_out_t, grad_bo_t,
             grad_fc, grad_b_fc]

    grads = early + late
    if fast:
        size = 8 * rows
        quarters = [None] * 4
        items, vec_at, vec_parts = [], None, []
        tail = jnp.zeros((full_length - used,), F32)
        for (lo, hi, shape), grad in zip(spans + [(used, full_length, (full_length - used,))], grads + [tail]):
            if len(shape) == 2:
                if vec_parts:
                    items.append((vec_at, jnp.concatenate(vec_parts).reshape(-1, LANES)))
                vec_parts = []
                items.append((lo // LANES, grad))
            else:
                vec_at = vec_at if vec_parts else lo // LANES
                vec_parts.append(grad)
        items.append((vec_at, jnp.concatenate(vec_parts).reshape(-1, LANES)))
        for b in (3, 2, 1, 0):
            mats, vecs = [], []
            for lo, value in items:
                n = value.size // LANES
                if lo < (b + 1) * size and lo + n > b * size:
                    (vecs if value.shape[1] == LANES else mats).append((lo, value))
            quarters[b] = reduce_block(*flatten(pos, b, mats, vecs, plan))
        param_grad = return_quarters(quarters, plan, pos)
    else:
        flat = jnp.concatenate([g.reshape(-1) for g in grads])
        flat = jnp.concatenate([flat, jnp.zeros((full_length - used,), F32)])
        param_grad = lax.psum_scatter(flat, BOTH, scatter_dimension=0, tiled=True)
    return (jnp.stack(outs), jnp.stack(input_grads), param_grad)


def solution(mesh):
    tokens = P(None, "dp", None, "sp", None)
    return jax.shard_map(
        shards,
        mesh=mesh,
        in_specs=(tokens, tokens, P(BOTH), P(None, "dp"), P(None, "dp", "sp")),
        out_specs=(tokens, tokens, P(BOTH)),
        check_vma=False,
    )
```

time: 2370 us -> 1090 us (0.46)
  local copies, waits for them, and re-layouts: 704 us -> 106 us
  waiting for transfers between devices: 770 us -> 223 us
  other arithmetic: 480 us -> 102 us
  Pallas kernels: 0 us -> 306 us
  matrix products: 308 us -> 191 us
  starting transfers between devices: 65.5 us -> 149 us
    unnamed x3 -> x0, waiting for transfers between devices: 511 us -> none
    unnamed x654 -> x355, local copies, waits for them, and re-layouts: 372 us -> 14.5 us
    all_gather x1 -> x0, other arithmetic: 349 us -> none  [shards(): gathered = lax.all_gather(params, ('dp', 'sp'), axis=0, tiled=True)]
    pallas_call x0 -> x27, Pallas kernels: none -> 306 us  [the longest x6 94.5 us: attend_back(): pl.pallas_call(attend_back_kernel, grid=(n, parts), in_specs=[own(0), own...]
    ppermute x0 -> x74, waiting for transfers between devices: none -> 201 us  [send(): return lax.ppermute(value, BOTH, flip_perm(dp_bits, sp_bits))]
    all_to_all x15 -> x13, waiting for transfers between devices: 155 us -> 21.9 us  [the longest x6 18.7 us: to_frames(): lax.all_to_all(rows.reshape(clips * frames, places, d), 'sp', split_axis=...]
    reshape x55 -> x17, local copies, waits for them, and re-layouts: 151 us -> 25.1 us  [the longest x3 8 us: to_places(): return lax.all_to_all(rows.reshape(seqs, length, d), 'sp', split_axis=1,...]
    dot_general x99 -> x49, matrix products: 308 us -> 191 us  [the longest x21 65.3 us: product_back(): lax.dot_general(grad_rows, weight, (((1,), (1,)), ((), ())), preferred_el...]
  transfers between devices with their start and end apart: 17 -> 87, of which waited for: 14 -> 36; matrix products, arithmetic and copies ran while one was open for 12% -> 22% of each run, Pallas kernels for 0% -> 20%
where the time goes in v1:
time: 1090 us; the launch traced here: 1080 us
  Pallas kernels  306 us (28%)
  waiting for transfers between devices  223 us (20%)
  matrix products  191 us (18%)
  starting transfers between devices  149 us (14%)
  local copies, waits for them, and re-layouts  106 us (10%)
  other arithmetic  102 us (9%)
    ppermute x74, waiting for transfers between devices, send(): return lax.ppermute(value, BOTH, flip_perm(dp_bits, sp_bits))  201 us
    pallas_call x6, Pallas kernels, attend_back(): pl.pallas_call(attend_back_kernel, grid=(n, parts), in_specs=[own(0), own...  94.5 us
    pallas_call x4, Pallas kernels, flatten(): pl.pallas_call(kernel, grid_spec=pltpu.PrefetchScalarGridSpec(num_scalar_...  94.1 us
    ppermute x74, starting transfers between devices, send(): return lax.ppermute(value, BOTH, flip_perm(dp_bits, sp_bits))  87.5 us
    dot_general x21, matrix products, product_back(): lax.dot_general(grad_rows, weight, (((1,), (1,)), ((), ())), preferred_el...  65.3 us
    dot_general x7, matrix products, dot_l(): lax.dot_general(a, b, (((0,), (0,)), ((), ())), preferred_element_type=F32)  63.2 us
    dot_general x21, matrix products, dot(): return jnp.dot(a, b, preferred_element_type=F32)  62.8 us
    pallas_call x7, Pallas kernels, unflatten(): pl.pallas_call(kernel, grid=(rows // step_rows,), in_specs=[pl.BlockSpec(...  51.3 us
  transfers between devices with their start and end apart: 87, of which 36 were waited for; matrix products, arithmetic and copies ran while one was open for 22% of the time, Pallas kernels for 20%

profile of v1, /device:TPU:0, one launch (start us, length us, event | category | flops | bytes accessed | tf_op | source)
XLA Modules:
  0.0 1080.2 jit_solution(9165019104710049049)
XLA Ops:
  38.4 17.5 %collective-permute-done.34 = bf16[624,128]{1,0:T(8,128)(2,1)S(1)} collective-permute-done((bf16[624,128]{1,0:T(8,128)(2,1)S(1)}, bf16[624,128]{1,0:T(8,128)(2,1)S(1)}, u32[]{:S(2)}, u32[]{:S(2)}) %collective-permute-start.34) | collective-permute-done | bytes 159776 | tf_op jit(solution)/shard_map/ppermute | solution.py:147
  85.5 13.5 %collective-permute-start.23 = (bf16[624,128]{1,0:T(8,128)(2,1)}, bf16[624,128]{1,0:T(8,128)(2,1)}, u32[]{:S(2)}, u32[]{:S(2)}) collective-permute-start(bf16[624,128]{1,0:T(8,128)(2,1)} %get-tuple-element.177), channel_id=1, source_target_pairs={{0,2},{1,3},{2,0},{3,1},{4,6},{5,7},{6,4},{7,5},{8,10},{9,11},{10,... | collective-permute-start | bytes 479240 | tf_op jit(solution)/shard_map/ppermute | solution.py:147
  134.0 10.5 collective-permute-done.27.refs_2_
  149.3 11.3 %collective-permute-done.18.refs_3_ = bf16[4,624,128]{2,1,0:T(8,128)(2,1)} collective-permute-done((bf16[4,624,128]{2,1,0:T(8,128)(2,1)}, bf16[4,624,128]{2,1,0:T(8,128)(2,1)}, u32[]{:S(2)}, u32[]{:S(2)}) %collective-permute-start.18) | collective-permute-done | bytes 639008 | tf_op jit(solution)/shard_map/ppermute | solution.py:147
  174.2 13.9 %collective-permute-done.8.refs_3_ = bf16[4,624,128]{2,1,0:T(8,128)(2,1)} collective-permute-done((bf16[4,624,128]{2,1,0:T(8,128)(2,1)}, bf16[4,624,128]{2,1,0:T(8,128)(2,1)}, u32[]{:S(2)}, u32[]{:S(2)}) %collective-permute-start.8) | collective-permute-done | bytes 639008 | tf_op jit(solution)/shard_map/ppermute | solution.py:147
  188.1 8.0 collective-permute-done.7.refs_2_
  236.8 8.7 unflatten.7
  319.1 12.6 %pad_maximum_fusion.in_ref = bf16[18800,128]{1,0:T(8,128)(2,1)} fusion(bf16[1136,128]{1,0:T(8,128)(2,1)S(1)} %copy-done.66, bf16[17664,128]{1,0:T(8,128)(2,1)S(1)} %bitcast.546), kind=kLoop, calls=%fused_computation.86 | loop fusion | flops 9625600 | bytes 9625600 | tf_op jit(solution)/shard_map/concatenate | solution.py:410
  356.8 11.1 %unflatten.13 = bf16[3072,768]{1,0:T(8,128)(2,1)} custom-call(bf16[19968,128]{1,0:T(8,128)(2,1)} %bitcast.539), custom_call_target="tpu_custom_call" | custom-call | bytes 9437184 | tf_op jit(solution)/shard_map/unflatten/pallas_call | solution.py:274
  368.0 8.6 unflatten.10
  376.5 12.0 %unflatten.12 = bf16[768,3072]{1,0:T(8,128)(2,1)} custom-call(bf16[18800,128]{1,0:T(8,128)(2,1)} %pad_maximum_fusion.in_ref), custom_call_target="tpu_custom_call" | custom-call | bytes 9437184 | tf_op jit(solution)/shard_map/unflatten/pallas_call | solution.py:274
  404.1 18.6 %all-to-all-done.5 = bf16[16,25,768]{2,1,0:T(8,128)(2,1)} async-done(((bf16[16,25,768]{2,1,0:T(8,128)(2,1)}), bf16[16,25,768]{2,1,0:T(8,128)(2,1)}, u32[]{:S(2)}, u32[]{:S(2)}) %all-to-all-start.5) | async-done | bytes 614432 | tf_op jit(solution)/shard_map/all_to_all | solution.py:514
  510.1 10.6 fusion.6.refs_1_
  529.2 10.7 fusion.refs_1_.refs_0_
  553.9 16.0 %attend_back.8 = (bf16[2,200,768]{2,1,0:T(8,128)(2,1)}, bf16[2,200,768]{2,1,0:T(8,128)(2,1)}, bf16[2,200,768]{2,1,0:T(8,128)(2,1)}) custom-call(bf16[2,200,2304]{2,1,0:T(8,128)(2,1)} %bitcast.525, bf16[2,200,2304]{2,1,0:T(8,128)(2,1)} %bitcast.526, bf16[2,200,2304]{2,1,0:T(8,128)(2,1)} %bitcast.527, f32[2,1,200]{2,1,0:T(1,128)} %squeeze.143.m_ref, ...), custom_call_target="tpu_custom_call" | custom-call | flops 1228800000 | bytes 4300800 | tf_op jit(solution)/shard_map/attend_back/pallas_call | solution.py:127
  580.7 15.6 %attend_back.6 = (bf16[2,200,768]{2,1,0:T(8,128)(2,1)}, bf16[2,200,768]{2,1,0:T(8,128)(2,1)}, bf16[2,200,768]{2,1,0:T(8,128)(2,1)}) custom-call(bf16[2,200,2304]{2,1,0:T(8,128)(2,1)} %bitcast.513, bf16[2,200,2304]{2,1,0:T(8,128)(2,1)} %bitcast.514, bf16[2,200,2304]{2,1,0:T(8,128)(2,1)} %bitcast.515, f32[2,1,200]{2,1,0:T(1,128)} %squeeze.140.m_ref, ...), custom_call_target="tpu_custom_call" | custom-call | flops 1228800000 | bytes 4300800 | tf_op jit(solution)/shard_map/attend_back/pallas_call | solution.py:127
  596.3 15.6 %attend_back.10 = (bf16[2,200,768]{2,1,0:T(8,128)(2,1)}, bf16[2,200,768]{2,1,0:T(8,128)(2,1)}, bf16[2,200,768]{2,1,0:T(8,128)(2,1)}) custom-call(bf16[2,200,2304]{2,1,0:T(8,128)(2,1)} %bitcast.519, bf16[2,200,2304]{2,1,0:T(8,128)(2,1)} %bitcast.520, bf16[2,200,2304]{2,1,0:T(8,128)(2,1)} %bitcast.521, f32[2,1,200]{2,1,0:T(1,128)} %squeeze.144.m_ref, ...), custom_call_target="tpu_custom_call" | custom-call | flops 1228800000 | bytes 4300800 | tf_op jit(solution)/shard_map/attend_back/pallas_call | solution.py:127
  632.3 23.7 %flatten.6 = (bf16[16,624,128]{2,1,0:T(8,128)(2,1)}, bf16[16,624,128]{2,1,0:T(8,128)(2,1)}) custom-call(s32[3]{0:T(128)} %pad_add_fusion.pos_ref, f32[768,768]{1,0:T(8,128)} %fusion.108.refs_2_.refs_0_, f32[768,3072]{1,0:T(8,128)} %fusion.refs_1_.refs_0_, f32[18,128]{1,0:T(8,128)} %pad_maximum_fusion.25.refs_2_), custom_call_target="tpu_custom_call" | custom-call | bytes 15335424 | tf_op jit(solution)/shard_map/flatten/pallas_call | solution.py:352
  656.8 22.0 %flatten.7 = (bf16[16,624,128]{2,1,0:T(8,128)(2,1)}, bf16[16,624,128]{2,1,0:T(8,128)(2,1)}) custom-call(s32[3]{0:T(128)} %pad_add_fusion.pos_ref, f32[768,3072]{1,0:T(8,128)} %fusion.refs_1_.refs_0_, f32[3072,768]{1,0:T(8,128)} %fusion.6.refs_1_, f32[24,128]{1,0:T(8,128)} %add_bitcast_fusion.refs_2_, f32[26,128]{1,0:T(8,128)} %pad_bitcast_fusion.refs_3_), custom_call_target="tpu_custom_call" | custom-call | bytes 15335424 | tf_op jit(solution)/shard_map/flatten/pallas_call | solution.py:352
  685.1 15.7 %fusion.30.refs_1_ = f32[768,2304]{1,0:T(8,128)} fusion(bf16[400,768]{1,0:T(8,128)(2,1)} %bitcast.597, bf16[400,768]{1,0:T(8,128)(2,1)} %bitcast.594, bf16[400,768]{1,0:T(8,128)(2,1)} %bitcast.591, bf16[400,768]{1,0:T(8,128)(2,1)S(1)} %bitcast.581, bf16[400,768]{1,0:T(8,128)(2,1)S(1)} %bitcast.578, bf16[400,768]{1,0:T(8,128)(2,1)S(1)} %bitcast.575, ...), kind=kOutput, calls=%fused_computation.33 | convolution fusion | flops 4302028800 | bytes 14450688 | tf_op jit(solution)/shard_map/dot_general | solution.py:38
  714.1 15.7 %attend_back.9 = (bf16[2,200,768]{2,1,0:T(8,128)(2,1)}, bf16[2,200,768]{2,1,0:T(8,128)(2,1)}, bf16[2,200,768]{2,1,0:T(8,128)(2,1)}) custom-call(bf16[2,200,2304]{2,1,0:T(8,128)(2,1)} %bitcast.507, bf16[2,200,2304]{2,1,0:T(8,128)(2,1)} %bitcast.508, bf16[2,200,2304]{2,1,0:T(8,128)(2,1)} %bitcast.509, f32[1,200,200]{2,1,0:T(8,128)} %compare_convert_fusion.m_ref, ...), custom_call_target="tpu_custom_call" | custom-call | flops 1228800000 | bytes 4300800 | tf_op jit(solution)/shard_map/attend_back/pallas_call | solution.py:127
  746.2 15.9 %attend_back.7 = (bf16[2,200,768]{2,1,0:T(8,128)(2,1)}, bf16[2,200,768]{2,1,0:T(8,128)(2,1)}, bf16[2,200,768]{2,1,0:T(8,128)(2,1)}) custom-call(bf16[2,200,2304]{2,1,0:T(8,128)(2,1)} %bitcast.495, bf16[2,200,2304]{2,1,0:T(8,128)(2,1)} %bitcast.496, bf16[2,200,2304]{2,1,0:T(8,128)(2,1)} %bitcast.497, f32[1,200,200]{2,1,0:T(8,128)} %compare_convert_fusion.m_ref, ...), custom_call_target="tpu_custom_call" | custom-call | flops 1228800000 | bytes 4300800 | tf_op jit(solution)/shard_map/attend_back/pallas_call | solution.py:127
  764.8 15.8 %attend_back.11 = (bf16[2,200,768]{2,1,0:T(8,128)(2,1)}, bf16[2,200,768]{2,1,0:T(8,128)(2,1)}, bf16[2,200,768]{2,1,0:T(8,128)(2,1)}) custom-call(bf16[2,200,2304]{2,1,0:T(8,128)(2,1)} %bitcast.501, bf16[2,200,2304]{2,1,0:T(8,128)(2,1)} %bitcast.502, bf16[2,200,2304]{2,1,0:T(8,128)(2,1)} %bitcast.503, f32[1,200,200]{2,1,0:T(8,128)} %compare_convert_fusion.m_ref, ...), custom_call_target="tpu_custom_call" | custom-call | flops 1228800000 | bytes 4300800 | tf_op jit(solution)/shard_map/attend_back/pallas_call | solution.py:127
  798.2 14.5 %fusion.12.refs_0_ = f32[768,2304]{1,0:T(8,128)} fusion(bf16[400,768]{1,0:T(8,128)(2,1)} %bitcast.625, bf16[400,768]{1,0:T(8,128)(2,1)} %bitcast.622, bf16[400,768]{1,0:T(8,128)(2,1)} %bitcast.619, bf16[400,768]{1,0:T(8,128)(2,1)} %bitcast.607, bf16[400,768]{1,0:T(8,128)(2,1)} %bitcast.604, bf16[400,768]{1,0:T(8,128)(2,1)} %bitcast.601, ...), kind=kOutput, calls=%fused_computation.15 | convolution fusion | flops 4302028800 | bytes 14450688 | tf_op jit(solution)/shard_map/dot_general | solution.py:38
  846.2 24.4 %flatten.4 = (bf16[16,624,128]{2,1,0:T(8,128)(2,1)}, bf16[16,624,128]{2,1,0:T(8,128)(2,1)}) custom-call(s32[3]{0:T(128)} %pad_add_fusion.pos_ref, f32[768,2304]{1,0:T(8,128)} %fusion.12.refs_0_, f32[768,768]{1,0:T(8,128)} %fusion.81.refs_1_, f32[768,768]{1,0:T(8,128)} %fusion.92.refs_2_.refs_0_, f32[12,128]{1,0:T(8,128)} %pad_maximum_fusion.26.refs_3_, ...), custom_call_target="tpu_custom_call" | custom-call | bytes 15335424 | tf_op jit(solution)/shard_map/flatten/pallas_call | solution.py:352
  873.7 24.0 %flatten.5 = (bf16[16,624,128]{2,1,0:T(8,128)(2,1)}, bf16[16,624,128]{2,1,0:T(8,128)(2,1)}) custom-call(s32[3]{0:T(128)} %pad_add_fusion.pos_ref, f32[768,768]{1,0:T(8,128)} %fusion.92.refs_2_.refs_0_, f32[768,2304]{1,0:T(8,128)} %fusion.30.refs_1_, f32[768,768]{1,0:T(8,128)} %fusion.108.refs_2_.refs_0_, f32[18,128]{1,0:T(8,128)} %pad_maximum_fusion.24.refs_3_, ...), custom_call_target="tpu_custom_call" | custom-call | bytes 15335424 | tf_op jit(solution)/shard_map/flatten/pallas_call | solution.py:352
  915.5 10.0 collective-permute-done.58
  925.9 13.2 %collective-permute-done.60 = bf16[4,624,128]{2,1,0:T(8,128)(2,1)S(1)} collective-permute-done((bf16[4,624,128]{2,1,0:T(8,128)(2,1)S(1)}, bf16[4,624,128]{2,1,0:T(8,128)(2,1)S(1)}, u32[]{:S(2)}, u32[]{:S(2)}) %collective-permute-start.60) | collective-permute-done | bytes 639008 | tf_op jit(solution)/shard_map/ppermute | solution.py:147
  955.2 11.0 %collective-permute-done.67 = bf16[4,624,128]{2,1,0:T(8,128)(2,1)} collective-permute-done((bf16[4,624,128]{2,1,0:T(8,128)(2,1)}, bf16[4,624,128]{2,1,0:T(8,128)(2,1)}, u32[]{:S(2)}, u32[]{:S(2)}) %collective-permute-start.67) | collective-permute-done | bytes 639008 | tf_op jit(solution)/shard_map/ppermute | solution.py:147
  978.4 9.0 collective-permute-done.62
  1008.6 13.1 %collective-permute-done.46 = bf16[4,624,128]{2,1,0:T(8,128)(2,1)S(1)} collective-permute-done((bf16[4,624,128]{2,1,0:T(8,128)(2,1)S(1)}, bf16[4,624,128]{2,1,0:T(8,128)(2,1)S(1)}, u32[]{:S(2)}, u32[]{:S(2)}) %collective-permute-start.46) | collective-permute-done | bytes 639008 | tf_op jit(solution)/shard_map/ppermute | solution.py:147
  1034.8 12.1 %collective-permute-done.53 = bf16[4,624,128]{2,1,0:T(8,128)(2,1)S(1)} collective-permute-done((bf16[4,624,128]{2,1,0:T(8,128)(2,1)S(1)}, bf16[4,624,128]{2,1,0:T(8,128)(2,1)S(1)}, u32[]{:S(2)}, u32[]{:S(2)}) %collective-permute-start.53) | collective-permute-done | bytes 639008 | tf_op jit(solution)/shard_map/ppermute | solution.py:147
  (818 shorter events, 621.8 us)
Async XLA Ops:
  2.9 56.9 %all-to-all-start.1 = ((bf16[3,16,25]{2,0,1:T(4,128)(2,1)}), bf16[3,16,25]{2,0,1:T(4,128)(2,1)S(1)}, u32[]{:S(2)}, u32[]{:S(2)}) async-start(bf16[3,16,25]{2,0,1:T(4,128)(2,1)} %bitcast.37), calls=%async_computation.1 | async-start | bytes 32768 | tf_op jit(solution)/shard_map/all_to_all | solution.py:532
  30.5 34.5 %collective-permute-start.5 = (bf16[624,128]{1,0:T(8,128)(2,1)}, bf16[624,128]{1,0:T(8,128)(2,1)}, u32[]{:S(2)}, u32[]{:S(2)}) collective-permute-start(bf16[624,128]{1,0:T(8,128)(2,1)} %get-tuple-element.175), channel_id=1, source_target_pairs={{0,6},{1,7},{2,4},{3,5},{4,2},{5,3},{6,0},{7,1},{8,14},{9,15},{10,... | collective-permute-start | bytes 479240 | tf_op jit(solution)/shard_map/ppermute | solution.py:147
  33.9 35.0 %collective-permute-start.4 = (bf16[624,128]{1,0:T(8,128)(2,1)}, bf16[624,128]{1,0:T(8,128)(2,1)}, u32[]{:S(2)}, u32[]{:S(2)}) collective-permute-start(bf16[624,128]{1,0:T(8,128)(2,1)} %get-tuple-element.175), channel_id=1, source_target_pairs={{0,4},{1,5},{2,6},{3,7},{4,0},{5,1},{6,2},{7,3},{8,12},{9,13},{10,... | collective-permute-start | bytes 479240 | tf_op jit(solution)/shard_map/ppermute | solution.py:147
  59.8 56.7 %all-to-all-start.7 = ((bf16[16,25,768]{2,1,0:T(8,128)(2,1)}), bf16[16,25,768]{2,1,0:T(8,128)(2,1)S(1)}, u32[]{:S(2)}, u32[]{:S(2)}) async-start(bf16[16,25,768]{2,1,0:T(8,128)(2,1)} %copy.249), calls=%async_computation.7 | async-start | bytes 1572864 | tf_op jit(solution)/shard_map/all_to_all | solution.py:514
  68.9 44.4 %collective-permute-start.39 = (bf16[4,624,128]{2,1,0:T(8,128)(2,1)S(1)}, bf16[4,624,128]{2,1,0:T(8,128)(2,1)}, u32[]{:S(2)}, u32[]{:S(2)}) collective-permute-start(bf16[4,624,128]{2,1,0:T(8,128)(2,1)S(1)} %pad_maximum_fusion.21.refs_0_), channel_id=1, source_target_pairs={{0,1},{1,0},{2,3},{3,2},{4,5},{5,4},{6,7},{7,6},{8,9},{9,8},{10,11... | collective-permute-start | bytes 1916936 | tf_op jit(solution)/shard_map/ppermute | solution.py:147
  74.5 39.5 %collective-permute-start.38 = (bf16[4,624,128]{2,1,0:T(8,128)(2,1)S(1)}, bf16[4,624,128]{2,1,0:T(8,128)(2,1)}, u32[]{:S(2)}, u32[]{:S(2)}) collective-permute-start(bf16[4,624,128]{2,1,0:T(8,128)(2,1)S(1)} %pad_maximum_fusion.21.refs_0_), channel_id=1, source_target_pairs={{0,24},{1,25},{2,26},{3,27},{4,28},{5,29},{6,30},{7,31},{8,16},{9,... | collective-permute-start | bytes 1916936 | tf_op jit(solution)/shard_map/ppermute | solution.py:147
  76.0 39.6 %collective-permute-start.37 = (bf16[4,624,128]{2,1,0:T(8,128)(2,1)S(1)}, bf16[4,624,128]{2,1,0:T(8,128)(2,1)}, u32[]{:S(2)}, u32[]{:S(2)}) collective-permute-start(bf16[4,624,128]{2,1,0:T(8,128)(2,1)S(1)} %pad_maximum_fusion.21.refs_0_), channel_id=1, source_target_pairs={{0,16},{1,17},{2,18},{3,19},{4,20},{5,21},{6,22},{7,23},{8,24},{9,... | collective-permute-start | bytes 1916936 | tf_op jit(solution)/shard_map/ppermute | solution.py:147
  116.5 48.6 %all-to-all-start.9 = ((bf16[16,25,768]{2,1,0:T(8,128)(2,1)}), bf16[16,25,768]{2,1,0:T(8,128)(2,1)}, u32[]{:S(2)}, u32[]{:S(2)}) async-start(bf16[16,25,768]{2,1,0:T(8,128)(2,1)} %copy.256), calls=%async_computation.9 | async-start | bytes 1572864 | tf_op jit(solution)/shard_map/all_to_all | solution.py:514
  120.8 39.8 %collective-permute-start.18 = (bf16[4,624,128]{2,1,0:T(8,128)(2,1)}, bf16[4,624,128]{2,1,0:T(8,128)(2,1)}, u32[]{:S(2)}, u32[]{:S(2)}) collective-permute-start(bf16[4,624,128]{2,1,0:T(8,128)(2,1)} %pad_maximum_fusion.19.refs_0_), channel_id=1, source_target_pairs={{0,24},{1,25},{2,26},{3,27},{4,28},{5,29},{6,30},{7,31},{8,16},{9,... | collective-permute-start | bytes 1916936 | tf_op jit(solution)/shard_map/ppermute | solution.py:147
  133.2 38.6 %collective-permute-start.17 = (bf16[4,624,128]{2,1,0:T(8,128)(2,1)}, bf16[4,624,128]{2,1,0:T(8,128)(2,1)}, u32[]{:S(2)}, u32[]{:S(2)}) collective-permute-start(bf16[4,624,128]{2,1,0:T(8,128)(2,1)} %pad_maximum_fusion.19.refs_0_), channel_id=1, source_target_pairs={{0,16},{1,17},{2,18},{3,19},{4,20},{5,21},{6,22},{7,23},{8,24},{9,... | collective-permute-start | bytes 1916936 | tf_op jit(solution)/shard_map/ppermute | solution.py:147
  146.2 41.8 %collective-permute-start.8 = (bf16[4,624,128]{2,1,0:T(8,128)(2,1)}, bf16[4,624,128]{2,1,0:T(8,128)(2,1)}, u32[]{:S(2)}, u32[]{:S(2)}) collective-permute-start(bf16[4,624,128]{2,1,0:T(8,128)(2,1)} %pad_maximum_fusion.18.refs_0_), channel_id=1, source_target_pairs={{0,24},{1,25},{2,26},{3,27},{4,28},{5,29},{6,30},{7,31},{8,16},{9,... | collective-permute-start | bytes 1916936 | tf_op jit(solution)/shard_map/ppermute | solution.py:147
  160.6 35.6 %collective-permute-start.7 = (bf16[4,624,128]{2,1,0:T(8,128)(2,1)}, bf16[4,624,128]{2,1,0:T(8,128)(2,1)}, u32[]{:S(2)}, u32[]{:S(2)}) collective-permute-start(bf16[4,624,128]{2,1,0:T(8,128)(2,1)} %pad_maximum_fusion.18.refs_0_), channel_id=1, source_target_pairs={{0,16},{1,17},{2,18},{3,19},{4,20},{5,21},{6,22},{7,23},{8,24},{9,... | collective-permute-start | bytes 1916936 | tf_op jit(solution)/shard_map/ppermute | solution.py:147
  165.1 50.9 %all-to-all-start.11 = ((bf16[16,25,768]{2,1,0:T(8,128)(2,1)}), bf16[16,25,768]{2,1,0:T(8,128)(2,1)}, u32[]{:S(2)}, u32[]{:S(2)}) async-start(bf16[16,25,768]{2,1,0:T(8,128)(2,1)} %copy.263), calls=%async_computation.11 | async-start | bytes 1572864 | tf_op jit(solution)/shard_map/all_to_all | solution.py:514
  171.8 38.4 %collective-permute-start.6 = (bf16[4,624,128]{2,1,0:T(8,128)(2,1)}, bf16[4,624,128]{2,1,0:T(8,128)(2,1)}, u32[]{:S(2)}, u32[]{:S(2)}) collective-permute-start(bf16[4,624,128]{2,1,0:T(8,128)(2,1)} %pad_maximum_fusion.18.refs_0_), channel_id=1, source_target_pairs={{0,8},{1,9},{2,10},{3,11},{4,12},{5,13},{6,14},{7,15},{8,0},{9,1},... | collective-permute-start | bytes 1916936 | tf_op jit(solution)/shard_map/ppermute | solution.py:147
  173.7 37.1 %collective-permute-start.42 = (bf16[4,624,128]{2,1,0:T(8,128)(2,1)}, bf16[4,624,128]{2,1,0:T(8,128)(2,1)}, u32[]{:S(2)}, u32[]{:S(2)}) collective-permute-start(bf16[4,624,128]{2,1,0:T(8,128)(2,1)} %collective-permute-done.38.refs_3_), channel_id=1, source_target_pairs={{0,1},{1,0},{2,3},{3,2},{4,5},{5,4},{6,7},{7,6},{8,9},{9,8},{10,11... | collective-permute-start | bytes 1916936 | tf_op jit(solution)/shard_map/ppermute | solution.py:147
  173.7 37.1 %collective-permute-start.41 = (bf16[4,624,128]{2,1,0:T(8,128)(2,1)}, bf16[4,624,128]{2,1,0:T(8,128)(2,1)}, u32[]{:S(2)}, u32[]{:S(2)}) collective-permute-start(bf16[4,624,128]{2,1,0:T(8,128)(2,1)} %collective-permute-done.37.refs_2_), channel_id=1, source_target_pairs={{0,1},{1,0},{2,3},{3,2},{4,5},{5,4},{6,7},{7,6},{8,9},{9,8},{10,11... | collective-permute-start | bytes 1916936 | tf_op jit(solution)/shard_map/ppermute | solution.py:147
  212.9 40.0 %collective-permute-start.20 = (bf16[4,624,128]{2,1,0:T(8,128)(2,1)}, bf16[4,624,128]{2,1,0:T(8,128)(2,1)}, u32[]{:S(2)}, u32[]{:S(2)}) collective-permute-start(bf16[4,624,128]{2,1,0:T(8,128)(2,1)} %collective-permute-done.16.refs_1_), channel_id=1, source_target_pairs={{0,1},{1,0},{2,3},{3,2},{4,5},{5,4},{6,7},{7,6},{8,9},{9,8},{10,11... | collective-permute-start | bytes 1916936 | tf_op jit(solution)/shard_map/ppermute | solution.py:147
  218.0 43.4 %collective-permute-start.29 = (bf16[4,624,128]{2,1,0:T(8,128)(2,1)}, bf16[4,624,128]{2,1,0:T(8,128)(2,1)}, u32[]{:S(2)}, u32[]{:S(2)}) collective-permute-start(bf16[4,624,128]{2,1,0:T(8,128)(2,1)} %pad_maximum_fusion.20.refs_0_), channel_id=1, source_target_pairs={{0,1},{1,0},{2,3},{3,2},{4,5},{5,4},{6,7},{7,6},{8,9},{9,8},{10,11... | collective-permute-start | bytes 1916936 | tf_op jit(solution)/shard_map/ppermute | solution.py:147
  218.2 43.3 %collective-permute-start.32 = (bf16[4,624,128]{2,1,0:T(8,128)(2,1)}, bf16[4,624,128]{2,1,0:T(8,128)(2,1)}, u32[]{:S(2)}, u32[]{:S(2)}) collective-permute-start(bf16[4,624,128]{2,1,0:T(8,128)(2,1)} %collective-permute-done.28.refs_3_), channel_id=1, source_target_pairs={{0,1},{1,0},{2,3},{3,2},{4,5},{5,4},{6,7},{7,6},{8,9},{9,8},{10,11... | collective-permute-start | bytes 1916936 | tf_op jit(solution)/shard_map/ppermute | solution.py:147
  218.6 42.9 %collective-permute-start.31 = (bf16[4,624,128]{2,1,0:T(8,128)(2,1)}, bf16[4,624,128]{2,1,0:T(8,128)(2,1)}, u32[]{:S(2)}, u32[]{:S(2)}) collective-permute-start(bf16[4,624,128]{2,1,0:T(8,128)(2,1)} %collective-permute-done.27.refs_2_), channel_id=1, source_target_pairs={{0,1},{1,0},{2,3},{3,2},{4,5},{5,4},{6,7},{7,6},{8,9},{9,8},{10,11... | collective-permute-start | bytes 1916936 | tf_op jit(solution)/shard_map/ppermute | solution.py:147
  218.7 42.8 %collective-permute-start.30 = (bf16[4,624,128]{2,1,0:T(8,128)(2,1)}, bf16[4,624,128]{2,1,0:T(8,128)(2,1)}, u32[]{:S(2)}, u32[]{:S(2)}) collective-permute-start(bf16[4,624,128]{2,1,0:T(8,128)(2,1)} %collective-permute-done.26.refs_1_), channel_id=1, source_target_pairs={{0,1},{1,0},{2,3},{3,2},{4,5},{5,4},{6,7},{7,6},{8,9},{9,8},{10,11... | collective-permute-start | bytes 1916936 | tf_op jit(solution)/shard_map/ppermute | solution.py:147
  295.4 53.4 %all-to-all-start = ((bf16[16,25,768]{2,1,0:T(8,128)(2,1)}), bf16[16,25,768]{2,1,0:T(8,128)(2,1)S(1)}, u32[]{:S(2)}, u32[]{:S(2)}) async-start(bf16[16,25,768]{2,1,0:T(8,128)(2,1)} %reshape.932), calls=%async_computation | async-start | bytes 1572864 | tf_op jit(solution)/shard_map/all_to_all | solution.py:514
  348.8 46.8 %all-to-all-start.3 = ((bf16[16,25,768]{2,1,0:T(8,128)(2,1)}), bf16[16,25,768]{2,1,0:T(8,128)(2,1)S(1)}, u32[]{:S(2)}, u32[]{:S(2)}) async-start(bf16[16,25,768]{2,1,0:T(8,128)(2,1)} %reshape.942), calls=%async_computation.3 | async-start | bytes 1572864 | tf_op jit(solution)/shard_map/all_to_all | solution.py:514
  626.8 52.9 %all-to-all-start.10 = ((bf16[2,200,768]{2,0,1:T(2,128)(2,1)}), bf16[2,200,768]{2,0,1:T(2,128)(2,1)S(1)}, u32[]{:S(2)}, u32[]{:S(2)}) async-start(bf16[2,200,768]{2,0,1:T(2,128)(2,1)} %copy.259), calls=%async_computation.10 | async-start | bytes 1228800 | tf_op jit(solution)/shard_map/all_to_all | solution.py:519
  656.0 248.3 %collective-permute-start.57 = (bf16[4,4,624,128]{3,2,1,0:T(8,128)(2,1)}, bf16[4,4,624,128]{3,2,1,0:T(8,128)(2,1)}, u32[]{:S(2)}, u32[]{:S(2)}) collective-permute-start(bf16[4,4,624,128]{3,2,1,0:T(8,128)(2,1)} %bitcast.652), channel_id=1, source_target_pairs={{0,1},{1,0},{2,3},{3,2},{4,5},{5,4},{6,7},{7,6},{8,9},{9,8},{10,11... | collective-permute-start | bytes 7667720 | tf_op jit(solution)/shard_map/ppermute | solution.py:147
  678.9 231.3 %collective-permute-start.64 = (bf16[4,4,624,128]{3,2,1,0:T(8,128)(2,1)}, bf16[4,4,624,128]{3,2,1,0:T(8,128)(2,1)}, u32[]{:S(2)}, u32[]{:S(2)}) collective-permute-start(bf16[4,4,624,128]{3,2,1,0:T(8,128)(2,1)} %bitcast.651), channel_id=1, source_target_pairs={{0,1},{1,0},{2,3},{3,2},{4,5},{5,4},{6,7},{7,6},{8,9},{9,8},{10,11... | collective-permute-start | bytes 7667720 | tf_op jit(solution)/shard_map/ppermute | solution.py:147
  736.5 56.6 %all-to-all-start.2 = ((bf16[2,200,768]{2,0,1:T(2,128)(2,1)}), bf16[2,200,768]{2,0,1:T(2,128)(2,1)}, u32[]{:S(2)}, u32[]{:S(2)}) async-start(bf16[2,200,768]{2,0,1:T(2,128)(2,1)} %copy.226), calls=%async_computation.2 | async-start | bytes 1228800 | tf_op jit(solution)/shard_map/all_to_all | solution.py:519
  870.6 116.8 %collective-permute-start.43 = (bf16[4,4,624,128]{3,2,1,0:T(8,128)(2,1)}, bf16[4,4,624,128]{3,2,1,0:T(8,128)(2,1)}, u32[]{:S(2)}, u32[]{:S(2)}) collective-permute-start(bf16[4,4,624,128]{3,2,1,0:T(8,128)(2,1)} %bitcast.653), channel_id=1, source_target_pairs={{0,1},{1,0},{2,3},{3,2},{4,5},{5,4},{6,7},{7,6},{8,9},{9,8},{10,11... | collective-permute-start | bytes 7667720 | tf_op jit(solution)/shard_map/ppermute | solution.py:147
  897.7 95.0 %collective-permute-start.50 = (bf16[4,4,624,128]{3,2,1,0:T(8,128)(2,1)}, bf16[4,4,624,128]{3,2,1,0:T(8,128)(2,1)}, u32[]{:S(2)}, u32[]{:S(2)}) collective-permute-start(bf16[4,4,624,128]{3,2,1,0:T(8,128)(2,1)} %bitcast.654), channel_id=1, source_target_pairs={{0,1},{1,0},{2,3},{3,2},{4,5},{5,4},{6,7},{7,6},{8,9},{9,8},{10,11... | collective-permute-start | bytes 7667720 | tf_op jit(solution)/shard_map/ppermute | solution.py:147
  996.2 38.5 %collective-permute-start.51 = (bf16[4,624,128]{2,1,0:T(8,128)(2,1)S(1)}, bf16[4,624,128]{2,1,0:T(8,128)(2,1)S(1)}, u32[]{:S(2)}, u32[]{:S(2)}) collective-permute-start(bf16[4,624,128]{2,1,0:T(8,128)(2,1)S(1)} %get-tuple-element.143), channel_id=1, source_target_pairs={{0,8},{1,9},{2,10},{3,11},{4,12},{5,13},{6,14},{7,15},{8,0},{9,1},... | collective-permute-start | bytes 1916936 | tf_op jit(solution)/shard_map/ppermute | solution.py:147
  1003.9 42.9 %collective-permute-start.53 = (bf16[4,624,128]{2,1,0:T(8,128)(2,1)S(1)}, bf16[4,624,128]{2,1,0:T(8,128)(2,1)S(1)}, u32[]{:S(2)}, u32[]{:S(2)}) collective-permute-start(bf16[4,624,128]{2,1,0:T(8,128)(2,1)S(1)} %get-tuple-element.144), channel_id=1, source_target_pairs={{0,24},{1,25},{2,26},{3,27},{4,28},{5,29},{6,30},{7,31},{8,16},{9,... | collective-permute-start | bytes 1916936 | tf_op jit(solution)/shard_map/ppermute | solution.py:147
  1007.4 40.8 %collective-permute-start.52 = (bf16[4,624,128]{2,1,0:T(8,128)(2,1)S(1)}, bf16[4,624,128]{2,1,0:T(8,128)(2,1)S(1)}, u32[]{:S(2)}, u32[]{:S(2)}) collective-permute-start(bf16[4,624,128]{2,1,0:T(8,128)(2,1)S(1)} %get-tuple-element.145), channel_id=1, source_target_pairs={{0,16},{1,17},{2,18},{3,19},{4,20},{5,21},{6,22},{7,23},{8,24},{9,... | collective-permute-start | bytes 1916936 | tf_op jit(solution)/shard_map/ppermute | solution.py:147
  (231 other events, 3306.9 us)

commit v2 on v1

v2 whole, which is shorter than its diff:
```python
import math

import jax
import jax.numpy as jnp
from jax import lax
from jax.experimental import pallas as pl
from jax.experimental.pallas import tpu as pltpu
from jax.sharding import PartitionSpec as P

H = 12
FF = 3072
EPS = 1e-06
MASKED = -1000000000.0
LANES = 128
BOTH = ("dp", "sp")
BF = jnp.bfloat16
F32 = jnp.float32


def segment_shapes(d, ff):
    return [
        (d,), (d,), (d, 3 * d), (d,), (d,), (d, d), (d,), (d, d), (d,),
        (d,), (d,), (d, 3 * d), (d,), (d,), (d, d), (d,),
        (d,), (d,), (d, ff), (ff,), (ff, d), (d,),
    ]


def pair_masks(rows):
    lane = lax.broadcasted_iota(jnp.int32, (rows, LANES), 1)
    return lane < LANES // 2


def dot_l(a, b):
    return lax.dot_general(a, b, (((0,), (0,)), ((), ())), preferred_element_type=F32)


def dot(a, b):
    return jnp.dot(a, b, preferred_element_type=F32)


def turn(t):
    return jnp.transpose(t.astype(F32)).astype(BF)


def halves(t):
    half = LANES // 2
    zero = jnp.zeros_like(t[:half])
    return jnp.concatenate([t[:half], zero]), jnp.concatenate([zero, t[half:]])


def exp_of(k, q_turned, keep):
    s = jnp.where(keep, dot(k, q_turned), MASKED)
    e = jnp.exp(s - jnp.max(s, axis=0, keepdims=True))
    return e, 1.0 / jnp.sum(e, axis=0, keepdims=True)


def softmax_of(q, k, keep):
    s = lax.dot_general(q, k, (((1,), (1,)), ((), ())), preferred_element_type=F32)
    s = jnp.where(keep, s, MASKED)
    e = jnp.exp(s - jnp.max(s, axis=-1, keepdims=True))
    return e.astype(BF), 1.0 / jnp.sum(e, axis=-1, keepdims=True)


def attend_kernel(q_ref, k_ref, v_ref, m_ref, o_ref):
    rows, width = q_ref.shape[1], q_ref.shape[2]
    keep = m_ref[0] > 0.5
    first = pair_masks(rows)
    for at in range(0, width, LANES):
        q = q_ref[0, :, at : at + LANES] * jnp.asarray(0.125, BF)
        k = k_ref[0, :, at : at + LANES]
        v = v_ref[0, :, at : at + LANES]
        zero = jnp.zeros_like(q)
        ea, scale_a = softmax_of(jnp.where(first, q, zero), k, keep)
        eb, scale_b = softmax_of(jnp.where(first, zero, q), k, keep)
        o_ref[0, :, at : at + LANES] = jnp.where(first, dot(ea, v) * scale_a, dot(eb, v) * scale_b).astype(BF)


def attend_back_kernel(q_ref, k_ref, v_ref, m_ref, d_ref, o_ref):
    rows, width = q_ref.shape[1], q_ref.shape[2]
    d_model = o_ref.shape[2] // 3
    keep = jnp.broadcast_to(m_ref[0], (rows, rows)) > 0.5
    half = LANES // 2
    first = pair_masks(rows)
    for at in range(0, width, LANES):
        q = q_ref[0, :, at : at + LANES] * jnp.asarray(0.125, BF)
        k = k_ref[0, :, at : at + LANES]
        v = v_ref[0, :, at : at + LANES]
        d = d_ref[0, :, at : at + LANES]
        k_turned = turn(k)
        qs, ds_ = halves(turn(q)), halves(turn(d))
        dqs, dks, dvs = [], [], []
        for head in range(2):
            e, scale = exp_of(k, qs[head], keep)
            p = e * scale
            dp = dot(v, ds_[head])
            ds = (p * (dp - jnp.sum(p * dp, axis=0, keepdims=True))).astype(BF)
            dqs.append(dot(k_turned[head * half : (head + 1) * half], ds))
            dks.append(dot(ds, q))
            dvs.append(dot(p.astype(BF), d))
        results = (
            jnp.transpose(jnp.concatenate(dqs) * 0.125),
            jnp.where(first, *dks),
            jnp.where(first, *dvs),
        )
        for third, result in enumerate(results):
            to = pl.multiple_of(third * d_model + pl.program_id(1) * width + at, LANES)
            o_ref[0, :, pl.ds(to, LANES)] = result.astype(BF)


def head_split(width):
    for parts in (2, 3, 1):
        if width % (parts * LANES) == 0:
            return parts
    return 1


def attention_specs(packed, keep, d):
    parts = head_split(d)
    w = d // parts
    rows = packed.shape[1]
    own = lambda third: pl.BlockSpec((1, rows, w), lambda i, j: (i, 0, third * parts + j))
    one = keep.shape[0] == 1
    mask = pl.BlockSpec((1,) + keep.shape[1:], lambda i, j: (0 if one else i, 0, 0))
    flat = pl.BlockSpec((1, rows, w), lambda i, j: (i, 0, j))
    return parts, own, mask, flat


def attend(packed, keep, d):
    n, rows, _ = packed.shape
    parts, own, mask, flat = attention_specs(packed, keep, d)
    return pl.pallas_call(
        attend_kernel,
        grid=(n, parts),
        in_specs=[own(0), own(1), own(2), mask],
        out_specs=flat,
        out_shape=jax.ShapeDtypeStruct((n, rows, d), BF),
        cost_estimate=pl.CostEstimate(
            flops=4 * n * rows * rows * d * 2,
            bytes_accessed=n * rows * d * 8,
            transcendentals=n * rows * rows * (d // 64),
        ),
        name="attend",
    )(packed, packed, packed, keep)


def attend_back(packed, keep, grad, d):
    n, rows, _ = packed.shape
    parts, own, mask, flat = attention_specs(packed, keep, d)
    return pl.pallas_call(
        attend_back_kernel,
        grid=(n, parts),
        in_specs=[own(0), own(1), own(2), mask, flat],
        out_specs=pl.BlockSpec((1, rows, 3 * d), lambda i, j: (i, 0, 0)),
        out_shape=jax.ShapeDtypeStruct((n, rows, 3 * d), BF),
        cost_estimate=pl.CostEstimate(
            flops=10 * n * rows * rows * d * 2,
            bytes_accessed=n * rows * d * 14,
            transcendentals=n * rows * rows * (d // 64),
        ),
        name="attend_back",
    )(packed, packed, packed, keep, grad)


def flip_perm(dp_bits=0, sp_bits=0):
    return [(d * 8 + s, (d ^ dp_bits) * 8 + (s ^ sp_bits)) for d in range(4) for s in range(8)]


def send(value, dp_bits=0, sp_bits=0):
    return lax.ppermute(value, BOTH, flip_perm(dp_bits, sp_bits))


def pick(stack, at):
    return lax.dynamic_index_in_dim(stack, at, 0, keepdims=False)


def place_of():
    dp, sp = lax.axis_index("dp"), lax.axis_index("sp")
    return jnp.stack([dp, sp >> 1, sp & 1]).astype(jnp.int32)


def round_up(value, step):
    return -(-value // step) * step


class Plan:
    def __init__(self, rows):
        self.rows = rows
        self.part = round_up(-(-rows // 4), 16)
        self.gap = 4 * self.part - rows
        self.block = 32 * self.part

    def padded(self, row):
        return row + self.gap * (row // self.rows)


def assemble_kernel(pos_ref, *refs):
    ins, out, buf, sem_in, sem_out = refs[:8], refs[8], refs[9], refs[10], refs[11]
    dp, z, core = pos_ref[0], pos_ref[1], pos_ref[2]
    loads = []
    for j in range(8):
        for k in range(4):
            at = j * 4 + k
            load = pltpu.make_async_copy(ins[j].at[k], buf.at[at], sem_in.at[at])
            load.start()
            loads.append(load)
    stores = []
    for j in range(8):
        for k in range(4):
            at = j * 4 + k
            loads[at].wait()
            to = ((z ^ k) * 2 + (core ^ (j // 4))) * 4 + (dp ^ (j % 4))
            store = pltpu.make_async_copy(buf.at[at], out.at[to], sem_out.at[at])
            store.start()
            stores.append(store)
    for store in stores:
        store.wait()


def assemble(pos, pieces):
    part = pieces[0].shape[1]
    any_spec = pl.BlockSpec(memory_space=pl.ANY)
    out = pl.pallas_call(
        assemble_kernel,
        grid_spec=pltpu.PrefetchScalarGridSpec(
            num_scalar_prefetch=1,
            grid=(1,),
            in_specs=[any_spec] * 8,
            out_specs=any_spec,
            scratch_shapes=[
                pltpu.VMEM((32, part, LANES), BF),
                pltpu.SemaphoreType.DMA((32,)),
                pltpu.SemaphoreType.DMA((32,)),
            ],
        ),
        out_shape=jax.ShapeDtypeStruct((32, part, LANES), BF),
        cost_estimate=pl.CostEstimate(flops=0, bytes_accessed=32 * part * LANES * 4, transcendentals=0),
        name="assemble",
    )(pos, *pieces)
    return out.reshape(32 * part, LANES)


def tie(*values):
    return lax.optimization_barrier(values)


class Gather:
    SCHEDULE = (
        ((0, 0),),
        ((0, 1), (1, 0)),
        ((0, 2), (2, 0)),
        ((0, 3), (1, 1), (3, 0)),
        ((1, 2), (2, 1)),
        ((1, 3), (2, 2), (3, 1)),
        ((2, 3), (3, 2)),
        ((3, 3),),
    )

    def __init__(self, shard, plan, pos):
        self.plan, self.pos = plan, pos
        dp = pos[0]
        mine = jnp.pad(shard.reshape(plan.rows, LANES), ((0, plan.gap), (0, 0)))
        mine = mine.reshape(4, plan.part, LANES)
        spread = jnp.zeros_like(mine)
        for k in range(4):
            piece = pick(mine, dp ^ k)
            got = piece if k == 0 else send(piece, k)
            spread = lax.dynamic_update_slice(spread, got[None], (dp ^ k, 0, 0))
        self.state = [[spread[b]] for b in range(4)]
        self.stage_number = 0

    def stage(self):
        for b, step in self.SCHEDULE[self.stage_number]:
            now = self.state[b]
            if step == 0:
                now = now + [send(now[0], 0, 2 * k) for k in range(1, 4)]
            elif step == 1:
                line = jnp.stack(now)
                now = [line, send(line, 1), send(line, 2)]
            elif step == 2:
                line, by_x, by_y = now
                now = [line, by_x, by_y, jnp.concatenate([send(by_x[:2], 2), send(by_y[2:], 1)])]
            else:
                now = now + [send(part, 0, 1) for part in now]
            self.state[b] = now
        self.stage_number += 1

    def sync(self, *values):
        self.state, values = tie(self.state, values)
        return values

    def block(self, b):
        return assemble(self.pos, self.state[b])


CHUNK = 1152


def unflatten(src, base, off, rows, width, plan):
    lanes = width // LANES
    step_rows = CHUNK // lanes
    size = src.shape[0]
    window = round_up(CHUNK + plan.gap + 16, 16)

    def where_from(i):
        first = off + CHUNK * i
        at = first + plan.gap * (first // plan.rows) - base
        return first, at, jnp.minimum(at // 16 * 16, size - window)

    def kernel(in_ref, out_ref, wide):
        first, at, start = where_from(pl.program_id(0))
        delta = at - start
        left = plan.rows - first % plan.rows
        wide[...] = in_ref[...].astype(F32)

        @pl.when(left >= CHUNK)
        def _():
            for b in range(lanes):
                got = wide[pl.ds(delta + b, step_rows, stride=lanes), :]
                out_ref[:, b * LANES : (b + 1) * LANES] = got.astype(BF)

        @pl.when(left < CHUNK)
        def _():
            row = lax.broadcasted_iota(jnp.int32, (step_rows, LANES), 0) * lanes
            for b in range(lanes):
                near = wide[pl.ds(delta + b, step_rows, stride=lanes), :]
                far = wide[pl.ds(delta + b + plan.gap, step_rows, stride=lanes), :]
                got = jnp.where(row + b < left, near, far)
                out_ref[:, b * LANES : (b + 1) * LANES] = got.astype(BF)

    return pl.pallas_call(
        kernel,
        grid=(rows // step_rows,),
        in_specs=[
            pl.BlockSpec(
                (pl.Element(window), pl.Element(LANES)),
                lambda i: (pl.multiple_of(where_from(i)[2], 16), 0),
            )
        ],
        out_specs=pl.BlockSpec((step_rows, width), lambda i: (i, 0)),
        out_shape=jax.ShapeDtypeStruct((rows, width), BF),
        scratch_shapes=[pltpu.VMEM((window, LANES), F32)],
        cost_estimate=pl.CostEstimate(flops=0, bytes_accessed=rows * width * 4, transcendentals=0),
        name="unflatten",
    )(src)


def flatten(pos, b, mats, vecs, plan):
    part, span = plan.part, plan.rows
    shapes = []
    for off, mat in mats:
        lanes = mat.shape[1] // LANES
        shapes.append((off, mat.shape[0], lanes, round_up(-(-span // lanes) + 8, 8)))
    pad = round_up(max([w * c for _, _, c, w in shapes] + [v.shape[0] for _, v in vecs]), 8) + 8

    def first_row(t, pos_ref):
        z = pos_ref[1] ^ (t % 4)
        core = jnp.where(t < 4, 1 - pos_ref[2], pos_ref[2])
        return (8 * b + z * 2 + core) * span

    def start_row(p0, off, rows, lanes, w):
        return jnp.minimum(jnp.maximum(p0 - off, 0) // lanes // 8 * 8, rows - w)

    def kernel(pos_ref, *refs):
        ins = refs[: len(mats)]
        vins = refs[len(mats) : len(mats) + len(vecs)]
        theirs, ours, wide = refs[len(mats) + len(vecs) :]
        t = pl.program_id(0)
        p0 = first_row(t, pos_ref)
        for (off, rows, lanes, w), ref in zip(shapes, ins):

            @pl.when((p0 + span > off) & (p0 < off + rows * lanes))
            def _():
                at = off + lanes * start_row(p0, off, rows, lanes, w) - p0 + pad
                for c in range(lanes):
                    wide[pl.ds(at + c, w, stride=lanes), :] = ref[:, c * LANES : (c + 1) * LANES]

        for (off, vec), ref in zip(vecs, vins):
            n = vec.shape[0]

            @pl.when((p0 + span > off) & (p0 < off + n))
            def _():
                at = off - p0 + pad
                for r in range(n):
                    wide[pl.ds(at + r, 1), :] = ref[r : r + 1, :]

        for out, mine in ((theirs, t < 4), (ours, t >= 4)):

            @pl.when(mine)
            def _():
                for k in range(4):
                    at = pl.multiple_of(pad + (pos_ref[0] ^ k) * part, 8)
                    out[k, 0] = wide[pl.ds(at, part), :].astype(BF)

    in_specs = [
        pl.BlockSpec(
            (pl.Element(w), pl.Element(lanes * LANES)),
            lambda t, p, off=off, rows=rows, lanes=lanes, w=w: (
                pl.multiple_of(start_row(first_row(t, p), off, rows, lanes, w), 8),
                0,
            ),
        )
        for off, rows, lanes, w in shapes
    ] + [pl.BlockSpec(v.shape, lambda t, p: (0, 0)) for _, v in vecs]
    shape = jax.ShapeDtypeStruct((4, 4, part, LANES), BF)
    return pl.pallas_call(
        kernel,
        grid_spec=pltpu.PrefetchScalarGridSpec(
            num_scalar_prefetch=1,
            grid=(8,),
            in_specs=in_specs,
            out_specs=[
                pl.BlockSpec((4, 1, part, LANES), lambda t, p: (0, jnp.minimum(t, 3), 0, 0)),
                pl.BlockSpec((4, 1, part, LANES), lambda t, p: (0, jnp.maximum(t - 4, 0), 0, 0)),
            ],
            scratch_shapes=[pltpu.VMEM((2 * pad + 4 * part, LANES), F32)],
        ),
        out_shape=[shape, shape],
        cost_estimate=pl.CostEstimate(flops=0, bytes_accessed=plan.block * LANES * 6, transcendentals=0),
        name="flatten",
    )(pos, *[m for _, m in mats], *[v for _, v in vecs])


class Reduce:
    def __init__(self, theirs, ours):
        self.state = (theirs, ours)
        self.stage_number = 0

    def stage(self):
        s, now = self.stage_number, self.state
        wide = lambda *parts: sum(p.astype(F32) for p in parts)
        if s == 0:
            theirs, ours = now
            self.state = (ours, send(theirs, 0, 1))
        elif s == 1:
            ours = wide(*now).astype(BF)
            self.state = (ours, send(ours[3, :2], 1), send(ours[3, 2:], 2))
        elif s == 2:
            ours, by_x, by_y = now
            to_x = jnp.concatenate([ours[1, :2], wide(ours[1, 2:], by_y).astype(BF)])
            to_y = jnp.concatenate([wide(ours[2, :2], by_x).astype(BF), ours[2, 2:]])
            self.state = (ours[0], send(to_x, 1), send(to_y, 2))
        elif s == 3:
            line = wide(*now).astype(BF)
            self.state = (line[0],) + tuple(send(line[k], 0, 2 * k) for k in range(1, 4))
        else:
            self.state = wide(*now)
        self.stage_number = s + 1


def advance(reduces, *values):
    states, values = tie([r.state for r in reduces], values)
    for r, state in zip(reduces, states):
        r.state = state
        r.stage()
    return values


def return_quarters(quarters, plan, pos):
    stack = jnp.stack(quarters)
    dp = pos[0]
    out = jnp.zeros_like(stack)
    for k in range(4):
        piece = pick(stack, dp ^ k)
        got = piece if k == 0 else send(piece, k)
        out = lax.dynamic_update_slice(out, got[None], (dp ^ k, 0, 0))
    return out.reshape(4 * plan.part, LANES)[: plan.rows].reshape(-1)


def segment_rows(d, ff):
    spans, at = [], 0
    for shape in segment_shapes(d, ff):
        length = math.prod(shape)
        spans.append((at, at + length, shape))
        at += length
    return spans, at


def cut(blocks, lo, hi):
    size = blocks[0].shape[0]
    pieces = []
    for i, block in enumerate(blocks):
        a, b = max(lo, i * size), min(hi, (i + 1) * size)
        if a < b:
            pieces.append(block[a - i * size : b - i * size])
    return pieces[0] if len(pieces) == 1 else jnp.concatenate(pieces)


def cut_padded(blocks, lo, hi, plan):
    pieces = []
    while lo < hi:
        end = min(hi, (lo // plan.rows + 1) * plan.rows)
        pieces.append(cut(blocks, plan.padded(lo), plan.padded(lo) + end - lo))
        lo = end
    return pieces[0] if len(pieces) == 1 else jnp.concatenate(pieces)


def matrix_of(blocks, lo, shape, plan):
    rows, width = shape
    first = plan.padded(lo)
    last = plan.padded(lo + rows * (width // LANES) - 1) + 1
    a, b = first // plan.block, (last - 1) // plan.block
    if a == b:
        return unflatten(blocks[a], a * plan.block, lo, rows, width, plan)
    base = first // 16 * 16
    return unflatten(cut(blocks, base, round_up(last, 16)), base, lo, rows, width, plan)


def stats(v):
    center = v - jnp.mean(v, axis=-1, keepdims=True)
    scale = lax.rsqrt(jnp.mean(center * center, axis=-1, keepdims=True) + EPS)
    return center * scale, scale


def norm_back(hat, scale, gain, grad):
    inner = grad * gain
    back = scale * (
        inner
        - jnp.mean(inner, axis=-1, keepdims=True)
        - hat * jnp.mean(inner * hat, axis=-1, keepdims=True)
    )
    return back, jnp.sum(grad * hat, axis=0), jnp.sum(grad, axis=0)


def product_back(grad_rows, weight):
    return lax.dot_general(grad_rows, weight, (((1,), (1,)), ((), ())), preferred_element_type=F32)


def row_sum(grad):
    return jnp.sum(grad.astype(F32), axis=0)


def gelu_pair(u):
    half = 0.5 * (1.0 + lax.erf(u * (2.0 ** -0.5)))
    slope = half + u * jnp.exp(-0.5 * u * u) * ((2.0 * math.pi) ** -0.5)
    return (u * half).astype(BF), slope


def bias_row(q_bias, v_bias):
    return jnp.concatenate([q_bias, jnp.zeros_like(q_bias), v_bias])


def shards(inputs, cotangent, params, clip_counts, slot_live):
    micro, clips, frames, places, d = inputs.shape
    n_sp = lax.axis_size("sp")
    n_dev = lax.axis_size("dp") * n_sp
    full_length = params.shape[0] * n_dev
    tokens = micro * clips * frames * places
    seqs = micro * clips * frames // n_sp
    length = places * n_sp
    rows = params.shape[0] // LANES
    fast = n_sp == 8 and n_dev == 32 and params.shape[0] % (2 * LANES) == 0
    spans, used = segment_rows(d, FF)
    inputs_now, cot_now, live_now = inputs, cotangent, slot_live

    if fast:
        plan, pos = Plan(rows), place_of()
        blocks = [None] * 4
        made = {}

        def piece(i):
            if i not in made:
                lo, hi, shape = spans[i]
                if len(shape) == 1:
                    made[i] = cut_padded(blocks, lo // LANES, hi // LANES, plan).reshape(shape).astype(F32)
                else:
                    made[i] = matrix_of(blocks, lo // LANES, shape, plan)
            return made[i]

        gather = Gather(params, plan, pos)
        for _ in range(4):
            gather.stage()
            cot_now, live_now = gather.sync(cot_now, live_now)
        blocks[0] = gather.block(0)
        gather.stage()
        made[2], made[5] = gather.sync(piece(2), piece(5))
        gather.stage()
    else:
        flat = lax.all_gather(params, BOTH, axis=0, tiled=True).reshape(-1, LANES)

        def piece(i):
            lo, hi, shape = spans[i]
            got = flat[lo // LANES : hi // LANES].reshape(shape)
            return got.astype(F32) if len(shape) == 1 else got

    in_use = (jnp.arange(clips, dtype=jnp.int32)[None] < clip_counts).astype(F32)
    live = live_now.astype(F32) * in_use[:, :, None]
    live_low = live.astype(BF)[:, :, None, :, None]

    def to_frames(value):
        return lax.all_to_all(
            value.reshape(micro, clips * frames, places, d), "sp", split_axis=1, concat_axis=2, tiled=True
        ).reshape(seqs * length, d)

    def to_places(value):
        return lax.all_to_all(
            value.reshape(micro, seqs // micro, length, d), "sp", split_axis=2, concat_axis=1, tiled=True
        ).reshape(micro, clips, frames, places, d)

    live_sent = jnp.broadcast_to(live.astype(BF)[:, :, None], (micro, clips, frames, places)).reshape(
        micro, clips * frames, places
    )
    live_frames = lax.all_to_all(live_sent, "sp", split_axis=1, concat_axis=2, tiled=True)
    keep_rows = live_frames.astype(F32).reshape(seqs, 1, length)
    keep_s = keep_rows.reshape(seqs, length, 1)
    dx3 = to_frames(cot_now * live_low)

    span_t = frames * places
    place = jnp.arange(span_t, dtype=jnp.int32) % places
    same = (place[:, None] == place[None]).astype(F32)[None]

    x = inputs_now.reshape(tokens, d).astype(F32)
    hat1, scale1 = stats(x)
    tg = piece(0)
    h1 = (hat1 * tg + piece(1)).astype(BF)
    w_qkv_t = piece(2)
    qkv_t = (dot(h1, w_qkv_t) + bias_row(piece(3), piece(4))).astype(BF)
    qkv_t = qkv_t.reshape(micro * clips, span_t, 3 * d)
    if fast:
        (qkv_t,) = gather.sync(qkv_t)
        gather.stage()
    o_t = attend(qkv_t, same, d).reshape(tokens, d)
    if fast:
        o_t, dx3 = gather.sync(o_t, dx3)
        gather.stage()
        blocks[1] = gather.block(1)
    w_out_t = piece(5)
    a_t = (dot(o_t, w_out_t) + piece(6)).astype(BF)
    w_fc = piece(7)
    x1 = (x + dot(a_t, w_fc) + piece(8)).astype(BF)
    if fast:
        (x1,) = gather.sync(x1)
    xb = to_frames(x1)
    if fast:
        blocks[2], blocks[3] = gather.block(2), gather.block(3)

    w_qkv_s, w_out_s, w_up, w_down = piece(11), piece(14), piece(18), piece(20)
    if fast:
        xb, w_qkv_s, w_out_s, w_up, w_down = tie(xb, w_qkv_s, w_out_s, w_up, w_down)
    xb = xb.astype(F32)
    hat2, scale2 = stats(xb)
    sg = piece(9)
    h2 = (hat2 * sg + piece(10)).astype(BF)
    qkv_s = (dot(h2, w_qkv_s) + bias_row(piece(12), piece(13))).astype(BF)
    qkv_s = qkv_s.reshape(seqs, length, 3 * d)
    o_s = attend(qkv_s, keep_rows, d).reshape(-1, d)
    x2 = xb + dot(o_s, w_out_s) + piece(15)
    hat3, scale3 = stats(x2)
    mg = piece(16)
    h3 = (hat3 * mg + piece(17)).astype(BF)
    g, slope = gelu_pair(dot(h3, w_up) + piece(19))
    x3 = (x2 + dot(g, w_down) + piece(21)).astype(BF)
    out = to_places(x3) * live_low

    du = (product_back(dx3, w_down) * slope).astype(BF)
    back3, grad_mg, grad_mb = norm_back(hat3, scale3, mg, product_back(du, w_up))
    dx2 = dx3.astype(F32) + back3
    da_s = dx2.astype(BF)
    do_s = product_back(da_s, w_out_s).astype(BF)
    dqkv_s = attend_back(qkv_s, keep_s, do_s.reshape(seqs, length, d), d).reshape(-1, 3 * d)
    back2, grad_sg, grad_sb = norm_back(hat2, scale2, sg, product_back(dqkv_s, w_qkv_s))
    dx1 = to_places((dx2 + back2).astype(BF)).reshape(tokens, d)

    grads = [None] * len(spans)
    grads[20], grads[21] = dot_l(g, dx3), row_sum(dx3)
    grads[18], grads[19] = dot_l(h3, du), row_sum(du)
    grads[14], grads[15] = dot_l(o_s, da_s), row_sum(da_s)
    grads[16], grads[17] = grad_mg, grad_mb
    grads[9], grads[10] = grad_sg, grad_sb

    def block_of(b):
        size = 8 * rows
        tail = jnp.zeros((full_length - used,), F32)
        mats, vecs, run, run_at = [], [], [], 0
        for i, (lo, hi, shape) in enumerate(spans + [(used, full_length, (full_length - used,))]):
            inside = lo < (b + 1) * size * LANES and hi > b * size * LANES
            if len(shape) == 2 or not inside:
                if run:
                    vecs.append((run_at, jnp.concatenate(run).reshape(-1, LANES)))
                run = []
                if inside:
                    mats.append((lo // LANES, grads[i]))
            else:
                run_at = run_at if run else lo // LANES
                run.append(grads[i] if i < len(grads) else tail)
        if run:
            vecs.append((run_at, jnp.concatenate(run).reshape(-1, LANES)))
        return Reduce(*flatten(pos, b, mats, vecs, plan))

    if fast:
        r3 = block_of(3)
        r3.stage()
        r2 = block_of(2)
        r2.stage()
    grads[11] = dot_l(h2, dqkv_s)
    sums = row_sum(dqkv_s)
    grads[12], grads[13] = sums[:d], sums[2 * d :]
    if fast:
        dx1, grads[11] = advance((r3, r2), dx1, grads[11])

    da_t = product_back(dx1, w_fc).astype(BF)
    do_t = product_back(da_t, w_out_t).astype(BF)
    grads[7], grads[8] = dot_l(a_t, dx1), row_sum(dx1)
    if fast:
        do_t, grads[7] = advance((r3, r2), do_t, grads[7])
        r1 = block_of(1)
        r1.stage()
    dqkv_t = attend_back(qkv_t, same, do_t.reshape(micro * clips, span_t, d), d).reshape(tokens, 3 * d)
    if fast:
        (dqkv_t,) = advance((r3, r2, r1), dqkv_t)
    sums = row_sum(dqkv_t)
    grads[3], grads[4] = sums[:d], sums[2 * d :]
    back1, grads[0], grads[1] = norm_back(hat1, scale1, tg, product_back(dqkv_t, w_qkv_t))
    grads[5], grads[6] = dot_l(o_t, da_t), row_sum(da_t)
    grads[2] = dot_l(h1, dqkv_t)
    input_grad = (dx1.astype(F32) + back1).astype(BF).reshape(inputs.shape)

    if fast:
        (grads[2],) = advance((r3, r2, r1), grads[2])
        r0 = block_of(0)
        r0.stage()
        advance((r1, r0))
        advance((r1, r0))
        advance((r0,))
        advance((r0,))
        param_grad = return_quarters([r0.state, r1.state, r2.state, r3.state], plan, pos)
    else:
        flat = jnp.concatenate([g.reshape(-1) for g in grads] + [jnp.zeros((full_length - used,), F32)])
        param_grad = lax.psum_scatter(flat, BOTH, scatter_dimension=0, tiled=True)
    return (out, input_grad, param_grad)


def solution(mesh):
    tokens = P(None, "dp", None, "sp", None)
    return jax.shard_map(
        shards,
        mesh=mesh,
        in_specs=(tokens, tokens, P(BOTH), P(None, "dp"), P(None, "dp", "sp")),
        out_specs=(tokens, tokens, P(BOTH)),
        check_vma=False,
    )
```

time: 1090 us -> 813 us (0.75)
  Pallas kernels: 306 us -> 212 us
  matrix products: 191 us -> 146 us
  waiting for transfers between devices: 223 us -> 178 us
  starting transfers between devices: 149 us -> 108 us
  other arithmetic: 102 us -> 62.6 us
  local copies, waits for them, and re-layouts: 106 us -> 93.7 us
    ppermute x74 -> x82, waiting for transfers between devices: 201 us -> 130 us  [send(): return lax.ppermute(value, BOTH, flip_perm(dp_bits, sp_bits))]
    pallas_call x4, Pallas kernels: 94.1 us -> 44.7 us  [flatten(): pl.pallas_call(kernel, grid_spec=pltpu.PrefetchScalarGridSpec(num_scalar_...]
    all_to_all x12 -> x4, starting transfers between devices: 55.5 us -> 18.8 us  [the longest x2 9.93 us: to_frames(): lax.all_to_all(value.reshape(micro, clips * frames, places, d), 'sp', spl...]
    pallas_call x6 -> x2, Pallas kernels: 94.5 us -> 63 us  [attend_back(): pl.pallas_call(attend_back_kernel, grid=(n, parts), in_specs=[own(0), own...]
    all_to_all x12 -> x4, waiting for transfers between devices: 21.9 us -> 46.2 us  [the longest x2 29.2 us: to_frames(): lax.all_to_all(value.reshape(micro, clips * frames, places, d), 'sp', spl...]
    dot_general x21 -> x7, matrix products: 65.3 us -> 47.9 us  [product_back(): lax.dot_general(grad_rows, weight, (((1,), (1,)), ((), ())), preferred_el...]
    dot_general x7, matrix products: 63.2 us -> 48 us  [dot_l(): lax.dot_general(a, b, (((0,), (0,)), ((), ())), preferred_element_type=F32)]
    reduce_sum x13 -> x4, other arithmetic: 21.5 us -> 6.45 us  [row_sum(): return jnp.sum(grad.astype(F32), axis=0)]
  transfers between devices with their start and end apart: 87 -> 87, of which waited for: 36 -> 36; matrix products, arithmetic and copies ran while one was open for 22% -> 24% of each run, Pallas kernels for 20% -> 20%
where the time goes in v2:
time: 813 us; the launch traced here: 804 us
  Pallas kernels  212 us (26%)
  waiting for transfers between devices  178 us (22%)
  matrix products  146 us (18%)
  starting transfers between devices  108 us (13%)
  local copies, waits for them, and re-layouts  93.7 us (12%)
  other arithmetic  62.6 us (8%)
    ppermute x82, waiting for transfers between devices, send(): return lax.ppermute(value, BOTH, flip_perm(dp_bits, sp_bits))  130 us
    ppermute x82, starting transfers between devices, send(): return lax.ppermute(value, BOTH, flip_perm(dp_bits, sp_bits))  85.7 us
    pallas_call x2, Pallas kernels, attend_back(): pl.pallas_call(attend_back_kernel, grid=(n, parts), in_specs=[own(0), own...  63 us
    pallas_call x7, Pallas kernels, unflatten(): pl.pallas_call(kernel, grid=(rows // step_rows,), in_specs=[pl.BlockSpec(...  51.5 us
    dot_general x7, matrix products, dot(): return jnp.dot(a, b, preferred_element_type=F32)  50.2 us
    dot_general x7, matrix products, dot_l(): lax.dot_general(a, b, (((0,), (0,)), ((), ())), preferred_element_type=F32)  48 us
    dot_general x7, matrix products, product_back(): lax.dot_general(grad_rows, weight, (((1,), (1,)), ((), ())), preferred_el...  47.9 us
    pallas_call x4, Pallas kernels, flatten(): pl.pallas_call(kernel, grid_spec=pltpu.PrefetchScalarGridSpec(num_scalar_...  44.7 us
  transfers between devices with their start and end apart: 87, of which 36 were waited for; matrix products, arithmetic and copies ran while one was open for 24% of the time, Pallas kernels for 20%

profile of v2, /device:TPU:0, one launch (start us, length us, event | category | flops | bytes accessed | tf_op | source)
XLA Modules:
  0.0 803.7 jit_solution(2626076823785990879)
XLA Ops:
  21.5 8.3 %collective-permute-done.4 = bf16[624,128]{1,0:T(8,128)(2,1)S(1)} collective-permute-done((bf16[624,128]{1,0:T(8,128)(2,1)S(1)}, bf16[624,128]{1,0:T(8,128)(2,1)S(1)}, u32[]{:S(2)}, u32[]{:S(2)}) %collective-permute-start.4) | collective-permute-done | bytes 159776 | tf_op jit(solution)/shard_map/ppermute | solution.py:169
  38.6 8.2 %collective-permute-done.9 = bf16[624,128]{1,0:T(8,128)(2,1)S(1)} collective-permute-done((bf16[624,128]{1,0:T(8,128)(2,1)S(1)}, bf16[624,128]{1,0:T(8,128)(2,1)S(1)}, u32[]{:S(2)}, u32[]{:S(2)}) %collective-permute-start.9) | collective-permute-done | bytes 159776 | tf_op jit(solution)/shard_map/ppermute | solution.py:169
  58.3 9.0 %collective-permute-done.14 = bf16[624,128]{1,0:T(8,128)(2,1)S(1)} collective-permute-done((bf16[624,128]{1,0:T(8,128)(2,1)S(1)}, bf16[624,128]{1,0:T(8,128)(2,1)S(1)}, u32[]{:S(2)}, u32[]{:S(2)}) %collective-permute-start.14) | collective-permute-done | bytes 159776 | tf_op jit(solution)/shard_map/ppermute | solution.py:169
  125.8 8.7 %unflatten.7 = bf16[768,2304]{1,0:T(8,128)(2,1)} custom-call(bf16[19968,128]{1,0:T(8,128)(2,1)} %bitcast.348), custom_call_target="tpu_custom_call" | custom-call | bytes 7077888 | tf_op jit(solution)/shard_map/unflatten/pallas_call | solution.py:330
  158.1 9.3 %fusion.6 = bf16[1200,2304]{1,0:T(8,128)(2,1)} fusion(bf16[768,2304]{1,0:T(8,128)(2,1)S(1)} %copy-done.16, f32[2304]{0:T(1024)S(1)} %fusion.39, f32[1200,768]{1,0:T(8,128)} %reshape.490, f32[768]{0:T(1024)S(1)} %get-tuple-element.422, f32[768]{0:T(1024)S(1)} %get-tuple-element.423, f32[1200]{0:T(1024)} %rsqrt.28, f32[1200]{0:T(1024)} %div.39), kind=kOutput, calls=%fused_computation.13 | convolution fusion | flops 4256870400 | bytes 12779904 | tf_op jit(solution)/shard_map/dot_general | solution.py:38
  183.6 15.0 %attend.2 = bf16[6,200,768]{2,1,0:T(8,128)(2,1)} custom-call(bf16[6,200,2304]{2,1,0:T(8,128)(2,1)} %bitcast.336, bf16[6,200,2304]{2,1,0:T(8,128)(2,1)} %bitcast.337, bf16[6,200,2304]{2,1,0:T(8,128)(2,1)} %bitcast.338, f32[1,200,200]{2,1,0:T(8,128)} %compare_convert_fusion.m_ref), custom_call_target="tpu_custom_call" | custom-call | flops 1474560000 | bytes 7372800 | tf_op jit(solution)/shard_map/attend/pallas_call | solution.py:131
  220.7 8.6 %unflatten.10 = bf16[768,2304]{1,0:T(8,128)(2,1)} custom-call(bf16[19968,128]{1,0:T(8,128)(2,1)} %bitcast.354), custom_call_target="tpu_custom_call" | custom-call | bytes 7077888 | tf_op jit(solution)/shard_map/unflatten/pallas_call | solution.py:330
  259.6 11.1 %unflatten.13 = bf16[3072,768]{1,0:T(8,128)(2,1)} custom-call(bf16[19968,128]{1,0:T(8,128)(2,1)} %bitcast.364), custom_call_target="tpu_custom_call" | custom-call | bytes 9437184 | tf_op jit(solution)/shard_map/unflatten/pallas_call | solution.py:330
  291.6 12.0 %unflatten.12 = bf16[768,3072]{1,0:T(8,128)(2,1)} custom-call(bf16[18800,128]{1,0:T(8,128)(2,1)} %pad_maximum_fusion.in_ref), custom_call_target="tpu_custom_call" | custom-call | bytes 9437184 | tf_op jit(solution)/shard_map/unflatten/pallas_call | solution.py:330
  305.7 29.2 %all-to-all-done.1 = bf16[3,16,25,768]{3,2,0,1:T(8,128)(2,1)S(1)} async-done(((bf16[3,16,25,768]{3,2,0,1:T(8,128)(2,1)}), bf16[3,16,25,768]{3,2,0,1:T(8,128)(2,1)S(1)}, u32[]{:S(2)}, u32[]{:S(2)}) %all-to-all-start.1) | async-done | bytes 1843232 | tf_op jit(solution)/shard_map/all_to_all | solution.py:590
  348.0 15.0 %attend.3 = bf16[6,200,768]{2,1,0:T(8,128)(2,1)} custom-call(bf16[6,200,2304]{2,1,0:T(8,128)(2,1)} %bitcast.342, bf16[6,200,2304]{2,1,0:T(8,128)(2,1)} %bitcast.343, bf16[6,200,2304]{2,1,0:T(8,128)(2,1)} %bitcast.344, f32[6,1,200]{2,1,0:T(1,128)} %reshape.501.m_ref), custom_call_target="tpu_custom_call" | custom-call | flops 1474560000 | bytes 7372800 | tf_op jit(solution)/shard_map/attend/pallas_call | solution.py:131
  367.1 11.9 %multiply_convert_fusion = (bf16[1200,3072]{1,0:T(8,128)(2,1)}, f32[1200,3072]{1,0:T(8,128)}) fusion(f32[3072]{0:T(1024)S(1)} %fusion.41, bf16[768,3072]{1,0:T(8,128)(2,1)S(1)} %bitcast.376, f32[1200,768]{1,0:T(8,128)S(1)} %get-tuple-element.482, f32[768]{0:T(1024)S(1)} %get-tuple-element.412, f32[768]{0:T(1024)S(1)} %get-tuple-element.411, ...), kind=kOutput, calls=%fused_computation.8 | convolution fusion | flops 5689036800 | bytes 30551424 | tf_op jit(solution)/shard_map/dot_general | solution.py:38
  379.0 13.1 %convert_reduce_fusion = (f32[3072]{0:T(1024)}, bf16[1200,3072]{1,0:T(8,128)(2,1)S(1)}) fusion(f32[1200,3072]{1,0:T(8,128)} %get-tuple-element.484, bf16[1200,768]{1,0:T(8,128)(2,1)S(1)} %copy-done.11, bf16[3072,768]{1,0:T(8,128)(2,1)S(1)} %bitcast.378), kind=kOutput, calls=%fused_computation.7 | convolution fusion | flops 5706544128 | bytes 28692480 | tf_op jit(solution)/shard_map/dot_general | solution.py:525
  395.2 10.0 %fusion.64.refs_0_.refs_1_ = f32[768,3072]{1,0:T(8,128)} fusion(bf16[1200,3072]{1,0:T(8,128)(2,1)S(1)} %get-tuple-element.486, f32[1200,768]{1,0:T(8,128)S(1)} %get-tuple-element.482, f32[768]{0:T(1024)S(1)} %get-tuple-element.412, f32[768]{0:T(1024)S(1)} %get-tuple-element.411, f32[1200]{0:T(1024)S(1)} %add_rsqrt_fusion.1, ...), kind=kOutput, calls=%fused_computation.243 | convolution fusion | flops 5666918400 | bytes 20512128 | tf_op jit(solution)/shard_map/dot_general | solution.py:34
  405.1 10.0 %multiply_reduce_fusion.2 = (f32[768]{0:T(1024)S(1)}, f32[1200]{0:T(1024)S(1)}, f32[1200]{0:T(1024)S(1)}, f32[768]{0:T(1024)S(1)}, f32[1200,768]{1,0:T(8,128)S(1)}) fusion(f32[1200,768]{1,0:T(8,128)S(1)} %get-tuple-element.482, f32[1200]{0:T(1024)S(1)} %add_rsqrt_fusion.1, f32[1200]{0:T(1024)S(1)} %broadcast_multiply_fusion.8, ...), kind=kOutput, calls=%fused_computation.54 | convolution fusion | flops 5670600704 | bytes 19492608 | tf_op jit(solution)/shard_map/dot_general | solution.py:525
  423.3 9.2 %fusion.66.refs_1_ = f32[3072,768]{1,0:T(8,128)} fusion(bf16[1200,3072]{1,0:T(8,128)(2,1)S(1)} %bitcast.414, bf16[1200,768]{1,0:T(8,128)(2,1)S(1)} %copy-done.11), kind=kOutput, calls=%fused_computation.245 | convolution fusion | flops 5662310400 | bytes 18653184 | tf_op jit(solution)/shard_map/dot_general | solution.py:34
  433.0 10.4 %flatten.4 = (bf16[4,4,624,128]{3,2,1,0:T(8,128)(2,1)}, bf16[4,4,624,128]{3,2,1,0:T(8,128)(2,1)}) custom-call(s32[3]{0:T(128)} %pad_add_fusion.pos_ref, f32[768,3072]{1,0:T(8,128)} %fusion.64.refs_0_.refs_1_, f32[3072,768]{1,0:T(8,128)} %fusion.66.refs_1_, f32[24,128]{1,0:T(8,128)} %bitcast.404, f32[26,128]{1,0:T(8,128)} %pad_bitcast_fusion.refs_3_), custom_call_target="tpu_custom_call" | custom-call | bytes 15335424 | tf_op jit(solution)/shard_map/flatten/pallas_call | solution.py:405
  444.0 11.1 %flatten.5 = (bf16[4,4,624,128]{3,2,1,0:T(8,128)(2,1)}, bf16[4,4,624,128]{3,2,1,0:T(8,128)(2,1)}) custom-call(s32[3]{0:T(128)} %pad_add_fusion.pos_ref, f32[768,768]{1,0:T(8,128)} %fusion.58.refs_0_.refs_2_, f32[768,3072]{1,0:T(8,128)} %fusion.64.refs_0_.refs_1_, f32[18,128]{1,0:T(8,128)} %pad_maximum_fusion.22.refs_2_), custom_call_target="tpu_custom_call" | custom-call | bytes 15335424 | tf_op jit(solution)/shard_map/flatten/pallas_call | solution.py:405
  455.7 31.5 %attend_back.2 = bf16[6,200,2304]{2,1,0:T(8,128)(2,1)} custom-call(bf16[6,200,2304]{2,1,0:T(8,128)(2,1)} %bitcast.345, bf16[6,200,2304]{2,1,0:T(8,128)(2,1)} %bitcast.346, bf16[6,200,2304]{2,1,0:T(8,128)(2,1)} %bitcast.347, f32[6,200,1]{2,1,0:T(8,128)} %reshape.518.m_ref, bf16[6,200,768]{2,1,0:T(8,128)(2,1)} %bitcast.386), custom_call_target="tpu_custom_call" | custom-call | flops 3686400000 | bytes 12902400 | tf_op jit(solution)/shard_map/attend_back/pallas_call | solution.py:149
  487.2 9.3 %fusion.24 = (f32[768]{0:T(1024)S(1)}, f32[1200]{0:T(1024)S(1)}, f32[1200]{0:T(1024)S(1)}, f32[768]{0:T(1024)S(1)}, f32[1200,768]{1,0:T(8,128)S(1)}) fusion(bf16[1200,768]{1,0:T(8,128)(2,1)S(1)} %reshape.471, f32[1200]{0:T(1024)S(1)} %add_rsqrt_fusion.2, f32[1200]{0:T(1024)S(1)} %broadcast_multiply_fusion.9, f32[768]{0:T(1024)S(1)} %get-tuple-element.414, ...), kind=kOutput, calls=%fused_computation.48 | convolution fusion | flops 4255944704 | bytes 14626560 | tf_op jit(solution)/shard_map/dot_general | solution.py:525
  505.5 10.1 %fusion.27 = bf16[1200,768]{1,0:T(8,128)(2,1)S(1)} fusion(f32[1200,768]{1,0:T(8,128)} %copy-done.1, bf16[1200,3072]{1,0:T(8,128)(2,1)} %get-tuple-element.483, bf16[3072,768]{1,0:T(8,128)(2,1)} %unflatten.13, f32[768]{0:T(1024)S(1)} %fusion.42), kind=kOutput, calls=%fused_computation.63 | convolution fusion | flops 5665075200 | bytes 17624064 | tf_op jit(solution)/shard_map/dot_general | solution.py:38
  522.3 9.8 %fusion.60.refs_1_ = f32[768,2304]{1,0:T(8,128)} fusion(bf16[1200,2304]{1,0:T(8,128)(2,1)} %bitcast.362, bf16[1200,768]{1,0:T(8,128)(2,1)S(1)} %reshape.471, f32[768]{0:T(1024)S(1)} %copy-done.75, f32[768]{0:T(1024)S(1)} %get-tuple-element.414, f32[1200]{0:T(1024)S(1)} %add_rsqrt_fusion.2, f32[1200]{0:T(1024)S(1)} %broadcast_multiply_fusion.9), kind=kOutput, calls=%fused_computation.241 | convolution fusion | flops 4252262400 | bytes 14466432 | tf_op jit(solution)/shard_map/dot_general | solution.py:34
  532.1 17.0 %all-to-all-done.4 = bf16[3,2,200,768]{3,1,0,2:T(2,128)(2,1)} async-done(((bf16[3,2,200,768]{3,1,0,2:T(2,128)(2,1)}), bf16[3,2,200,768]{3,1,0,2:T(2,128)(2,1)}, u32[]{:S(2)}, u32[]{:S(2)}) %all-to-all-start.4) | async-done | bytes 1843232 | tf_op jit(solution)/shard_map/all_to_all | solution.py:595
  585.4 11.4 %flatten.6 = (bf16[4,4,624,128]{3,2,1,0:T(8,128)(2,1)}, bf16[4,4,624,128]{3,2,1,0:T(8,128)(2,1)}) custom-call(s32[3]{0:T(128)} %pad_add_fusion.pos_ref, f32[768,768]{1,0:T(8,128)} %fusion.67.refs_0_.refs_2_, f32[768,2304]{1,0:T(8,128)} %fusion.60.refs_1_, f32[768,768]{1,0:T(8,128)} %fusion.58.refs_0_.refs_2_, f32[18,128]{1,0:T(8,128)} %pad_maximum_fusion.23.refs_3_, ...), custom_call_target="tpu_custom_call" | custom-call | bytes 15335424 | tf_op jit(solution)/shard_map/flatten/pallas_call | solution.py:405
  610.3 31.5 %attend_back.3 = bf16[6,200,2304]{2,1,0:T(8,128)(2,1)} custom-call(bf16[6,200,2304]{2,1,0:T(8,128)(2,1)} %bitcast.339, bf16[6,200,2304]{2,1,0:T(8,128)(2,1)} %bitcast.340, bf16[6,200,2304]{2,1,0:T(8,128)(2,1)} %bitcast.341, f32[1,200,200]{2,1,0:T(8,128)} %compare_convert_fusion.m_ref, bf16[6,200,768]{2,1,0:T(8,128)(2,1)} %bitcast.383), custom_call_target="tpu_custom_call" | custom-call | flops 3686400000 | bytes 12902400 | tf_op jit(solution)/shard_map/attend_back/pallas_call | solution.py:149
  655.6 7.4 fusion.63.refs_0_
  679.5 8.2 %collective-permute-done.62 = bf16[624,128]{1,0:T(8,128)(2,1)S(1)} collective-permute-done((bf16[624,128]{1,0:T(8,128)(2,1)S(1)}, bf16[624,128]{1,0:T(8,128)(2,1)S(1)}, u32[]{:S(2)}, u32[]{:S(2)}) %collective-permute-start.62) | collective-permute-done | bytes 159776 | tf_op jit(solution)/shard_map/ppermute | solution.py:169
  688.5 11.8 %flatten.7 = (bf16[4,4,624,128]{3,2,1,0:T(8,128)(2,1)}, bf16[4,4,624,128]{3,2,1,0:T(8,128)(2,1)}) custom-call(s32[3]{0:T(128)} %pad_add_fusion.pos_ref, f32[768,2304]{1,0:T(8,128)} %fusion.63.refs_0_, f32[768,768]{1,0:T(8,128)} %fusion.68.refs_1_, f32[768,768]{1,0:T(8,128)} %fusion.67.refs_0_.refs_2_, f32[12,128]{1,0:T(8,128)} %pad_maximum_fusion.25.refs_3_, ...), custom_call_target="tpu_custom_call" | custom-call | bytes 15335424 | tf_op jit(solution)/shard_map/flatten/pallas_call | solution.py:405
  715.8 13.0 %collective-permute-done.66 = bf16[4,624,128]{2,1,0:T(8,128)(2,1)S(1)} collective-permute-done((bf16[4,624,128]{2,1,0:T(8,128)(2,1)S(1)}, bf16[4,624,128]{2,1,0:T(8,128)(2,1)S(1)}, u32[]{:S(2)}, u32[]{:S(2)}) %collective-permute-start.66) | collective-permute-done | bytes 639008 | tf_op jit(solution)/shard_map/ppermute | solution.py:169
  741.7 8.8 %collective-permute-done.70 = bf16[624,128]{1,0:T(8,128)(2,1)S(1)} collective-permute-done((bf16[624,128]{1,0:T(8,128)(2,1)S(1)}, bf16[624,128]{1,0:T(8,128)(2,1)S(1)}, u32[]{:S(2)}, u32[]{:S(2)}) %collective-permute-start.70) | collective-permute-done | bytes 159776 | tf_op jit(solution)/shard_map/ppermute | solution.py:169
  753.4 9.3 %collective-permute-done.74 = bf16[4,624,128]{2,1,0:T(8,128)(2,1)S(1)} collective-permute-done((bf16[4,624,128]{2,1,0:T(8,128)(2,1)S(1)}, bf16[4,624,128]{2,1,0:T(8,128)(2,1)S(1)}, u32[]{:S(2)}, u32[]{:S(2)}) %collective-permute-start.74) | collective-permute-done | bytes 639008 | tf_op jit(solution)/shard_map/ppermute | solution.py:169
  773.3 8.2 %collective-permute-done.77 = bf16[624,128]{1,0:T(8,128)(2,1)S(1)} collective-permute-done((bf16[624,128]{1,0:T(8,128)(2,1)S(1)}, bf16[624,128]{1,0:T(8,128)(2,1)S(1)}, u32[]{:S(2)}, u32[]{:S(2)}) %collective-permute-start.77) | collective-permute-done | bytes 159776 | tf_op jit(solution)/shard_map/ppermute | solution.py:169
  (521 shorter events, 403.9 us)
Async XLA Ops:
  95.8 44.5 %collective-permute-start.27 = (bf16[4,624,128]{2,1,0:T(8,128)(2,1)}, bf16[4,624,128]{2,1,0:T(8,128)(2,1)}, u32[]{:S(2)}, u32[]{:S(2)}) collective-permute-start(bf16[4,624,128]{2,1,0:T(8,128)(2,1)} %pad_maximum_fusion.8.refs_0_), channel_id=1, source_target_pairs={{0,8},{1,9},{2,10},{3,11},{4,12},{5,13},{6,14},{7,15},{8,0},{9,1},... | collective-permute-start | bytes 1916936 | tf_op jit(solution)/shard_map/ppermute | solution.py:169
  97.3 43.0 %collective-permute-start.28 = (bf16[4,624,128]{2,1,0:T(8,128)(2,1)}, bf16[4,624,128]{2,1,0:T(8,128)(2,1)}, u32[]{:S(2)}, u32[]{:S(2)}) collective-permute-start(bf16[4,624,128]{2,1,0:T(8,128)(2,1)} %pad_maximum_fusion.8.refs_0_), channel_id=1, source_target_pairs={{0,16},{1,17},{2,18},{3,19},{4,20},{5,21},{6,22},{7,23},{8,24},{9,... | collective-permute-start | bytes 1916936 | tf_op jit(solution)/shard_map/ppermute | solution.py:169
  99.6 38.7 %collective-permute-start.26 = (bf16[2,624,128]{2,1,0:T(8,128)(2,1)}, bf16[2,624,128]{2,1,0:T(8,128)(2,1)}, u32[]{:S(2)}, u32[]{:S(2)}) collective-permute-start(bf16[2,624,128]{2,1,0:T(8,128)(2,1)} %slice.293), channel_id=1, source_target_pairs={{0,8},{1,9},{2,10},{3,11},{4,12},{5,13},{6,14},{7,15},{8,0},{9,1},... | collective-permute-start | bytes 958472 | tf_op jit(solution)/shard_map/ppermute | solution.py:169
  101.9 36.4 %collective-permute-start.25 = (bf16[2,624,128]{2,1,0:T(8,128)(2,1)}, bf16[2,624,128]{2,1,0:T(8,128)(2,1)}, u32[]{:S(2)}, u32[]{:S(2)}) collective-permute-start(bf16[2,624,128]{2,1,0:T(8,128)(2,1)} %slice.292), channel_id=1, source_target_pairs={{0,16},{1,17},{2,18},{3,19},{4,20},{5,21},{6,22},{7,23},{8,24},{9,... | collective-permute-start | bytes 958472 | tf_op jit(solution)/shard_map/ppermute | solution.py:169
  113.5 86.0 %all-to-all-start = ((bf16[3,16,25,768]{3,2,0,1:T(8,128)(2,1)}), bf16[3,16,25,768]{3,2,0,1:T(8,128)(2,1)}, u32[]{:S(2)}, u32[]{:S(2)}) async-start(bf16[3,16,25,768]{3,2,0,1:T(8,128)(2,1)} %copy.55), calls=%async_computation | async-start | bytes 4718592 | tf_op jit(solution)/shard_map/all_to_all | solution.py:590
  150.8 19.4 %collective-permute-start.36 = (bf16[4,624,128]{2,1,0:T(8,128)(2,1)S(1)}, bf16[4,624,128]{2,1,0:T(8,128)(2,1)}, u32[]{:S(2)}, u32[]{:S(2)}) collective-permute-start(bf16[4,624,128]{2,1,0:T(8,128)(2,1)S(1)} %pad_maximum_fusion.10.refs_0_), channel_id=1, source_target_pairs={{0,16},{1,17},{2,18},{3,19},{4,20},{5,21},{6,22},{7,23},{8,24},{9,... | collective-permute-start | bytes 1916936 | tf_op jit(solution)/shard_map/ppermute | solution.py:169
  171.7 34.6 %collective-permute-start.37 = (bf16[4,624,128]{2,1,0:T(8,128)(2,1)}, bf16[4,624,128]{2,1,0:T(8,128)(2,1)}, u32[]{:S(2)}, u32[]{:S(2)}) collective-permute-start(bf16[4,624,128]{2,1,0:T(8,128)(2,1)} %pad_maximum_fusion.8.refs_0_), channel_id=1, source_target_pairs={{0,1},{1,0},{2,3},{3,2},{4,5},{5,4},{6,7},{7,6},{8,9},{9,8},{10,11... | collective-permute-start | bytes 1916936 | tf_op jit(solution)/shard_map/ppermute | solution.py:169
  171.7 34.6 %collective-permute-start.38 = (bf16[4,624,128]{2,1,0:T(8,128)(2,1)}, bf16[4,624,128]{2,1,0:T(8,128)(2,1)}, u32[]{:S(2)}, u32[]{:S(2)}) collective-permute-start(bf16[4,624,128]{2,1,0:T(8,128)(2,1)} %collective-permute-done.27.refs_1_), channel_id=1, source_target_pairs={{0,1},{1,0},{2,3},{3,2},{4,5},{5,4},{6,7},{7,6},{8,9},{9,8},{10,11... | collective-permute-start | bytes 1916936 | tf_op jit(solution)/shard_map/ppermute | solution.py:169
  172.3 34.1 %collective-permute-start.39 = (bf16[4,624,128]{2,1,0:T(8,128)(2,1)}, bf16[4,624,128]{2,1,0:T(8,128)(2,1)}, u32[]{:S(2)}, u32[]{:S(2)}) collective-permute-start(bf16[4,624,128]{2,1,0:T(8,128)(2,1)} %collective-permute-done.28.refs_2_), channel_id=1, source_target_pairs={{0,1},{1,0},{2,3},{3,2},{4,5},{5,4},{6,7},{7,6},{8,9},{9,8},{10,11... | collective-permute-start | bytes 1916936 | tf_op jit(solution)/shard_map/ppermute | solution.py:169
  172.3 34.1 %collective-permute-start.40 = (bf16[4,624,128]{2,1,0:T(8,128)(2,1)S(1)}, bf16[4,624,128]{2,1,0:T(8,128)(2,1)}, u32[]{:S(2)}, u32[]{:S(2)}) collective-permute-start(bf16[4,624,128]{2,1,0:T(8,128)(2,1)S(1)} %pad_maximum_fusion.9.refs_3_), channel_id=1, source_target_pairs={{0,1},{1,0},{2,3},{3,2},{4,5},{5,4},{6,7},{7,6},{8,9},{9,8},{10,11... | collective-permute-start | bytes 1916936 | tf_op jit(solution)/shard_map/ppermute | solution.py:169
  179.6 19.0 %collective-permute-start.41 = (bf16[2,624,128]{2,1,0:T(8,128)(2,1)S(1)}, bf16[2,624,128]{2,1,0:T(8,128)(2,1)S(1)}, u32[]{:S(2)}, u32[]{:S(2)}) collective-permute-start(bf16[2,624,128]{2,1,0:T(8,128)(2,1)S(1)} %slice.300), channel_id=1, source_target_pairs={{0,16},{1,17},{2,18},{3,19},{4,20},{5,21},{6,22},{7,23},{8,24},{9,... | collective-permute-start | bytes 958472 | tf_op jit(solution)/shard_map/ppermute | solution.py:169
  215.1 24.9 %collective-permute-start.43 = (bf16[4,624,128]{2,1,0:T(8,128)(2,1)S(1)}, bf16[4,624,128]{2,1,0:T(8,128)(2,1)}, u32[]{:S(2)}, u32[]{:S(2)}) collective-permute-start(bf16[4,624,128]{2,1,0:T(8,128)(2,1)S(1)} %copy-done.22), channel_id=1, source_target_pairs={{0,1},{1,0},{2,3},{3,2},{4,5},{5,4},{6,7},{7,6},{8,9},{9,8},{10,11... | collective-permute-start | bytes 1916936 | tf_op jit(solution)/shard_map/ppermute | solution.py:169
  215.1 24.9 %collective-permute-start.44 = (bf16[4,624,128]{2,1,0:T(8,128)(2,1)S(1)}, bf16[4,624,128]{2,1,0:T(8,128)(2,1)}, u32[]{:S(2)}, u32[]{:S(2)}) collective-permute-start(bf16[4,624,128]{2,1,0:T(8,128)(2,1)S(1)} %copy-done.33), channel_id=1, source_target_pairs={{0,1},{1,0},{2,3},{3,2},{4,5},{5,4},{6,7},{7,6},{8,9},{9,8},{10,11... | collective-permute-start | bytes 1916936 | tf_op jit(solution)/shard_map/ppermute | solution.py:169
  215.6 24.4 %collective-permute-start.45 = (bf16[4,624,128]{2,1,0:T(8,128)(2,1)}, bf16[4,624,128]{2,1,0:T(8,128)(2,1)}, u32[]{:S(2)}, u32[]{:S(2)}) collective-permute-start(bf16[4,624,128]{2,1,0:T(8,128)(2,1)} %collective-permute-done.36.refs_2_), channel_id=1, source_target_pairs={{0,1},{1,0},{2,3},{3,2},{4,5},{5,4},{6,7},{7,6},{8,9},{9,8},{10,11... | collective-permute-start | bytes 1916936 | tf_op jit(solution)/shard_map/ppermute | solution.py:169
  215.7 24.3 %collective-permute-start.46 = (bf16[4,624,128]{2,1,0:T(8,128)(2,1)S(1)}, bf16[4,624,128]{2,1,0:T(8,128)(2,1)}, u32[]{:S(2)}, u32[]{:S(2)}) collective-permute-start(bf16[4,624,128]{2,1,0:T(8,128)(2,1)S(1)} %copy-done.24), channel_id=1, source_target_pairs={{0,1},{1,0},{2,3},{3,2},{4,5},{5,4},{6,7},{7,6},{8,9},{9,8},{10,11... | collective-permute-start | bytes 1916936 | tf_op jit(solution)/shard_map/ppermute | solution.py:169
  274.9 60.0 %all-to-all-start.1 = ((bf16[3,16,25,768]{3,2,0,1:T(8,128)(2,1)}), bf16[3,16,25,768]{3,2,0,1:T(8,128)(2,1)S(1)}, u32[]{:S(2)}, u32[]{:S(2)}) async-start(bf16[3,16,25,768]{3,2,0,1:T(8,128)(2,1)} %copy.58), calls=%async_computation.1 | async-start | bytes 4718592 | tf_op jit(solution)/shard_map/all_to_all | solution.py:590
  443.4 116.4 %collective-permute-start.47 = (bf16[4,4,624,128]{3,2,1,0:T(8,128)(2,1)}, bf16[4,4,624,128]{3,2,1,0:T(8,128)(2,1)}, u32[]{:S(2)}, u32[]{:S(2)}) collective-permute-start(bf16[4,4,624,128]{3,2,1,0:T(8,128)(2,1)} %get-tuple-element.324), channel_id=1, source_target_pairs={{0,1},{1,0},{2,3},{3,2},{4,5},{5,4},{6,7},{7,6},{8,9},{9,8},{10,11... | collective-permute-start | bytes 7667720 | tf_op jit(solution)/shard_map/ppermute | solution.py:169
  455.1 104.7 %collective-permute-start.48 = (bf16[4,4,624,128]{3,2,1,0:T(8,128)(2,1)}, bf16[4,4,624,128]{3,2,1,0:T(8,128)(2,1)}, u32[]{:S(2)}, u32[]{:S(2)}) collective-permute-start(bf16[4,4,624,128]{3,2,1,0:T(8,128)(2,1)} %get-tuple-element.326), channel_id=1, source_target_pairs={{0,1},{1,0},{2,3},{3,2},{4,5},{5,4},{6,7},{7,6},{8,9},{9,8},{10,11... | collective-permute-start | bytes 7667720 | tf_op jit(solution)/shard_map/ppermute | solution.py:169
  501.2 47.9 %all-to-all-start.4 = ((bf16[3,2,200,768]{3,1,0,2:T(2,128)(2,1)}), bf16[3,2,200,768]{3,1,0,2:T(2,128)(2,1)}, u32[]{:S(2)}, u32[]{:S(2)}) async-start(bf16[3,2,200,768]{3,1,0,2:T(2,128)(2,1)} %copy.68), calls=%async_computation.4 | async-start | bytes 3686400 | tf_op jit(solution)/shard_map/all_to_all | solution.py:595
  549.1 151.1 %all-to-all-start.3 = ((bf16[3,2,200,768]{3,1,0,2:T(2,128)(2,1)}), bf16[3,2,200,768]{3,1,0,2:T(2,128)(2,1)}, u32[]{:S(2)}, u32[]{:S(2)}) async-start(bf16[3,2,200,768]{3,1,0,2:T(2,128)(2,1)} %copy.63), calls=%async_computation.3 | async-start | bytes 3686400 | tf_op jit(solution)/shard_map/all_to_all | solution.py:595
  596.8 45.1 %collective-permute-start.57 = (bf16[4,4,624,128]{3,2,1,0:T(8,128)(2,1)}, bf16[4,4,624,128]{3,2,1,0:T(8,128)(2,1)}, u32[]{:S(2)}, u32[]{:S(2)}) collective-permute-start(bf16[4,4,624,128]{3,2,1,0:T(8,128)(2,1)} %get-tuple-element.341), channel_id=1, source_target_pairs={{0,1},{1,0},{2,3},{3,2},{4,5},{5,4},{6,7},{7,6},{8,9},{9,8},{10,11... | collective-permute-start | bytes 7667720 | tf_op jit(solution)/shard_map/ppermute | solution.py:169
  603.3 38.5 %collective-permute-start.53 = (bf16[4,624,128]{2,1,0:T(8,128)(2,1)}, bf16[4,624,128]{2,1,0:T(8,128)(2,1)}, u32[]{:S(2)}, u32[]{:S(2)}) collective-permute-start(bf16[4,624,128]{2,1,0:T(8,128)(2,1)} %pad_maximum_fusion.12), channel_id=1, source_target_pairs={{0,8},{1,9},{2,10},{3,11},{4,12},{5,13},{6,14},{7,15},{8,0},{9,1},... | collective-permute-start | bytes 1916936 | tf_op jit(solution)/shard_map/ppermute | solution.py:169
  605.6 36.2 %collective-permute-start.54 = (bf16[4,624,128]{2,1,0:T(8,128)(2,1)}, bf16[4,624,128]{2,1,0:T(8,128)(2,1)}, u32[]{:S(2)}, u32[]{:S(2)}) collective-permute-start(bf16[4,624,128]{2,1,0:T(8,128)(2,1)} %pad_maximum_fusion.13), channel_id=1, source_target_pairs={{0,16},{1,17},{2,18},{3,19},{4,20},{5,21},{6,22},{7,23},{8,24},{9,... | collective-permute-start | bytes 1916936 | tf_op jit(solution)/shard_map/ppermute | solution.py:169
  608.4 33.4 %collective-permute-start.55 = (bf16[4,624,128]{2,1,0:T(8,128)(2,1)}, bf16[4,624,128]{2,1,0:T(8,128)(2,1)}, u32[]{:S(2)}, u32[]{:S(2)}) collective-permute-start(bf16[4,624,128]{2,1,0:T(8,128)(2,1)} %pad_maximum_fusion.14), channel_id=1, source_target_pairs={{0,8},{1,9},{2,10},{3,11},{4,12},{5,13},{6,14},{7,15},{8,0},{9,1},... | collective-permute-start | bytes 1916936 | tf_op jit(solution)/shard_map/ppermute | solution.py:169
  609.7 32.1 %collective-permute-start.56 = (bf16[4,624,128]{2,1,0:T(8,128)(2,1)}, bf16[4,624,128]{2,1,0:T(8,128)(2,1)}, u32[]{:S(2)}, u32[]{:S(2)}) collective-permute-start(bf16[4,624,128]{2,1,0:T(8,128)(2,1)} %pad_maximum_fusion.15), channel_id=1, source_target_pairs={{0,16},{1,17},{2,18},{3,19},{4,20},{5,21},{6,22},{7,23},{8,24},{9,... | collective-permute-start | bytes 1916936 | tf_op jit(solution)/shard_map/ppermute | solution.py:169
  643.6 30.3 %collective-permute-start.58 = (bf16[624,128]{1,0:T(8,128)(2,1)S(1)}, bf16[624,128]{1,0:T(8,128)(2,1)S(1)}, u32[]{:S(2)}, u32[]{:S(2)}) collective-permute-start(bf16[624,128]{1,0:T(8,128)(2,1)S(1)} %get-tuple-element.467), channel_id=1, source_target_pairs={{0,2},{1,3},{2,0},{3,1},{4,6},{5,7},{6,4},{7,5},{8,10},{9,11},{10,... | collective-permute-start | bytes 479240 | tf_op jit(solution)/shard_map/ppermute | solution.py:169
  645.0 29.1 %collective-permute-start.59 = (bf16[624,128]{1,0:T(8,128)(2,1)S(1)}, bf16[624,128]{1,0:T(8,128)(2,1)S(1)}, u32[]{:S(2)}, u32[]{:S(2)}) collective-permute-start(bf16[624,128]{1,0:T(8,128)(2,1)S(1)} %get-tuple-element.466), channel_id=1, source_target_pairs={{0,4},{1,5},{2,6},{3,7},{4,0},{5,1},{6,2},{7,3},{8,12},{9,13},{10,... | collective-permute-start | bytes 479240 | tf_op jit(solution)/shard_map/ppermute | solution.py:169
  647.5 29.8 %collective-permute-start.60 = (bf16[624,128]{1,0:T(8,128)(2,1)S(1)}, bf16[624,128]{1,0:T(8,128)(2,1)S(1)}, u32[]{:S(2)}, u32[]{:S(2)}) collective-permute-start(bf16[624,128]{1,0:T(8,128)(2,1)S(1)} %get-tuple-element.465), channel_id=1, source_target_pairs={{0,6},{1,7},{2,4},{3,5},{4,2},{5,3},{6,0},{7,1},{8,14},{9,15},{10,... | collective-permute-start | bytes 479240 | tf_op jit(solution)/shard_map/ppermute | solution.py:169
  652.4 35.3 %collective-permute-start.64 = (bf16[2,624,128]{2,1,0:T(8,128)(2,1)S(1)}, bf16[2,624,128]{2,1,0:T(8,128)(2,1)S(1)}, u32[]{:S(2)}, u32[]{:S(2)}) collective-permute-start(bf16[2,624,128]{2,1,0:T(8,128)(2,1)S(1)} %get-tuple-element.435), channel_id=1, source_target_pairs={{0,8},{1,9},{2,10},{3,11},{4,12},{5,13},{6,14},{7,15},{8,0},{9,1},... | collective-permute-start | bytes 958472 | tf_op jit(solution)/shard_map/ppermute | solution.py:169
  653.9 33.9 %collective-permute-start.65 = (bf16[2,624,128]{2,1,0:T(8,128)(2,1)S(1)}, bf16[2,624,128]{2,1,0:T(8,128)(2,1)S(1)}, u32[]{:S(2)}, u32[]{:S(2)}) collective-permute-start(bf16[2,624,128]{2,1,0:T(8,128)(2,1)S(1)} %get-tuple-element.434), channel_id=1, source_target_pairs={{0,16},{1,17},{2,18},{3,19},{4,20},{5,21},{6,22},{7,23},{8,24},{9,... | collective-permute-start | bytes 958472 | tf_op jit(solution)/shard_map/ppermute | solution.py:169
  700.3 28.8 %collective-permute-start.68 = (bf16[4,4,624,128]{3,2,1,0:T(8,128)(2,1)}, bf16[4,4,624,128]{3,2,1,0:T(8,128)(2,1)}, u32[]{:S(2)}, u32[]{:S(2)}) collective-permute-start(bf16[4,4,624,128]{3,2,1,0:T(8,128)(2,1)} %get-tuple-element.357), channel_id=1, source_target_pairs={{0,1},{1,0},{2,3},{3,2},{4,5},{5,4},{6,7},{7,6},{8,9},{9,8},{10,11... | collective-permute-start | bytes 7667720 | tf_op jit(solution)/shard_map/ppermute | solution.py:169
  731.5 18.9 %collective-permute-start.72 = (bf16[2,624,128]{2,1,0:T(8,128)(2,1)S(1)}, bf16[2,624,128]{2,1,0:T(8,128)(2,1)S(1)}, u32[]{:S(2)}, u32[]{:S(2)}) collective-permute-start(bf16[2,624,128]{2,1,0:T(8,128)(2,1)S(1)} %get-tuple-element.429), channel_id=1, source_target_pairs={{0,8},{1,9},{2,10},{3,11},{4,12},{5,13},{6,14},{7,15},{8,0},{9,1},... | collective-permute-start | bytes 958472 | tf_op jit(solution)/shard_map/ppermute | solution.py:169
  (145 other events, 1662.2 us)

commit v3 on v2

--- a/solution.py
+++ b/solution.py
@@ -7,7 +7,7 @@
 from jax.experimental.pallas import tpu as pltpu
 from jax.sharding import PartitionSpec as P
 
-H = 12
+
 FF = 3072
 EPS = 1e-06
 MASKED = -1000000000.0
@@ -269,6 +269,10 @@
         self.stage_number = 0
 
     def stage(self):
+        self.exchange()
+        self.stage_number += 1
+
+    def exchange(self):
         for b, step in self.SCHEDULE[self.stage_number]:
             now = self.state[b]
             if step == 0:
@@ -282,7 +286,6 @@
             else:
                 now = now + [send(part, 0, 1) for part in now]
             self.state[b] = now
-        self.stage_number += 1
 
     def sync(self, *values):
         self.state, values = tie(self.state, values)
@@ -295,22 +298,45 @@
 CHUNK = 1152
 
 
-def unflatten(src, base, off, rows, width, plan):
+def unflatten(blocks, a, off, rows, width, plan):
     lanes = width // LANES
     step_rows = CHUNK // lanes
-    size = src.shape[0]
+    size = plan.block
     window = round_up(CHUNK + plan.gap + 16, 16)
+    two = plan.padded(off + rows * lanes - 1) >= (a + 1) * size
 
     def where_from(i):
         first = off + CHUNK * i
-        at = first + plan.gap * (first // plan.rows) - base
-        return first, at, jnp.minimum(at // 16 * 16, size - window)
-
-    def kernel(in_ref, out_ref, wide):
-        first, at, start = where_from(pl.program_id(0))
+        at = first + plan.gap * (first // plan.rows) - a * size
+        start = jnp.minimum(at // 16 * 16, size - window)
+        start_next = jnp.clip((at - size) // 16 * 16, 0, size - window)
+        return first, at, start, start_next
+
+    def kernel(*refs):
+        in_ref, out_ref, wide = refs[0], refs[-2], refs[-1]
+        first, at, start, start_next = where_from(pl.program_id(0))
+        left = plan.rows - first % plan.rows
         delta = at - start
-        left = plan.rows - first % plan.rows
-        wide[...] = in_ref[...].astype(F32)
+        over = delta + plan.gap
+        if two:
+            delta = jnp.where(at < size, delta, at - size - start_next)
+            crossing = (at < size) & (at + left + plan.gap >= size)
+            over = jnp.where(crossing, window - left, delta + plan.gap)
+
+            @pl.when(at < size)
+            def _():
+                wide[:window] = in_ref[...].astype(F32)
+
+            @pl.when(at >= size)
+            def _():
+                wide[:window] = refs[1][...].astype(F32)
+
+            @pl.when(crossing)
+            def _():
+                wide[window:] = refs[1][...].astype(F32)
+
+        else:
+            wide[:window] = in_ref[...].astype(F32)
 
         @pl.when(left >= CHUNK)
         def _():
@@ -323,28 +349,27 @@
             row = lax.broadcasted_iota(jnp.int32, (step_rows, LANES), 0) * lanes
             for b in range(lanes):
                 near = wide[pl.ds(delta + b, step_rows, stride=lanes), :]
-                far = wide[pl.ds(delta + b + plan.gap, step_rows, stride=lanes), :]
+                far = wide[pl.ds(over + b, step_rows, stride=lanes), :]
                 got = jnp.where(row + b < left, near, far)
                 out_ref[:, b * LANES : (b + 1) * LANES] = got.astype(BF)
 
+    element = (pl.Element(window), pl.Element(LANES))
+    in_specs = [pl.BlockSpec(element, lambda i: (pl.multiple_of(where_from(i)[2], 16), 0))]
+    if two:
+        in_specs.append(pl.BlockSpec(element, lambda i: (pl.multiple_of(where_from(i)[3], 16), 0)))
     return pl.pallas_call(
         kernel,
         grid=(rows // step_rows,),
-        in_specs=[
-            pl.BlockSpec(
-                (pl.Element(window), pl.Element(LANES)),
-                lambda i: (pl.multiple_of(where_from(i)[2], 16), 0),
-            )
-        ],
+        in_specs=in_specs,
         out_specs=pl.BlockSpec((step_rows, width), lambda i: (i, 0)),
         out_shape=jax.ShapeDtypeStruct((rows, width), BF),
-        scratch_shapes=[pltpu.VMEM((window, LANES), F32)],
-        cost_estimate=pl.CostEstimate(flops=0, bytes_accessed=rows * width * 4, transcendentals=0),
+        scratch_shapes=[pltpu.VMEM((window * (2 if two else 1), LANES), F32)],
+        cost_estimate=pl.CostEstimate(flops=0, bytes_accessed=rows * width * 12, transcendentals=0),
         name="unflatten",
-    )(src)
-
-
-def flatten(pos, b, mats, vecs, plan):
+    )(*blocks[a : a + 2 if two else a + 1])
+
+
+def flatten(pos, b, mats, vecs, plan, core):
     part, span = plan.part, plan.rows
     shapes = []
     for off, mat in mats:
@@ -353,9 +378,7 @@
     pad = round_up(max([w * c for _, _, c, w in shapes] + [v.shape[0] for _, v in vecs]), 8) + 8
 
     def first_row(t, pos_ref):
-        z = pos_ref[1] ^ (t % 4)
-        core = jnp.where(t < 4, 1 - pos_ref[2], pos_ref[2])
-        return (8 * b + z * 2 + core) * span
+        return (8 * b + (pos_ref[1] ^ t) * 2 + (pos_ref[2] ^ core)) * span
 
     def start_row(p0, off, rows, lanes, w):
         return jnp.minimum(jnp.maximum(p0 - off, 0) // lanes // 8 * 8, rows - w)
@@ -363,9 +386,8 @@
     def kernel(pos_ref, *refs):
         ins = refs[: len(mats)]
         vins = refs[len(mats) : len(mats) + len(vecs)]
-        theirs, ours, wide = refs[len(mats) + len(vecs) :]
-        t = pl.program_id(0)
-        p0 = first_row(t, pos_ref)
+        out, wide = refs[len(mats) + len(vecs) :]
+        p0 = first_row(pl.program_id(0), pos_ref)
         for (off, rows, lanes, w), ref in zip(shapes, ins):
 
             @pl.when((p0 + span > off) & (p0 < off + rows * lanes))
@@ -383,13 +405,9 @@
                 for r in range(n):
                     wide[pl.ds(at + r, 1), :] = ref[r : r + 1, :]
 
-        for out, mine in ((theirs, t < 4), (ours, t >= 4)):
-
-            @pl.when(mine)
-            def _():
-                for k in range(4):
-                    at = pl.multiple_of(pad + (pos_ref[0] ^ k) * part, 8)
-                    out[k, 0] = wide[pl.ds(at, part), :].astype(BF)
+        for k in range(4):
+            at = pl.multiple_of(pad + (pos_ref[0] ^ k) * part, 8)
+            out[k, 0] = wide[pl.ds(at, part), :].astype(BF)
 
     in_specs = [
         pl.BlockSpec(
@@ -406,26 +424,39 @@
         kernel,
         grid_spec=pltpu.PrefetchScalarGridSpec(
             num_scalar_prefetch=1,
-            grid=(8,),
+            grid=(4,),
             in_specs=in_specs,
-            out_specs=[
-                pl.BlockSpec((4, 1, part, LANES), lambda t, p: (0, jnp.minimum(t, 3), 0, 0)),
-                pl.BlockSpec((4, 1, part, LANES), lambda t, p: (0, jnp.maximum(t - 4, 0), 0, 0)),
-            ],
+            out_specs=pl.BlockSpec((4, 1, part, LANES), lambda t, p: (0, t, 0, 0)),
             scratch_shapes=[pltpu.VMEM((2 * pad + 4 * part, LANES), F32)],
         ),
-        out_shape=[shape, shape],
+        out_shape=shape,
         cost_estimate=pl.CostEstimate(flops=0, bytes_accessed=plan.block * LANES * 6, transcendentals=0),
         name="flatten",
     )(pos, *[m for _, m in mats], *[v for _, v in vecs])
 
 
+class SumAll:
+    def __init__(self, value):
+        self.state = (value,)
+        self.stage_number = 0
+
+    def stage(self):
+        total = sum(self.state)
+        hops = ([(0, 1)], [(1, 0), (2, 0), (3, 0)], [(0, 2), (0, 4), (0, 6)], [])[self.stage_number]
+        self.state = (total,) + tuple(send(total, *hop) for hop in hops)
+        self.stage_number += 1
+
+
 class Reduce:
-    def __init__(self, theirs, ours):
-        self.state = (theirs, ours)
+    def __init__(self, half):
+        self.state = (half(1), half(0))
         self.stage_number = 0
 
     def stage(self):
+        self.exchange()
+        self.stage_number += 1
+
+    def exchange(self):
         s, now = self.stage_number, self.state
         wide = lambda *parts: sum(p.astype(F32) for p in parts)
         if s == 0:
@@ -444,7 +475,6 @@
             self.state = (line[0],) + tuple(send(line[k], 0, 2 * k) for k in range(1, 4))
         else:
             self.state = wide(*now)
-        self.stage_number = s + 1
 
 
 def advance(reduces, *values):
@@ -495,14 +525,7 @@
 
 
 def matrix_of(blocks, lo, shape, plan):
-    rows, width = shape
-    first = plan.padded(lo)
-    last = plan.padded(lo + rows * (width // LANES) - 1) + 1
-    a, b = first // plan.block, (last - 1) // plan.block
-    if a == b:
-        return unflatten(blocks[a], a * plan.block, lo, rows, width, plan)
-    base = first // 16 * 16
-    return unflatten(cut(blocks, base, round_up(last, 16)), base, lo, rows, width, plan)
+    return unflatten(blocks, plan.padded(lo) // plan.block, lo, *shape, plan)
 
 
 def stats(v):
@@ -539,7 +562,7 @@
     return jnp.concatenate([q_bias, jnp.zeros_like(q_bias), v_bias])
 
 
-def shards(inputs, cotangent, params, clip_counts, slot_live):
+def layer(inputs, cotangent, params, clip_counts, slot_live):
     micro, clips, frames, places, d = inputs.shape
     n_sp = lax.axis_size("sp")
     n_dev = lax.axis_size("dp") * n_sp
@@ -567,13 +590,8 @@
             return made[i]
 
         gather = Gather(params, plan, pos)
-        for _ in range(4):
-            gather.stage()
-            cot_now, live_now = gather.sync(cot_now, live_now)
-        blocks[0] = gather.block(0)
         gather.stage()
-        made[2], made[5] = gather.sync(piece(2), piece(5))
-        gather.stage()
+        inputs_now, cot_now, live_now = gather.sync(inputs_now, cot_now, live_now)
     else:
         flat = lax.all_gather(params, BOTH, axis=0, tiled=True).reshape(-1, LANES)
 
@@ -596,39 +614,54 @@
             value.reshape(micro, seqs // micro, length, d), "sp", split_axis=2, concat_axis=1, tiled=True
         ).reshape(micro, clips, frames, places, d)
 
+    x_low = inputs_now.reshape(tokens, d)
+    masked = (cot_now * live_low).reshape(micro, clips * frames, places, d)
     live_sent = jnp.broadcast_to(live.astype(BF)[:, :, None], (micro, clips, frames, places)).reshape(
         micro, clips * frames, places
     )
+    if fast:
+        gather.stage()
+        x_low, live_sent = gather.sync(x_low, live_sent)
+    x = x_low.astype(F32)
+    hat1, scale1 = stats(x)
     live_frames = lax.all_to_all(live_sent, "sp", split_axis=1, concat_axis=2, tiled=True)
     keep_rows = live_frames.astype(F32).reshape(seqs, 1, length)
     keep_s = keep_rows.reshape(seqs, length, 1)
-    dx3 = to_frames(cot_now * live_low)
 
     span_t = frames * places
     place = jnp.arange(span_t, dtype=jnp.int32) % places
     same = (place[:, None] == place[None]).astype(F32)[None]
 
-    x = inputs_now.reshape(tokens, d).astype(F32)
-    hat1, scale1 = stats(x)
+    if fast:
+        gather.stage()
+        hat1, scale1 = gather.sync(hat1, scale1)
+        gather.stage()
+        blocks[0] = gather.block(0)
+        made[2] = piece(2)
+        made[2], masked = gather.sync(made[2], masked)
+        gather.stage()
+
+    dx3 = to_frames(masked)
     tg = piece(0)
     h1 = (hat1 * tg + piece(1)).astype(BF)
     w_qkv_t = piece(2)
     qkv_t = (dot(h1, w_qkv_t) + bias_row(piece(3), piece(4))).astype(BF)
     qkv_t = qkv_t.reshape(micro * clips, span_t, 3 * d)
-    if fast:
-        (qkv_t,) = gather.sync(qkv_t)
+    o_t = attend(qkv_t, same, d).reshape(tokens, d)
+    if fast:
+        (o_t,) = gather.sync(o_t)
         gather.stage()
-    o_t = attend(qkv_t, same, d).reshape(tokens, d)
-    if fast:
-        o_t, dx3 = gather.sync(o_t, dx3)
-        gather.stage()
-        blocks[1] = gather.block(1)
     w_out_t = piece(5)
     a_t = (dot(o_t, w_out_t) + piece(6)).astype(BF)
+    if fast:
+        (a_t,) = gather.sync(a_t)
+        blocks[1] = gather.block(1)
+        gather.stage()
     w_fc = piece(7)
     x1 = (x + dot(a_t, w_fc) + piece(8)).astype(BF)
     if fast:
-        (x1,) = gather.sync(x1)
+        x1, dx3 = gather.sync(x1, dx3)
+        gather.stage()
     xb = to_frames(x1)
     if fast:
         blocks[2], blocks[3] = gather.block(2), gather.block(3)
@@ -649,7 +682,7 @@
     h3 = (hat3 * mg + piece(17)).astype(BF)
     g, slope = gelu_pair(dot(h3, w_up) + piece(19))
     x3 = (x2 + dot(g, w_down) + piece(21)).astype(BF)
-    out = to_places(x3) * live_low
+    out = to_places(x3)
 
     du = (product_back(dx3, w_down) * slope).astype(BF)
     back3, grad_mg, grad_mb = norm_back(hat3, scale3, mg, product_back(du, w_up))
@@ -684,7 +717,11 @@
                 run.append(grads[i] if i < len(grads) else tail)
         if run:
             vecs.append((run_at, jnp.concatenate(run).reshape(-1, LANES)))
-        return Reduce(*flatten(pos, b, mats, vecs, plan))
+
+        def half(core):
+            return flatten(pos, b, mats, vecs, plan, core)
+
+        return Reduce(half)
 
     if fast:
         r3 = block_of(3)
@@ -709,20 +746,31 @@
         (dqkv_t,) = advance((r3, r2, r1), dqkv_t)
     sums = row_sum(dqkv_t)
     grads[3], grads[4] = sums[:d], sums[2 * d :]
-    back1, grads[0], grads[1] = norm_back(hat1, scale1, tg, product_back(dqkv_t, w_qkv_t))
     grads[5], grads[6] = dot_l(o_t, da_t), row_sum(da_t)
     grads[2] = dot_l(h1, dqkv_t)
-    input_grad = (dx1.astype(F32) + back1).astype(BF).reshape(inputs.shape)
-
-    if fast:
-        (grads[2],) = advance((r3, r2, r1), grads[2])
+    if fast:
+        grads[2], dqkv_t, out = advance((r3, r2, r1), grads[2], dqkv_t, out)
+        grads[0] = grads[1] = jnp.zeros((d,), F32)
         r0 = block_of(0)
         r0.stage()
-        advance((r1, r0))
-        advance((r1, r0))
+    back1, grad_tg, grad_tb = norm_back(hat1, scale1, tg, product_back(dqkv_t, w_qkv_t))
+    if fast:
+        norm_sum = SumAll(jnp.concatenate([grad_tg, grad_tb]).reshape(-1, LANES))
+        norm_sum.stage()
+        back1, out = advance((r1, r0, norm_sum), back1, out)
+        (back1,) = advance((r1, r0, norm_sum), back1)
+    else:
+        grads[0], grads[1] = grad_tg, grad_tb
+    out = out * live_low
+    input_grad = (dx1.astype(F32) + back1).astype(BF).reshape(inputs.shape)
+
+    if fast:
+        advance((r0, norm_sum))
         advance((r0,))
-        advance((r0,))
-        param_grad = return_quarters([r0.state, r1.state, r2.state, r3.state], plan, pos)
+        first = (pos[0] + pos[1] + pos[2] == 0).astype(F32)
+        extra = norm_sum.state[0] * first
+        extra = jnp.pad(extra, ((0, plan.part - extra.shape[0]), (0, 0)))
+        param_grad = return_quarters([r0.state + extra, r1.state, r2.state, r3.state], plan, pos)
     else:
         flat = jnp.concatenate([g.reshape(-1) for g in grads] + [jnp.zeros((full_length - used,), F32)])
         param_grad = lax.psum_scatter(flat, BOTH, scatter_dimension=0, tiled=True)
@@ -732,7 +780,7 @@
 def solution(mesh):
     tokens = P(None, "dp", None, "sp", None)
     return jax.shard_map(
-        shards,
+        layer,
         mesh=mesh,
         in_specs=(tokens, tokens, P(BOTH), P(None, "dp"), P(None, "dp", "sp")),
         out_specs=(tokens, tokens, P(BOTH)),

time: 813 us -> 757 us (0.931)
  waiting for transfers between devices: 178 us -> 104 us
  local copies, waits for them, and re-layouts: 93.7 us -> 79.5 us
  starting transfers between devices: 108 us -> 120 us
  matrix products: 146 us -> 156 us
  Pallas kernels: 212 us -> 221 us
    ppermute x82 -> x89, waiting for transfers between devices: 130 us -> 96.7 us  [send(): return lax.ppermute(value, BOTH, flip_perm(dp_bits, sp_bits))]
    all_to_all x2, waiting for transfers between devices: 29.2 us -> 1.92 us  [to_frames(): lax.all_to_all(value.reshape(micro, clips * frames, places, d), 'sp', spl...]
    all_to_all x2, waiting for transfers between devices: 17 us -> 4.99 us  [to_places(): lax.all_to_all(value.reshape(micro, seqs // micro, length, d), 'sp', spli...]
    slice x16 -> x10, local copies, waits for them, and re-layouts: 19.2 us -> 9.85 us  [the longest x4 5.41 us: exchange(): by_y[2:]]
    ppermute x82 -> x89, starting transfers between devices: 85.7 us -> 94.8 us  [send(): return lax.ppermute(value, BOTH, flip_perm(dp_bits, sp_bits))]
    convert_element_type x7 -> x5, local copies, waits for them, and re-layouts: 10.1 us -> 1.9 us  [the longest x3 1.76 us: layer(): keep_rows = live_frames.astype(F32).reshape(seqs, 1, length)]
    pallas_call x4 -> x8, Pallas kernels: 44.7 us -> 52.8 us  [flatten(): pl.pallas_call(kernel, grid_spec=pltpu.PrefetchScalarGridSpec(num_scalar_...]
    concatenate x15 -> x13, other arithmetic: 16.4 us -> 9.17 us  [the longest x4 3.69 us: exchange(): jnp.concatenate([send(by_x[:2], 2), send(by_y[2:], 1)])]
  transfers between devices with their start and end apart: 87 -> 94, of which waited for: 36 -> 27; matrix products, arithmetic and copies ran while one was open for 24% -> 24% of each run, Pallas kernels for 20% -> 23%
where the time goes in v3:
time: 757 us; the launch traced here: 746 us
  Pallas kernels  221 us (29%)
  matrix products  156 us (21%)
  starting transfers between devices  120 us (16%)
  waiting for transfers between devices  104 us (14%)
  local copies, waits for them, and re-layouts  79.5 us (11%)
  other arithmetic  63.5 us (8%)
    ppermute x89, waiting for transfers between devices, send(): return lax.ppermute(value, BOTH, flip_perm(dp_bits, sp_bits))  96.7 us
    ppermute x89, starting transfers between devices, send(): return lax.ppermute(value, BOTH, flip_perm(dp_bits, sp_bits))  94.8 us
    pallas_call x2, Pallas kernels, attend_back(): pl.pallas_call(attend_back_kernel, grid=(n, parts), in_specs=[own(0), own...  63.2 us
    dot_general x7, matrix products, dot_l(): lax.dot_general(a, b, (((0,), (0,)), ((), ())), preferred_element_type=F32)  53.9 us
    pallas_call x8, Pallas kernels, flatten(): pl.pallas_call(kernel, grid_spec=pltpu.PrefetchScalarGridSpec(num_scalar_...  52.8 us
    dot_general x7, matrix products, dot(): return jnp.dot(a, b, preferred_element_type=F32)  52.5 us
    pallas_call x7, Pallas kernels, unflatten(): pl.pallas_call(kernel, grid=(rows // step_rows,), in_specs=in_specs, out_...  51.8 us
    dot_general x7, matrix products, product_back(): lax.dot_general(grad_rows, weight, (((1,), (1,)), ((), ())), preferred_el...  49.9 us
  transfers between devices with their start and end apart: 94, of which 27 were waited for; matrix products, arithmetic and copies ran while one was open for 24% of the time, Pallas kernels for 23%

profile of v3, /device:TPU:0, one launch (start us, length us, event | category | flops | bytes accessed | tf_op | source)
XLA Modules:
  0.0 745.7 jit_solution(13488436416375465749)
XLA Ops:
  22.2 8.3 %collective-permute-done.4 = bf16[624,128]{1,0:T(8,128)(2,1)S(1)} collective-permute-done((bf16[624,128]{1,0:T(8,128)(2,1)S(1)}, bf16[624,128]{1,0:T(8,128)(2,1)S(1)}, u32[]{:S(2)}, u32[]{:S(2)}) %collective-permute-start.4) | collective-permute-done | bytes 159776 | tf_op jit(solution)/shard_map/ppermute | solution.py:169
  82.6 8.8 %unflatten.7 = bf16[768,2304]{1,0:T(8,128)(2,1)} custom-call(bf16[19968,128]{1,0:T(8,128)(2,1)} %bitcast.344), custom_call_target="tpu_custom_call" | custom-call | bytes 21233664 | tf_op jit(solution)/shard_map/unflatten/pallas_call | solution.py:360
  107.7 10.0 %fusion.6 = bf16[1200,2304]{1,0:T(8,128)(2,1)} fusion(bf16[768,2304]{1,0:T(8,128)(2,1)} %unflatten.7, f32[2304]{0:T(1024)S(1)} %fusion.43, f32[1200,768]{1,0:T(8,128)} %fusion.8, f32[768]{0:T(1024)S(1)} %get-tuple-element.367, f32[768]{0:T(1024)S(1)} %get-tuple-element.368), kind=kOutput, calls=%fused_computation.13 | convolution fusion | flops 4255027200 | bytes 12770304 | tf_op jit(solution)/shard_map/dot_general | solution.py:38
  117.7 15.0 %attend.2 = bf16[6,200,768]{2,1,0:T(8,128)(2,1)} custom-call(bf16[6,200,2304]{2,1,0:T(8,128)(2,1)} %bitcast.332, bf16[6,200,2304]{2,1,0:T(8,128)(2,1)} %bitcast.333, bf16[6,200,2304]{2,1,0:T(8,128)(2,1)} %bitcast.334, f32[1,200,200]{2,1,0:T(8,128)} %compare_convert_fusion.m_ref), custom_call_target="tpu_custom_call" | custom-call | flops 1474560000 | bytes 7372800 | tf_op jit(solution)/shard_map/attend/pallas_call | solution.py:131
  142.7 6.7 collective-permute-done.33
  149.4 10.9 %collective-permute-done.34 = bf16[2,624,128]{2,1,0:T(8,128)(2,1)S(1)} collective-permute-done((bf16[2,624,128]{2,1,0:T(8,128)(2,1)S(1)}, bf16[2,624,128]{2,1,0:T(8,128)(2,1)S(1)}, u32[]{:S(2)}, u32[]{:S(2)}) %collective-permute-start.34) | collective-permute-done | bytes 319520 | tf_op jit(solution)/shard_map/ppermute | solution.py:169
  218.1 8.6 %unflatten.10 = bf16[768,2304]{1,0:T(8,128)(2,1)} custom-call(bf16[19968,128]{1,0:T(8,128)(2,1)} %bitcast.350), custom_call_target="tpu_custom_call" | custom-call | bytes 21233664 | tf_op jit(solution)/shard_map/unflatten/pallas_call | solution.py:360
  242.8 11.9 %unflatten.12 = bf16[768,3072]{1,0:T(8,128)(2,1)} custom-call(bf16[19968,128]{1,0:T(8,128)(2,1)} %bitcast.358, bf16[19968,128]{1,0:T(8,128)(2,1)} %bitcast.352), custom_call_target="tpu_custom_call" | custom-call | bytes 28311552 | tf_op jit(solution)/shard_map/unflatten/pallas_call | solution.py:360
  254.7 11.1 %unflatten.13 = bf16[3072,768]{1,0:T(8,128)(2,1)} custom-call(bf16[19968,128]{1,0:T(8,128)(2,1)} %bitcast.353), custom_call_target="tpu_custom_call" | custom-call | bytes 28311552 | tf_op jit(solution)/shard_map/unflatten/pallas_call | solution.py:360
  275.5 6.8 fusion.7
  282.2 15.0 %attend.3 = bf16[6,200,768]{2,1,0:T(8,128)(2,1)} custom-call(bf16[6,200,2304]{2,1,0:T(8,128)(2,1)} %bitcast.338, bf16[6,200,2304]{2,1,0:T(8,128)(2,1)} %bitcast.339, bf16[6,200,2304]{2,1,0:T(8,128)(2,1)} %bitcast.340, f32[6,1,200]{2,1,0:T(1,128)} %reshape.498.m_ref), custom_call_target="tpu_custom_call" | custom-call | flops 1474560000 | bytes 7372800 | tf_op jit(solution)/shard_map/attend/pallas_call | solution.py:131
  301.4 11.9 %multiply_convert_fusion = (bf16[1200,3072]{1,0:T(8,128)(2,1)}, f32[1200,3072]{1,0:T(8,128)}) fusion(f32[3072]{0:T(1024)S(1)} %fusion.45, bf16[768,3072]{1,0:T(8,128)(2,1)S(1)} %bitcast.370, f32[1200,768]{1,0:T(8,128)S(1)} %get-tuple-element.427, f32[768]{0:T(1024)S(1)} %get-tuple-element.357, f32[768]{0:T(1024)S(1)} %get-tuple-element.356, ...), kind=kOutput, calls=%fused_computation.8 | convolution fusion | flops 5689036800 | bytes 30551424 | tf_op jit(solution)/shard_map/dot_general | solution.py:38
  313.3 15.3 %convert_reduce_fusion = (f32[3072]{0:T(1024)}, bf16[1200,3072]{1,0:T(8,128)(2,1)}) fusion(f32[1200,3072]{1,0:T(8,128)} %get-tuple-element.429, bf16[1200,768]{1,0:T(8,128)(2,1)S(1)} %copy-done.14, bf16[3072,768]{1,0:T(8,128)(2,1)S(1)} %bitcast.372), kind=kOutput, calls=%fused_computation.7 | convolution fusion | flops 5706544128 | bytes 28692480 | tf_op jit(solution)/shard_map/dot_general | solution.py:548
  328.6 10.1 %multiply_reduce_fusion.2 = (f32[768]{0:T(1024)S(1)}, f32[1200]{0:T(1024)S(1)}, f32[1200]{0:T(1024)S(1)}, f32[768]{0:T(1024)S(1)}, f32[1200,768]{1,0:T(8,128)S(1)}) fusion(f32[1200,768]{1,0:T(8,128)S(1)} %get-tuple-element.427, f32[1200]{0:T(1024)S(1)} %add_rsqrt_fusion, f32[1200]{0:T(1024)S(1)} %broadcast_multiply_fusion.7, ...), kind=kOutput, calls=%fused_computation.59 | convolution fusion | flops 5670600704 | bytes 19492608 | tf_op jit(solution)/shard_map/dot_general | solution.py:548
  346.9 9.7 %fusion.67.refs_0_.refs_1_ = f32[768,3072]{1,0:T(8,128)} fusion(bf16[1200,3072]{1,0:T(8,128)(2,1)S(1)} %bitcast.407, f32[1200,768]{1,0:T(8,128)S(1)} %get-tuple-element.427, f32[768]{0:T(1024)S(1)} %get-tuple-element.357, f32[768]{0:T(1024)S(1)} %get-tuple-element.356, f32[1200]{0:T(1024)S(1)} %add_rsqrt_fusion, f32[1200]{0:T(1024)S(1)} %broadcast_multiply_fusion.7), kind=kOutput, calls=%fused_computation.245 | convolution fusion | flops 5666918400 | bytes 20512128 | tf_op jit(solution)/shard_map/dot_general | solution.py:34
  356.6 32.0 %attend_back.2 = bf16[6,200,2304]{2,1,0:T(8,128)(2,1)} custom-call(bf16[6,200,2304]{2,1,0:T(8,128)(2,1)} %bitcast.341, bf16[6,200,2304]{2,1,0:T(8,128)(2,1)} %bitcast.342, bf16[6,200,2304]{2,1,0:T(8,128)(2,1)} %bitcast.343, f32[6,200,1]{2,1,0:T(8,128)} %reshape.515.m_ref, bf16[6,200,768]{2,1,0:T(8,128)(2,1)} %bitcast.380), custom_call_target="tpu_custom_call" | custom-call | flops 3686400000 | bytes 12902400 | tf_op jit(solution)/shard_map/attend_back/pallas_call | solution.py:149
  388.6 9.3 %fusion.26 = (f32[768]{0:T(1024)S(1)}, f32[1200]{0:T(1024)S(1)}, f32[1200]{0:T(1024)S(1)}, f32[768]{0:T(1024)S(1)}, f32[1200,768]{1,0:T(8,128)S(1)}) fusion(bf16[1200,768]{1,0:T(8,128)(2,1)S(1)} %reshape.469, f32[1200]{0:T(1024)S(1)} %add_rsqrt_fusion.1, f32[1200]{0:T(1024)S(1)} %broadcast_multiply_fusion.8, f32[768]{0:T(1024)S(1)} %get-tuple-element.359, ...), kind=kOutput, calls=%fused_computation.51 | convolution fusion | flops 4255944704 | bytes 14626560 | tf_op jit(solution)/shard_map/dot_general | solution.py:548
  414.9 11.3 %fusion.69.refs_1_ = f32[3072,768]{1,0:T(8,128)} fusion(bf16[1200,3072]{1,0:T(8,128)(2,1)} %get-tuple-element.428, bf16[1200,768]{1,0:T(8,128)(2,1)} %reshape.467), kind=kOutput, calls=%fused_computation.247 | convolution fusion | flops 5662310400 | bytes 18653184 | tf_op jit(solution)/shard_map/dot_general | solution.py:34
  432.5 11.0 %fusion.30 = bf16[1200,768]{1,0:T(8,128)(2,1)} fusion(f32[1200,768]{1,0:T(8,128)} %copy-done.2, bf16[1200,3072]{1,0:T(8,128)(2,1)} %get-tuple-element.428, bf16[3072,768]{1,0:T(8,128)(2,1)} %unflatten.13, f32[768]{0:T(1024)S(1)} %fusion.46), kind=kOutput, calls=%fused_computation.66 | convolution fusion | flops 5665075200 | bytes 17624064 | tf_op jit(solution)/shard_map/dot_general | solution.py:38
  443.5 6.6 flatten.10
  464.7 9.7 %fusion.64.refs_1_ = f32[768,2304]{1,0:T(8,128)} fusion(bf16[1200,2304]{1,0:T(8,128)(2,1)} %bitcast.363, bf16[1200,768]{1,0:T(8,128)(2,1)S(1)} %reshape.469, f32[768]{0:T(1024)S(1)} %copy-done.60, f32[768]{0:T(1024)S(1)} %get-tuple-element.359, f32[1200]{0:T(1024)S(1)} %add_rsqrt_fusion.1, f32[1200]{0:T(1024)S(1)} %broadcast_multiply_fusion.8), kind=kOutput, calls=%fused_computation.244 | convolution fusion | flops 4252262400 | bytes 14466432 | tf_op jit(solution)/shard_map/dot_general | solution.py:34
  506.5 6.7 flatten.13
  544.2 6.8 flatten.12
  552.1 31.3 %attend_back.3 = bf16[6,200,2304]{2,1,0:T(8,128)(2,1)} custom-call(bf16[6,200,2304]{2,1,0:T(8,128)(2,1)} %bitcast.335, bf16[6,200,2304]{2,1,0:T(8,128)(2,1)} %bitcast.336, bf16[6,200,2304]{2,1,0:T(8,128)(2,1)} %bitcast.337, f32[1,200,200]{2,1,0:T(8,128)} %compare_convert_fusion.m_ref, bf16[6,200,768]{2,1,0:T(8,128)(2,1)} %bitcast.377), custom_call_target="tpu_custom_call" | custom-call | flops 3686400000 | bytes 12902400 | tf_op jit(solution)/shard_map/attend_back/pallas_call | solution.py:149
  583.4 11.6 %fusion.42.refs_0_ = f32[768,2304]{1,0:T(8,128)} fusion(bf16[1200,2304]{1,0:T(8,128)(2,1)} %bitcast.359, f32[1200,768]{1,0:T(8,128)} %fusion.8, f32[768]{0:T(1024)S(1)} %copy-done.58, f32[768]{0:T(1024)S(1)} %copy-done.56), kind=kOutput, calls=%fused_computation.122 | convolution fusion | flops 4249497600 | bytes 16300032 | tf_op jit(solution)/shard_map/dot_general | solution.py:34
  609.0 7.8 %collective-permute-done.62 = bf16[624,128]{1,0:T(8,128)(2,1)S(1)} collective-permute-done((bf16[624,128]{1,0:T(8,128)(2,1)S(1)}, bf16[624,128]{1,0:T(8,128)(2,1)S(1)}, u32[]{:S(2)}, u32[]{:S(2)}) %collective-permute-start.62) | collective-permute-done | bytes 159776 | tf_op jit(solution)/shard_map/ppermute | solution.py:169
  619.0 10.4 %collective-permute-done.59 = bf16[624,128]{1,0:T(8,128)(2,1)S(1)} collective-permute-done((bf16[624,128]{1,0:T(8,128)(2,1)S(1)}, bf16[624,128]{1,0:T(8,128)(2,1)S(1)}, u32[]{:S(2)}, u32[]{:S(2)}) %collective-permute-start.59) | collective-permute-done | bytes 159776 | tf_op jit(solution)/shard_map/ppermute | solution.py:169
  630.9 7.0 multiply_reduce_fusion
  638.7 7.0 flatten.15
  659.5 6.9 flatten.14
  686.5 8.0 %collective-permute-done.71 = bf16[624,128]{1,0:T(8,128)(2,1)S(1)} collective-permute-done((bf16[624,128]{1,0:T(8,128)(2,1)S(1)}, bf16[624,128]{1,0:T(8,128)(2,1)S(1)}, u32[]{:S(2)}, u32[]{:S(2)}) %collective-permute-start.71) | collective-permute-done | bytes 159776 | tf_op jit(solution)/shard_map/ppermute | solution.py:169
  707.2 7.2 collective-permute-start.83
  (494 shorter events, 392.5 us)
Async XLA Ops:
  67.8 24.5 %collective-permute-start.20 = (bf16[4,624,128]{2,1,0:T(8,128)(2,1)}, bf16[4,624,128]{2,1,0:T(8,128)(2,1)}, u32[]{:S(2)}, u32[]{:S(2)}) collective-permute-start(bf16[4,624,128]{2,1,0:T(8,128)(2,1)} %pad_maximum_fusion.3.refs_0_), channel_id=1, source_target_pairs={{0,8},{1,9},{2,10},{3,11},{4,12},{5,13},{6,14},{7,15},{8,0},{9,1},... | collective-permute-start | bytes 1916936 | tf_op jit(solution)/shard_map/ppermute | solution.py:169
  68.5 23.9 %collective-permute-start.21 = (bf16[4,624,128]{2,1,0:T(8,128)(2,1)}, bf16[4,624,128]{2,1,0:T(8,128)(2,1)}, u32[]{:S(2)}, u32[]{:S(2)}) collective-permute-start(bf16[4,624,128]{2,1,0:T(8,128)(2,1)} %pad_maximum_fusion.3.refs_0_), channel_id=1, source_target_pairs={{0,16},{1,17},{2,18},{3,19},{4,20},{5,21},{6,22},{7,23},{8,24},{9,... | collective-permute-start | bytes 1916936 | tf_op jit(solution)/shard_map/ppermute | solution.py:169
  72.4 19.9 %collective-permute-start.22 = (bf16[624,128]{1,0:T(8,128)(2,1)S(1)}, bf16[624,128]{1,0:T(8,128)(2,1)S(1)}, u32[]{:S(2)}, u32[]{:S(2)}) collective-permute-start(bf16[624,128]{1,0:T(8,128)(2,1)S(1)} %get-tuple-element.221), channel_id=1, source_target_pairs={{0,2},{1,3},{2,0},{3,1},{4,6},{5,7},{6,4},{7,5},{8,10},{9,11},{10,... | collective-permute-start | bytes 479240 | tf_op jit(solution)/shard_map/ppermute | solution.py:169
  93.1 41.5 %collective-permute-start.27 = (bf16[4,624,128]{2,1,0:T(8,128)(2,1)S(1)}, bf16[4,624,128]{2,1,0:T(8,128)(2,1)}, u32[]{:S(2)}, u32[]{:S(2)}) collective-permute-start(bf16[4,624,128]{2,1,0:T(8,128)(2,1)S(1)} %pad_maximum_fusion.5.refs_0_), channel_id=1, source_target_pairs={{0,8},{1,9},{2,10},{3,11},{4,12},{5,13},{6,14},{7,15},{8,0},{9,1},... | collective-permute-start | bytes 1916936 | tf_op jit(solution)/shard_map/ppermute | solution.py:169
  94.6 40.0 %collective-permute-start.28 = (bf16[4,624,128]{2,1,0:T(8,128)(2,1)S(1)}, bf16[4,624,128]{2,1,0:T(8,128)(2,1)}, u32[]{:S(2)}, u32[]{:S(2)}) collective-permute-start(bf16[4,624,128]{2,1,0:T(8,128)(2,1)S(1)} %pad_maximum_fusion.5.refs_0_), channel_id=1, source_target_pairs={{0,16},{1,17},{2,18},{3,19},{4,20},{5,21},{6,22},{7,23},{8,24},{9,... | collective-permute-start | bytes 1916936 | tf_op jit(solution)/shard_map/ppermute | solution.py:169
  98.0 34.7 %collective-permute-start.25 = (bf16[2,624,128]{2,1,0:T(8,128)(2,1)}, bf16[2,624,128]{2,1,0:T(8,128)(2,1)S(1)}, u32[]{:S(2)}, u32[]{:S(2)}) collective-permute-start(bf16[2,624,128]{2,1,0:T(8,128)(2,1)} %slice.274), channel_id=1, source_target_pairs={{0,16},{1,17},{2,18},{3,19},{4,20},{5,21},{6,22},{7,23},{8,24},{9,... | collective-permute-start | bytes 958472 | tf_op jit(solution)/shard_map/ppermute | solution.py:169
  100.0 32.7 %collective-permute-start.26 = (bf16[2,624,128]{2,1,0:T(8,128)(2,1)}, bf16[2,624,128]{2,1,0:T(8,128)(2,1)}, u32[]{:S(2)}, u32[]{:S(2)}) collective-permute-start(bf16[2,624,128]{2,1,0:T(8,128)(2,1)} %slice.275), channel_id=1, source_target_pairs={{0,8},{1,9},{2,10},{3,11},{4,12},{5,13},{6,14},{7,15},{8,0},{9,1},... | collective-permute-start | bytes 958472 | tf_op jit(solution)/shard_map/ppermute | solution.py:169
  102.8 90.2 %all-to-all-start = ((bf16[3,16,25,768]{3,2,0,1:T(8,128)(2,1)}), bf16[3,16,25,768]{3,2,0,1:T(8,128)(2,1)}, u32[]{:S(2)}, u32[]{:S(2)}) async-start(bf16[3,16,25,768]{3,2,0,1:T(8,128)(2,1)} %copy.29), calls=%async_computation | async-start | bytes 4718592 | tf_op jit(solution)/shard_map/all_to_all | solution.py:608
  136.5 23.8 %collective-permute-start.35 = (bf16[4,624,128]{2,1,0:T(8,128)(2,1)}, bf16[4,624,128]{2,1,0:T(8,128)(2,1)}, u32[]{:S(2)}, u32[]{:S(2)}) collective-permute-start(bf16[4,624,128]{2,1,0:T(8,128)(2,1)} %pad_maximum_fusion.7.refs_0_), channel_id=1, source_target_pairs={{0,8},{1,9},{2,10},{3,11},{4,12},{5,13},{6,14},{7,15},{8,0},{9,1},... | collective-permute-start | bytes 1916936 | tf_op jit(solution)/shard_map/ppermute | solution.py:169
  142.4 27.6 %collective-permute-start.36 = (bf16[4,624,128]{2,1,0:T(8,128)(2,1)}, bf16[4,624,128]{2,1,0:T(8,128)(2,1)}, u32[]{:S(2)}, u32[]{:S(2)}) collective-permute-start(bf16[4,624,128]{2,1,0:T(8,128)(2,1)} %pad_maximum_fusion.7.refs_0_), channel_id=1, source_target_pairs={{0,16},{1,17},{2,18},{3,19},{4,20},{5,21},{6,22},{7,23},{8,24},{9,... | collective-permute-start | bytes 1916936 | tf_op jit(solution)/shard_map/ppermute | solution.py:169
  142.7 27.3 %collective-permute-start.29 = (bf16[4,624,128]{2,1,0:T(8,128)(2,1)}, bf16[4,624,128]{2,1,0:T(8,128)(2,1)}, u32[]{:S(2)}, u32[]{:S(2)}) collective-permute-start(bf16[4,624,128]{2,1,0:T(8,128)(2,1)} %pad_maximum_fusion.3.refs_0_), channel_id=1, source_target_pairs={{0,1},{1,0},{2,3},{3,2},{4,5},{5,4},{6,7},{7,6},{8,9},{9,8},{10,11... | collective-permute-start | bytes 1916936 | tf_op jit(solution)/shard_map/ppermute | solution.py:169
  149.4 20.6 %collective-permute-start.30 = (bf16[4,624,128]{2,1,0:T(8,128)(2,1)}, bf16[4,624,128]{2,1,0:T(8,128)(2,1)}, u32[]{:S(2)}, u32[]{:S(2)}) collective-permute-start(bf16[4,624,128]{2,1,0:T(8,128)(2,1)} %collective-permute-done.20.refs_1_), channel_id=1, source_target_pairs={{0,1},{1,0},{2,3},{3,2},{4,5},{5,4},{6,7},{7,6},{8,9},{9,8},{10,11... | collective-permute-start | bytes 1916936 | tf_op jit(solution)/shard_map/ppermute | solution.py:169
  186.3 18.7 %collective-permute-start.37 = (bf16[4,624,128]{2,1,0:T(8,128)(2,1)S(1)}, bf16[4,624,128]{2,1,0:T(8,128)(2,1)}, u32[]{:S(2)}, u32[]{:S(2)}) collective-permute-start(bf16[4,624,128]{2,1,0:T(8,128)(2,1)S(1)} %pad_maximum_fusion.5.refs_0_), channel_id=1, source_target_pairs={{0,1},{1,0},{2,3},{3,2},{4,5},{5,4},{6,7},{7,6},{8,9},{9,8},{10,11... | collective-permute-start | bytes 1916936 | tf_op jit(solution)/shard_map/ppermute | solution.py:169
  186.3 18.7 %collective-permute-start.38 = (bf16[4,624,128]{2,1,0:T(8,128)(2,1)}, bf16[4,624,128]{2,1,0:T(8,128)(2,1)}, u32[]{:S(2)}, u32[]{:S(2)}) collective-permute-start(bf16[4,624,128]{2,1,0:T(8,128)(2,1)} %collective-permute-done.27.refs_1_), channel_id=1, source_target_pairs={{0,1},{1,0},{2,3},{3,2},{4,5},{5,4},{6,7},{7,6},{8,9},{9,8},{10,11... | collective-permute-start | bytes 1916936 | tf_op jit(solution)/shard_map/ppermute | solution.py:169
  209.2 59.9 %all-to-all-start.1 = ((bf16[3,16,25,768]{3,2,0,1:T(8,128)(2,1)}), bf16[3,16,25,768]{3,2,0,1:T(8,128)(2,1)S(1)}, u32[]{:S(2)}, u32[]{:S(2)}) async-start(bf16[3,16,25,768]{3,2,0,1:T(8,128)(2,1)} %copy.32), calls=%async_computation.1 | async-start | bytes 4718592 | tf_op jit(solution)/shard_map/all_to_all | solution.py:608
  214.5 22.4 %collective-permute-start.43 = (bf16[4,624,128]{2,1,0:T(8,128)(2,1)}, bf16[4,624,128]{2,1,0:T(8,128)(2,1)}, u32[]{:S(2)}, u32[]{:S(2)}) collective-permute-start(bf16[4,624,128]{2,1,0:T(8,128)(2,1)} %pad_maximum_fusion.7.refs_0_), channel_id=1, source_target_pairs={{0,1},{1,0},{2,3},{3,2},{4,5},{5,4},{6,7},{7,6},{8,9},{9,8},{10,11... | collective-permute-start | bytes 1916936 | tf_op jit(solution)/shard_map/ppermute | solution.py:169
  215.1 21.9 %collective-permute-start.44 = (bf16[4,624,128]{2,1,0:T(8,128)(2,1)}, bf16[4,624,128]{2,1,0:T(8,128)(2,1)}, u32[]{:S(2)}, u32[]{:S(2)}) collective-permute-start(bf16[4,624,128]{2,1,0:T(8,128)(2,1)} %collective-permute-done.35.refs_1_), channel_id=1, source_target_pairs={{0,1},{1,0},{2,3},{3,2},{4,5},{5,4},{6,7},{7,6},{8,9},{9,8},{10,11... | collective-permute-start | bytes 1916936 | tf_op jit(solution)/shard_map/ppermute | solution.py:169
  215.2 21.8 %collective-permute-start.45 = (bf16[4,624,128]{2,1,0:T(8,128)(2,1)}, bf16[4,624,128]{2,1,0:T(8,128)(2,1)}, u32[]{:S(2)}, u32[]{:S(2)}) collective-permute-start(bf16[4,624,128]{2,1,0:T(8,128)(2,1)} %collective-permute-done.36.refs_2_), channel_id=1, source_target_pairs={{0,1},{1,0},{2,3},{3,2},{4,5},{5,4},{6,7},{7,6},{8,9},{9,8},{10,11... | collective-permute-start | bytes 1916936 | tf_op jit(solution)/shard_map/ppermute | solution.py:169
  215.6 21.4 %collective-permute-start.46 = (bf16[4,624,128]{2,1,0:T(8,128)(2,1)S(1)}, bf16[4,624,128]{2,1,0:T(8,128)(2,1)}, u32[]{:S(2)}, u32[]{:S(2)}) collective-permute-start(bf16[4,624,128]{2,1,0:T(8,128)(2,1)S(1)} %copy-done.22), channel_id=1, source_target_pairs={{0,1},{1,0},{2,3},{3,2},{4,5},{5,4},{6,7},{7,6},{8,9},{9,8},{10,11... | collective-permute-start | bytes 1916936 | tf_op jit(solution)/shard_map/ppermute | solution.py:169
  402.1 72.3 %all-to-all-start.3 = ((bf16[3,2,200,768]{3,1,0,2:T(2,128)(2,1)}), bf16[3,2,200,768]{3,1,0,2:T(2,128)(2,1)}, u32[]{:S(2)}, u32[]{:S(2)}) async-start(bf16[3,2,200,768]{3,1,0,2:T(2,128)(2,1)} %copy.38), calls=%async_computation.3 | async-start | bytes 3686400 | tf_op jit(solution)/shard_map/all_to_all | solution.py:613
  413.8 72.2 %collective-permute-start.48 = (bf16[4,4,624,128]{3,2,1,0:T(8,128)(2,1)}, bf16[4,4,624,128]{3,2,1,0:T(8,128)(2,1)}, u32[]{:S(2)}, u32[]{:S(2)}) collective-permute-start(bf16[4,4,624,128]{3,2,1,0:T(8,128)(2,1)} %flatten.11), channel_id=1, source_target_pairs={{0,1},{1,0},{2,3},{3,2},{4,5},{5,4},{6,7},{7,6},{8,9},{9,8},{10,11... | collective-permute-start | bytes 7667720 | tf_op jit(solution)/shard_map/ppermute | solution.py:169
  432.2 53.8 %collective-permute-start.47 = (bf16[4,4,624,128]{3,2,1,0:T(8,128)(2,1)}, bf16[4,4,624,128]{3,2,1,0:T(8,128)(2,1)}, u32[]{:S(2)}, u32[]{:S(2)}) collective-permute-start(bf16[4,4,624,128]{3,2,1,0:T(8,128)(2,1)} %flatten.9), channel_id=1, source_target_pairs={{0,1},{1,0},{2,3},{3,2},{4,5},{5,4},{6,7},{7,6},{8,9},{9,8},{10,11... | collective-permute-start | bytes 7667720 | tf_op jit(solution)/shard_map/ppermute | solution.py:169
  474.4 49.1 %all-to-all-start.4 = ((bf16[3,2,200,768]{3,1,0,2:T(2,128)(2,1)}), bf16[3,2,200,768]{3,1,0,2:T(2,128)(2,1)}, u32[]{:S(2)}, u32[]{:S(2)}) async-start(bf16[3,2,200,768]{3,1,0,2:T(2,128)(2,1)} %copy.41), calls=%async_computation.4 | async-start | bytes 3686400 | tf_op jit(solution)/shard_map/all_to_all | solution.py:613
  513.2 70.1 %collective-permute-start.57 = (bf16[4,4,624,128]{3,2,1,0:T(8,128)(2,1)}, bf16[4,4,624,128]{3,2,1,0:T(8,128)(2,1)}, u32[]{:S(2)}, u32[]{:S(2)}) collective-permute-start(bf16[4,4,624,128]{3,2,1,0:T(8,128)(2,1)} %flatten.13), channel_id=1, source_target_pairs={{0,1},{1,0},{2,3},{3,2},{4,5},{5,4},{6,7},{7,6},{8,9},{9,8},{10,11... | collective-permute-start | bytes 7667720 | tf_op jit(solution)/shard_map/ppermute | solution.py:169
  536.1 47.3 %collective-permute-start.56 = (bf16[4,624,128]{2,1,0:T(8,128)(2,1)}, bf16[4,624,128]{2,1,0:T(8,128)(2,1)}, u32[]{:S(2)}, u32[]{:S(2)}) collective-permute-start(bf16[4,624,128]{2,1,0:T(8,128)(2,1)} %pad_maximum_fusion.12), channel_id=1, source_target_pairs={{0,16},{1,17},{2,18},{3,19},{4,20},{5,21},{6,22},{7,23},{8,24},{9,... | collective-permute-start | bytes 1916936 | tf_op jit(solution)/shard_map/ppermute | solution.py:169
  537.2 46.1 %collective-permute-start.55 = (bf16[4,624,128]{2,1,0:T(8,128)(2,1)}, bf16[4,624,128]{2,1,0:T(8,128)(2,1)}, u32[]{:S(2)}, u32[]{:S(2)}) collective-permute-start(bf16[4,624,128]{2,1,0:T(8,128)(2,1)} %pad_maximum_fusion.11), channel_id=1, source_target_pairs={{0,8},{1,9},{2,10},{3,11},{4,12},{5,13},{6,14},{7,15},{8,0},{9,1},... | collective-permute-start | bytes 1916936 | tf_op jit(solution)/shard_map/ppermute | solution.py:169
  539.0 44.4 %collective-permute-start.54 = (bf16[4,624,128]{2,1,0:T(8,128)(2,1)}, bf16[4,624,128]{2,1,0:T(8,128)(2,1)}, u32[]{:S(2)}, u32[]{:S(2)}) collective-permute-start(bf16[4,624,128]{2,1,0:T(8,128)(2,1)} %pad_maximum_fusion.10), channel_id=1, source_target_pairs={{0,16},{1,17},{2,18},{3,19},{4,20},{5,21},{6,22},{7,23},{8,24},{9,... | collective-permute-start | bytes 1916936 | tf_op jit(solution)/shard_map/ppermute | solution.py:169
  541.6 41.7 %collective-permute-start.53 = (bf16[4,624,128]{2,1,0:T(8,128)(2,1)}, bf16[4,624,128]{2,1,0:T(8,128)(2,1)}, u32[]{:S(2)}, u32[]{:S(2)}) collective-permute-start(bf16[4,624,128]{2,1,0:T(8,128)(2,1)} %pad_maximum_fusion.9), channel_id=1, source_target_pairs={{0,8},{1,9},{2,10},{3,11},{4,12},{5,13},{6,14},{7,15},{8,0},{9,1},... | collective-permute-start | bytes 1916936 | tf_op jit(solution)/shard_map/ppermute | solution.py:169
  599.2 30.3 %collective-permute-start.64 = (bf16[2,624,128]{2,1,0:T(8,128)(2,1)S(1)}, bf16[2,624,128]{2,1,0:T(8,128)(2,1)S(1)}, u32[]{:S(2)}, u32[]{:S(2)}) collective-permute-start(bf16[2,624,128]{2,1,0:T(8,128)(2,1)S(1)} %get-tuple-element.380), channel_id=1, source_target_pairs={{0,8},{1,9},{2,10},{3,11},{4,12},{5,13},{6,14},{7,15},{8,0},{9,1},... | collective-permute-start | bytes 958472 | tf_op jit(solution)/shard_map/ppermute | solution.py:169
  599.8 29.6 %collective-permute-start.65 = (bf16[2,624,128]{2,1,0:T(8,128)(2,1)S(1)}, bf16[2,624,128]{2,1,0:T(8,128)(2,1)S(1)}, u32[]{:S(2)}, u32[]{:S(2)}) collective-permute-start(bf16[2,624,128]{2,1,0:T(8,128)(2,1)S(1)} %get-tuple-element.379), channel_id=1, source_target_pairs={{0,16},{1,17},{2,18},{3,19},{4,20},{5,21},{6,22},{7,23},{8,24},{9,... | collective-permute-start | bytes 958472 | tf_op jit(solution)/shard_map/ppermute | solution.py:169
  638.0 28.5 %collective-permute-start.69 = (f32[12,128]{1,0:T(8,128)S(1)}, f32[12,128]{1,0:T(8,128)S(1)}, u32[]{:S(2)}, u32[]{:S(2)}) collective-permute-start(f32[12,128]{1,0:T(8,128)S(1)} %pad_maximum_fusion.23), channel_id=1, source_target_pairs={{0,1},{1,0},{2,3},{3,2},{4,5},{5,4},{6,7},{7,6},{8,9},{9,8},{10,11... | collective-permute-start | bytes 18440 | tf_op jit(solution)/shard_map/ppermute | solution.py:169
  645.6 23.5 %collective-permute-start.68 = (bf16[4,4,624,128]{3,2,1,0:T(8,128)(2,1)}, bf16[4,4,624,128]{3,2,1,0:T(8,128)(2,1)}, u32[]{:S(2)}, u32[]{:S(2)}) collective-permute-start(bf16[4,4,624,128]{3,2,1,0:T(8,128)(2,1)} %flatten.15), channel_id=1, source_target_pairs={{0,1},{1,0},{2,3},{3,2},{4,5},{5,4},{6,7},{7,6},{8,9},{9,8},{10,11... | collective-permute-start | bytes 7667720 | tf_op jit(solution)/shard_map/ppermute | solution.py:169
  (133 other events, 1639.0 us)

commit v4 on v3

--- a/solution.py
+++ b/solution.py
@@ -612,7 +612,7 @@
     def to_places(value):
         return lax.all_to_all(
             value.reshape(micro, seqs // micro, length, d), "sp", split_axis=2, concat_axis=1, tiled=True
-        ).reshape(micro, clips, frames, places, d)
+        )
 
     x_low = inputs_now.reshape(tokens, d)
     masked = (cot_now * live_low).reshape(micro, clips * frames, places, d)
@@ -749,19 +749,20 @@
     grads[5], grads[6] = dot_l(o_t, da_t), row_sum(da_t)
     grads[2] = dot_l(h1, dqkv_t)
     if fast:
-        grads[2], dqkv_t, out = advance((r3, r2, r1), grads[2], dqkv_t, out)
+        grads[2], dqkv_t = advance((r1,), grads[2], dqkv_t)
         grads[0] = grads[1] = jnp.zeros((d,), F32)
         r0 = block_of(0)
         r0.stage()
-    back1, grad_tg, grad_tb = norm_back(hat1, scale1, tg, product_back(dqkv_t, w_qkv_t))
+    dh1 = product_back(dqkv_t, w_qkv_t)
+    back1, grad_tg, grad_tb = norm_back(hat1, scale1, tg, dh1)
     if fast:
         norm_sum = SumAll(jnp.concatenate([grad_tg, grad_tb]).reshape(-1, LANES))
         norm_sum.stage()
-        back1, out = advance((r1, r0, norm_sum), back1, out)
+        back1, out = advance((r3, r2, r1, r0, norm_sum), back1, out)
         (back1,) = advance((r1, r0, norm_sum), back1)
     else:
         grads[0], grads[1] = grad_tg, grad_tb
-    out = out * live_low
+    out = out.reshape(inputs.shape) * live_low
     input_grad = (dx1.astype(F32) + back1).astype(BF).reshape(inputs.shape)
 
     if fast:

time: 757 us -> 744 us (0.983)
  waiting for transfers between devices: 104 us -> 87.8 us
    ppermute x89, waiting for transfers between devices: 96.7 us -> 81 us  [send(): return lax.ppermute(value, BOTH, flip_perm(dp_bits, sp_bits))]
  transfers between devices with their start and end apart: 94 -> 94, of which waited for: 27 -> 25; matrix products, arithmetic and copies ran while one was open for 24% -> 25% of each run, Pallas kernels for 23% -> 24%
where the time goes in v4:
time: 744 us; the launch traced here: 733 us
  Pallas kernels  221 us (30%)
  matrix products  160 us (22%)
  starting transfers between devices  121 us (16%)
  waiting for transfers between devices  87.8 us (12%)
  local copies, waits for them, and re-layouts  79.5 us (11%)
  other arithmetic  62.3 us (8%)
    ppermute x89, starting transfers between devices, send(): return lax.ppermute(value, BOTH, flip_perm(dp_bits, sp_bits))  95.8 us
    ppermute x89, waiting for transfers between devices, send(): return lax.ppermute(value, BOTH, flip_perm(dp_bits, sp_bits))  81 us
    pallas_call x2, Pallas kernels, attend_back(): pl.pallas_call(attend_back_kernel, grid=(n, parts), in_specs=[own(0), own...  63.2 us
    dot_general x7, matrix products, dot_l(): lax.dot_general(a, b, (((0,), (0,)), ((), ())), preferred_element_type=F32)  54.1 us
    dot_general x7, matrix products, product_back(): lax.dot_general(grad_rows, weight, (((1,), (1,)), ((), ())), preferred_el...  53 us
    pallas_call x8, Pallas kernels, flatten(): pl.pallas_call(kernel, grid_spec=pltpu.PrefetchScalarGridSpec(num_scalar_...  52.8 us
    dot_general x7, matrix products, dot(): return jnp.dot(a, b, preferred_element_type=F32)  52.5 us
    pallas_call x7, Pallas kernels, unflatten(): pl.pallas_call(kernel, grid=(rows // step_rows,), in_specs=in_specs, out_...  51.8 us
  transfers between devices with their start and end apart: 94, of which 25 were waited for; matrix products, arithmetic and copies ran while one was open for 25% of the time, Pallas kernels for 24%

profile of v4, /device:TPU:0, one launch (start us, length us, event | category | flops | bytes accessed | tf_op | source)
XLA Modules:
  0.0 733.0 jit_solution(5259381919783026058)
XLA Ops:
  22.2 8.3 %collective-permute-done.4 = bf16[624,128]{1,0:T(8,128)(2,1)S(1)} collective-permute-done((bf16[624,128]{1,0:T(8,128)(2,1)S(1)}, bf16[624,128]{1,0:T(8,128)(2,1)S(1)}, u32[]{:S(2)}, u32[]{:S(2)}) %collective-permute-start.4) | collective-permute-done | bytes 159776 | tf_op jit(solution)/shard_map/ppermute | solution.py:169
  82.7 8.8 %unflatten.7 = bf16[768,2304]{1,0:T(8,128)(2,1)} custom-call(bf16[19968,128]{1,0:T(8,128)(2,1)} %bitcast.346), custom_call_target="tpu_custom_call" | custom-call | bytes 21233664 | tf_op jit(solution)/shard_map/unflatten/pallas_call | solution.py:360
  107.7 10.0 %fusion.6 = bf16[1200,2304]{1,0:T(8,128)(2,1)} fusion(bf16[768,2304]{1,0:T(8,128)(2,1)} %unflatten.7, f32[2304]{0:T(1024)S(1)} %fusion.43, f32[1200,768]{1,0:T(8,128)} %fusion.8, f32[768]{0:T(1024)S(1)} %get-tuple-element.365, f32[768]{0:T(1024)S(1)} %get-tuple-element.366), kind=kOutput, calls=%fused_computation.13 | convolution fusion | flops 4255027200 | bytes 12770304 | tf_op jit(solution)/shard_map/dot_general | solution.py:38
  117.7 15.0 %attend.2 = bf16[6,200,768]{2,1,0:T(8,128)(2,1)} custom-call(bf16[6,200,2304]{2,1,0:T(8,128)(2,1)} %bitcast.334, bf16[6,200,2304]{2,1,0:T(8,128)(2,1)} %bitcast.335, bf16[6,200,2304]{2,1,0:T(8,128)(2,1)} %bitcast.336, f32[1,200,200]{2,1,0:T(8,128)} %compare_convert_fusion.m_ref), custom_call_target="tpu_custom_call" | custom-call | flops 1474560000 | bytes 7372800 | tf_op jit(solution)/shard_map/attend/pallas_call | solution.py:131
  142.7 6.7 collective-permute-done.33
  149.4 10.9 %collective-permute-done.34 = bf16[2,624,128]{2,1,0:T(8,128)(2,1)S(1)} collective-permute-done((bf16[2,624,128]{2,1,0:T(8,128)(2,1)S(1)}, bf16[2,624,128]{2,1,0:T(8,128)(2,1)S(1)}, u32[]{:S(2)}, u32[]{:S(2)}) %collective-permute-start.34) | collective-permute-done | bytes 319520 | tf_op jit(solution)/shard_map/ppermute | solution.py:169
  218.1 8.6 %unflatten.10 = bf16[768,2304]{1,0:T(8,128)(2,1)} custom-call(bf16[19968,128]{1,0:T(8,128)(2,1)} %bitcast.352), custom_call_target="tpu_custom_call" | custom-call | bytes 21233664 | tf_op jit(solution)/shard_map/unflatten/pallas_call | solution.py:360
  242.8 12.0 %unflatten.12 = bf16[768,3072]{1,0:T(8,128)(2,1)} custom-call(bf16[19968,128]{1,0:T(8,128)(2,1)} %bitcast.360, bf16[19968,128]{1,0:T(8,128)(2,1)} %bitcast.354), custom_call_target="tpu_custom_call" | custom-call | bytes 28311552 | tf_op jit(solution)/shard_map/unflatten/pallas_call | solution.py:360
  254.7 11.2 %unflatten.13 = bf16[3072,768]{1,0:T(8,128)(2,1)} custom-call(bf16[19968,128]{1,0:T(8,128)(2,1)} %bitcast.355), custom_call_target="tpu_custom_call" | custom-call | bytes 28311552 | tf_op jit(solution)/shard_map/unflatten/pallas_call | solution.py:360
  275.4 6.7 fusion.7
  282.2 15.0 %attend.3 = bf16[6,200,768]{2,1,0:T(8,128)(2,1)} custom-call(bf16[6,200,2304]{2,1,0:T(8,128)(2,1)} %bitcast.340, bf16[6,200,2304]{2,1,0:T(8,128)(2,1)} %bitcast.341, bf16[6,200,2304]{2,1,0:T(8,128)(2,1)} %bitcast.342, f32[6,1,200]{2,1,0:T(1,128)} %reshape.501.m_ref), custom_call_target="tpu_custom_call" | custom-call | flops 1474560000 | bytes 7372800 | tf_op jit(solution)/shard_map/attend/pallas_call | solution.py:131
  301.4 11.9 %multiply_convert_fusion = (bf16[1200,3072]{1,0:T(8,128)(2,1)}, f32[1200,3072]{1,0:T(8,128)}) fusion(f32[3072]{0:T(1024)S(1)} %fusion.45, bf16[768,3072]{1,0:T(8,128)(2,1)S(1)} %bitcast.372, f32[1200,768]{1,0:T(8,128)S(1)} %get-tuple-element.425, f32[768]{0:T(1024)S(1)} %get-tuple-element.355, f32[768]{0:T(1024)S(1)} %get-tuple-element.354, ...), kind=kOutput, calls=%fused_computation.8 | convolution fusion | flops 5689036800 | bytes 30551424 | tf_op jit(solution)/shard_map/dot_general | solution.py:38
  313.3 15.4 %convert_reduce_fusion = (f32[3072]{0:T(1024)}, bf16[1200,3072]{1,0:T(8,128)(2,1)}) fusion(f32[1200,3072]{1,0:T(8,128)} %get-tuple-element.427, bf16[1200,768]{1,0:T(8,128)(2,1)S(1)} %copy-done.14, bf16[3072,768]{1,0:T(8,128)(2,1)S(1)} %bitcast.374), kind=kOutput, calls=%fused_computation.7 | convolution fusion | flops 5706544128 | bytes 28692480 | tf_op jit(solution)/shard_map/dot_general | solution.py:548
  328.7 10.1 %multiply_reduce_fusion.2 = (f32[768]{0:T(1024)S(1)}, f32[1200]{0:T(1024)S(1)}, f32[1200]{0:T(1024)S(1)}, f32[768]{0:T(1024)S(1)}, f32[1200,768]{1,0:T(8,128)S(1)}) fusion(f32[1200,768]{1,0:T(8,128)S(1)} %get-tuple-element.425, f32[1200]{0:T(1024)S(1)} %add_rsqrt_fusion, f32[1200]{0:T(1024)S(1)} %broadcast_multiply_fusion.6, ...), kind=kOutput, calls=%fused_computation.59 | convolution fusion | flops 5670600704 | bytes 19492608 | tf_op jit(solution)/shard_map/dot_general | solution.py:548
  346.9 9.9 %fusion.67.refs_0_.refs_1_ = f32[768,3072]{1,0:T(8,128)} fusion(bf16[1200,3072]{1,0:T(8,128)(2,1)S(1)} %bitcast.409, f32[1200,768]{1,0:T(8,128)S(1)} %get-tuple-element.425, f32[768]{0:T(1024)S(1)} %get-tuple-element.355, f32[768]{0:T(1024)S(1)} %get-tuple-element.354, f32[1200]{0:T(1024)S(1)} %add_rsqrt_fusion, f32[1200]{0:T(1024)S(1)} %broadcast_multiply_fusion.6), kind=kOutput, calls=%fused_computation.245 | convolution fusion | flops 5666918400 | bytes 20512128 | tf_op jit(solution)/shard_map/dot_general | solution.py:34
  356.8 32.0 %attend_back.2 = bf16[6,200,2304]{2,1,0:T(8,128)(2,1)} custom-call(bf16[6,200,2304]{2,1,0:T(8,128)(2,1)} %bitcast.343, bf16[6,200,2304]{2,1,0:T(8,128)(2,1)} %bitcast.344, bf16[6,200,2304]{2,1,0:T(8,128)(2,1)} %bitcast.345, f32[6,200,1]{2,1,0:T(8,128)} %reshape.518.m_ref, bf16[6,200,768]{2,1,0:T(8,128)(2,1)} %bitcast.382), custom_call_target="tpu_custom_call" | custom-call | flops 3686400000 | bytes 12902400 | tf_op jit(solution)/shard_map/attend_back/pallas_call | solution.py:149
  388.8 9.3 %fusion.26 = (f32[768]{0:T(1024)S(1)}, f32[1200]{0:T(1024)S(1)}, f32[1200]{0:T(1024)S(1)}, f32[768]{0:T(1024)S(1)}, f32[1200,768]{1,0:T(8,128)S(1)}) fusion(bf16[1200,768]{1,0:T(8,128)(2,1)S(1)} %reshape.471, f32[1200]{0:T(1024)S(1)} %add_rsqrt_fusion.1, f32[1200]{0:T(1024)S(1)} %broadcast_multiply_fusion.7, f32[768]{0:T(1024)S(1)} %get-tuple-element.357, ...), kind=kOutput, calls=%fused_computation.51 | convolution fusion | flops 4255944704 | bytes 14626560 | tf_op jit(solution)/shard_map/dot_general | solution.py:548
  407.4 6.5 flatten.11
  415.1 11.3 %fusion.69.refs_1_ = f32[3072,768]{1,0:T(8,128)} fusion(bf16[1200,3072]{1,0:T(8,128)(2,1)} %get-tuple-element.426, bf16[1200,768]{1,0:T(8,128)(2,1)} %reshape.469), kind=kOutput, calls=%fused_computation.247 | convolution fusion | flops 5662310400 | bytes 18653184 | tf_op jit(solution)/shard_map/dot_general | solution.py:34
  432.8 11.0 %fusion.30 = bf16[1200,768]{1,0:T(8,128)(2,1)} fusion(f32[1200,768]{1,0:T(8,128)} %copy-done.2, bf16[1200,3072]{1,0:T(8,128)(2,1)} %get-tuple-element.426, bf16[3072,768]{1,0:T(8,128)(2,1)} %unflatten.13, f32[768]{0:T(1024)S(1)} %fusion.46), kind=kOutput, calls=%fused_computation.66 | convolution fusion | flops 5665075200 | bytes 17624064 | tf_op jit(solution)/shard_map/dot_general | solution.py:38
  443.8 6.6 flatten.10
  450.4 6.3 flatten.8
  465.0 9.7 %fusion.64.refs_1_ = f32[768,2304]{1,0:T(8,128)} fusion(bf16[1200,2304]{1,0:T(8,128)(2,1)} %bitcast.365, bf16[1200,768]{1,0:T(8,128)(2,1)S(1)} %reshape.471, f32[768]{0:T(1024)S(1)} %copy-done.53, f32[768]{0:T(1024)S(1)} %get-tuple-element.357, f32[1200]{0:T(1024)S(1)} %add_rsqrt_fusion.1, f32[1200]{0:T(1024)S(1)} %broadcast_multiply_fusion.7), kind=kOutput, calls=%fused_computation.244 | convolution fusion | flops 4252262400 | bytes 14466432 | tf_op jit(solution)/shard_map/dot_general | solution.py:34
  506.8 6.8 flatten.13
  544.5 6.8 flatten.12
  552.4 31.2 %attend_back.3 = bf16[6,200,2304]{2,1,0:T(8,128)(2,1)} custom-call(bf16[6,200,2304]{2,1,0:T(8,128)(2,1)} %bitcast.337, bf16[6,200,2304]{2,1,0:T(8,128)(2,1)} %bitcast.338, bf16[6,200,2304]{2,1,0:T(8,128)(2,1)} %bitcast.339, f32[1,200,200]{2,1,0:T(8,128)} %compare_convert_fusion.m_ref, bf16[6,200,768]{2,1,0:T(8,128)(2,1)} %bitcast.379), custom_call_target="tpu_custom_call" | custom-call | flops 3686400000 | bytes 12902400 | tf_op jit(solution)/shard_map/attend_back/pallas_call | solution.py:149
  583.7 11.5 %fusion.42.refs_0_ = f32[768,2304]{1,0:T(8,128)} fusion(bf16[1200,2304]{1,0:T(8,128)(2,1)} %bitcast.361, f32[1200,768]{1,0:T(8,128)} %fusion.8, f32[768]{0:T(1024)S(1)} %copy-done.51, f32[768]{0:T(1024)S(1)} %copy-done.49), kind=kOutput, calls=%fused_computation.122 | convolution fusion | flops 4249497600 | bytes 16300032 | tf_op jit(solution)/shard_map/dot_general | solution.py:34
  612.0 6.8 flatten.15
  619.0 10.1 %multiply_reduce_fusion = (f32[1200]{0:T(1024)S(1)}, f32[768]{0:T(1024)S(1)}, f32[1200]{0:T(1024)S(1)}, f32[768]{0:T(1024)S(1)}, f32[1200,768]{1,0:T(8,128)S(1)}) fusion(f32[1200,768]{1,0:T(8,128)} %fusion.8, f32[768]{0:T(1024)S(1)} %copy-done.49, bf16[1200,2304]{1,0:T(8,128)(2,1)} %bitcast.362, bf16[768,2304]{1,0:T(8,128)(2,1)} %unflatten.7), kind=kOutput, calls=%fused_computation.56 | convolution fusion | flops 4253179904 | bytes 16460160 | tf_op jit(solution)/shard_map/dot_general | solution.py:548
  643.5 6.9 flatten.14
  675.0 7.3 collective-permute-done.71
  725.0 6.5 collective-permute-done.88
  (480 shorter events, 383.3 us)
Async XLA Ops:
  67.9 24.5 %collective-permute-start.20 = (bf16[4,624,128]{2,1,0:T(8,128)(2,1)}, bf16[4,624,128]{2,1,0:T(8,128)(2,1)}, u32[]{:S(2)}, u32[]{:S(2)}) collective-permute-start(bf16[4,624,128]{2,1,0:T(8,128)(2,1)} %pad_maximum_fusion.3.refs_0_), channel_id=1, source_target_pairs={{0,8},{1,9},{2,10},{3,11},{4,12},{5,13},{6,14},{7,15},{8,0},{9,1},... | collective-permute-start | bytes 1916936 | tf_op jit(solution)/shard_map/ppermute | solution.py:169
  68.5 23.9 %collective-permute-start.21 = (bf16[4,624,128]{2,1,0:T(8,128)(2,1)}, bf16[4,624,128]{2,1,0:T(8,128)(2,1)}, u32[]{:S(2)}, u32[]{:S(2)}) collective-permute-start(bf16[4,624,128]{2,1,0:T(8,128)(2,1)} %pad_maximum_fusion.3.refs_0_), channel_id=1, source_target_pairs={{0,16},{1,17},{2,18},{3,19},{4,20},{5,21},{6,22},{7,23},{8,24},{9,... | collective-permute-start | bytes 1916936 | tf_op jit(solution)/shard_map/ppermute | solution.py:169
  93.1 41.5 %collective-permute-start.27 = (bf16[4,624,128]{2,1,0:T(8,128)(2,1)S(1)}, bf16[4,624,128]{2,1,0:T(8,128)(2,1)}, u32[]{:S(2)}, u32[]{:S(2)}) collective-permute-start(bf16[4,624,128]{2,1,0:T(8,128)(2,1)S(1)} %pad_maximum_fusion.5.refs_0_), channel_id=1, source_target_pairs={{0,8},{1,9},{2,10},{3,11},{4,12},{5,13},{6,14},{7,15},{8,0},{9,1},... | collective-permute-start | bytes 1916936 | tf_op jit(solution)/shard_map/ppermute | solution.py:169
  94.6 40.0 %collective-permute-start.28 = (bf16[4,624,128]{2,1,0:T(8,128)(2,1)S(1)}, bf16[4,624,128]{2,1,0:T(8,128)(2,1)}, u32[]{:S(2)}, u32[]{:S(2)}) collective-permute-start(bf16[4,624,128]{2,1,0:T(8,128)(2,1)S(1)} %pad_maximum_fusion.5.refs_0_), channel_id=1, source_target_pairs={{0,16},{1,17},{2,18},{3,19},{4,20},{5,21},{6,22},{7,23},{8,24},{9,... | collective-permute-start | bytes 1916936 | tf_op jit(solution)/shard_map/ppermute | solution.py:169
  98.0 34.7 %collective-permute-start.25 = (bf16[2,624,128]{2,1,0:T(8,128)(2,1)}, bf16[2,624,128]{2,1,0:T(8,128)(2,1)S(1)}, u32[]{:S(2)}, u32[]{:S(2)}) collective-permute-start(bf16[2,624,128]{2,1,0:T(8,128)(2,1)} %slice.274), channel_id=1, source_target_pairs={{0,16},{1,17},{2,18},{3,19},{4,20},{5,21},{6,22},{7,23},{8,24},{9,... | collective-permute-start | bytes 958472 | tf_op jit(solution)/shard_map/ppermute | solution.py:169
  100.0 32.7 %collective-permute-start.26 = (bf16[2,624,128]{2,1,0:T(8,128)(2,1)}, bf16[2,624,128]{2,1,0:T(8,128)(2,1)}, u32[]{:S(2)}, u32[]{:S(2)}) collective-permute-start(bf16[2,624,128]{2,1,0:T(8,128)(2,1)} %slice.275), channel_id=1, source_target_pairs={{0,8},{1,9},{2,10},{3,11},{4,12},{5,13},{6,14},{7,15},{8,0},{9,1},... | collective-permute-start | bytes 958472 | tf_op jit(solution)/shard_map/ppermute | solution.py:169
  102.8 90.1 %all-to-all-start = ((bf16[3,16,25,768]{3,2,0,1:T(8,128)(2,1)}), bf16[3,16,25,768]{3,2,0,1:T(8,128)(2,1)}, u32[]{:S(2)}, u32[]{:S(2)}) async-start(bf16[3,16,25,768]{3,2,0,1:T(8,128)(2,1)} %copy.29), calls=%async_computation | async-start | bytes 4718592 | tf_op jit(solution)/shard_map/all_to_all | solution.py:608
  136.5 23.8 %collective-permute-start.35 = (bf16[4,624,128]{2,1,0:T(8,128)(2,1)}, bf16[4,624,128]{2,1,0:T(8,128)(2,1)}, u32[]{:S(2)}, u32[]{:S(2)}) collective-permute-start(bf16[4,624,128]{2,1,0:T(8,128)(2,1)} %pad_maximum_fusion.7.refs_0_), channel_id=1, source_target_pairs={{0,8},{1,9},{2,10},{3,11},{4,12},{5,13},{6,14},{7,15},{8,0},{9,1},... | collective-permute-start | bytes 1916936 | tf_op jit(solution)/shard_map/ppermute | solution.py:169
  142.4 27.6 %collective-permute-start.36 = (bf16[4,624,128]{2,1,0:T(8,128)(2,1)}, bf16[4,624,128]{2,1,0:T(8,128)(2,1)}, u32[]{:S(2)}, u32[]{:S(2)}) collective-permute-start(bf16[4,624,128]{2,1,0:T(8,128)(2,1)} %pad_maximum_fusion.7.refs_0_), channel_id=1, source_target_pairs={{0,16},{1,17},{2,18},{3,19},{4,20},{5,21},{6,22},{7,23},{8,24},{9,... | collective-permute-start | bytes 1916936 | tf_op jit(solution)/shard_map/ppermute | solution.py:169
  142.7 27.3 %collective-permute-start.29 = (bf16[4,624,128]{2,1,0:T(8,128)(2,1)}, bf16[4,624,128]{2,1,0:T(8,128)(2,1)}, u32[]{:S(2)}, u32[]{:S(2)}) collective-permute-start(bf16[4,624,128]{2,1,0:T(8,128)(2,1)} %pad_maximum_fusion.3.refs_0_), channel_id=1, source_target_pairs={{0,1},{1,0},{2,3},{3,2},{4,5},{5,4},{6,7},{7,6},{8,9},{9,8},{10,11... | collective-permute-start | bytes 1916936 | tf_op jit(solution)/shard_map/ppermute | solution.py:169
  149.4 20.6 %collective-permute-start.30 = (bf16[4,624,128]{2,1,0:T(8,128)(2,1)}, bf16[4,624,128]{2,1,0:T(8,128)(2,1)}, u32[]{:S(2)}, u32[]{:S(2)}) collective-permute-start(bf16[4,624,128]{2,1,0:T(8,128)(2,1)} %collective-permute-done.20.refs_1_), channel_id=1, source_target_pairs={{0,1},{1,0},{2,3},{3,2},{4,5},{5,4},{6,7},{7,6},{8,9},{9,8},{10,11... | collective-permute-start | bytes 1916936 | tf_op jit(solution)/shard_map/ppermute | solution.py:169
  209.2 59.9 %all-to-all-start.1 = ((bf16[3,16,25,768]{3,2,0,1:T(8,128)(2,1)}), bf16[3,16,25,768]{3,2,0,1:T(8,128)(2,1)S(1)}, u32[]{:S(2)}, u32[]{:S(2)}) async-start(bf16[3,16,25,768]{3,2,0,1:T(8,128)(2,1)} %copy.32), calls=%async_computation.1 | async-start | bytes 4718592 | tf_op jit(solution)/shard_map/all_to_all | solution.py:608
  214.5 22.5 %collective-permute-start.43 = (bf16[4,624,128]{2,1,0:T(8,128)(2,1)}, bf16[4,624,128]{2,1,0:T(8,128)(2,1)}, u32[]{:S(2)}, u32[]{:S(2)}) collective-permute-start(bf16[4,624,128]{2,1,0:T(8,128)(2,1)} %pad_maximum_fusion.7.refs_0_), channel_id=1, source_target_pairs={{0,1},{1,0},{2,3},{3,2},{4,5},{5,4},{6,7},{7,6},{8,9},{9,8},{10,11... | collective-permute-start | bytes 1916936 | tf_op jit(solution)/shard_map/ppermute | solution.py:169
  215.1 21.9 %collective-permute-start.44 = (bf16[4,624,128]{2,1,0:T(8,128)(2,1)}, bf16[4,624,128]{2,1,0:T(8,128)(2,1)}, u32[]{:S(2)}, u32[]{:S(2)}) collective-permute-start(bf16[4,624,128]{2,1,0:T(8,128)(2,1)} %collective-permute-done.35.refs_1_), channel_id=1, source_target_pairs={{0,1},{1,0},{2,3},{3,2},{4,5},{5,4},{6,7},{7,6},{8,9},{9,8},{10,11... | collective-permute-start | bytes 1916936 | tf_op jit(solution)/shard_map/ppermute | solution.py:169
  215.1 21.8 %collective-permute-start.45 = (bf16[4,624,128]{2,1,0:T(8,128)(2,1)}, bf16[4,624,128]{2,1,0:T(8,128)(2,1)}, u32[]{:S(2)}, u32[]{:S(2)}) collective-permute-start(bf16[4,624,128]{2,1,0:T(8,128)(2,1)} %collective-permute-done.36.refs_2_), channel_id=1, source_target_pairs={{0,1},{1,0},{2,3},{3,2},{4,5},{5,4},{6,7},{7,6},{8,9},{9,8},{10,11... | collective-permute-start | bytes 1916936 | tf_op jit(solution)/shard_map/ppermute | solution.py:169
  215.6 21.4 %collective-permute-start.46 = (bf16[4,624,128]{2,1,0:T(8,128)(2,1)S(1)}, bf16[4,624,128]{2,1,0:T(8,128)(2,1)}, u32[]{:S(2)}, u32[]{:S(2)}) collective-permute-start(bf16[4,624,128]{2,1,0:T(8,128)(2,1)S(1)} %copy-done.21), channel_id=1, source_target_pairs={{0,1},{1,0},{2,3},{3,2},{4,5},{5,4},{6,7},{7,6},{8,9},{9,8},{10,11... | collective-permute-start | bytes 1916936 | tf_op jit(solution)/shard_map/ppermute | solution.py:169
  402.3 72.4 %all-to-all-start.3 = ((bf16[3,2,200,768]{3,1,0,2:T(2,128)(2,1)}), bf16[3,2,200,768]{3,1,0,2:T(2,128)(2,1)}, u32[]{:S(2)}, u32[]{:S(2)}) async-start(bf16[3,2,200,768]{3,1,0,2:T(2,128)(2,1)} %copy.38), calls=%async_computation.3 | async-start | bytes 3686400 | tf_op jit(solution)/shard_map/all_to_all | solution.py:613
  413.9 72.3 %collective-permute-start.48 = (bf16[4,4,624,128]{3,2,1,0:T(8,128)(2,1)}, bf16[4,4,624,128]{3,2,1,0:T(8,128)(2,1)}, u32[]{:S(2)}, u32[]{:S(2)}) collective-permute-start(bf16[4,4,624,128]{3,2,1,0:T(8,128)(2,1)} %flatten.11), channel_id=1, source_target_pairs={{0,1},{1,0},{2,3},{3,2},{4,5},{5,4},{6,7},{7,6},{8,9},{9,8},{10,11... | collective-permute-start | bytes 7667720 | tf_op jit(solution)/shard_map/ppermute | solution.py:169
  432.4 53.8 %collective-permute-start.47 = (bf16[4,4,624,128]{3,2,1,0:T(8,128)(2,1)}, bf16[4,4,624,128]{3,2,1,0:T(8,128)(2,1)}, u32[]{:S(2)}, u32[]{:S(2)}) collective-permute-start(bf16[4,4,624,128]{3,2,1,0:T(8,128)(2,1)} %flatten.9), channel_id=1, source_target_pairs={{0,1},{1,0},{2,3},{3,2},{4,5},{5,4},{6,7},{7,6},{8,9},{9,8},{10,11... | collective-permute-start | bytes 7667720 | tf_op jit(solution)/shard_map/ppermute | solution.py:169
  474.7 49.1 %all-to-all-start.4 = ((bf16[3,2,200,768]{3,1,0,2:T(2,128)(2,1)}), bf16[3,2,200,768]{3,1,0,2:T(2,128)(2,1)}, u32[]{:S(2)}, u32[]{:S(2)}) async-start(bf16[3,2,200,768]{3,1,0,2:T(2,128)(2,1)} %copy.41), calls=%async_computation.4 | async-start | bytes 3686400 | tf_op jit(solution)/shard_map/all_to_all | solution.py:613
  513.6 70.1 %collective-permute-start.57 = (bf16[4,4,624,128]{3,2,1,0:T(8,128)(2,1)}, bf16[4,4,624,128]{3,2,1,0:T(8,128)(2,1)}, u32[]{:S(2)}, u32[]{:S(2)}) collective-permute-start(bf16[4,4,624,128]{3,2,1,0:T(8,128)(2,1)} %flatten.13), channel_id=1, source_target_pairs={{0,1},{1,0},{2,3},{3,2},{4,5},{5,4},{6,7},{7,6},{8,9},{9,8},{10,11... | collective-permute-start | bytes 7667720 | tf_op jit(solution)/shard_map/ppermute | solution.py:169
  536.4 47.3 %collective-permute-start.56 = (bf16[4,624,128]{2,1,0:T(8,128)(2,1)}, bf16[4,624,128]{2,1,0:T(8,128)(2,1)}, u32[]{:S(2)}, u32[]{:S(2)}) collective-permute-start(bf16[4,624,128]{2,1,0:T(8,128)(2,1)} %pad_maximum_fusion.12), channel_id=1, source_target_pairs={{0,16},{1,17},{2,18},{3,19},{4,20},{5,21},{6,22},{7,23},{8,24},{9,... | collective-permute-start | bytes 1916936 | tf_op jit(solution)/shard_map/ppermute | solution.py:169
  537.6 46.1 %collective-permute-start.55 = (bf16[4,624,128]{2,1,0:T(8,128)(2,1)}, bf16[4,624,128]{2,1,0:T(8,128)(2,1)}, u32[]{:S(2)}, u32[]{:S(2)}) collective-permute-start(bf16[4,624,128]{2,1,0:T(8,128)(2,1)} %pad_maximum_fusion.11), channel_id=1, source_target_pairs={{0,8},{1,9},{2,10},{3,11},{4,12},{5,13},{6,14},{7,15},{8,0},{9,1},... | collective-permute-start | bytes 1916936 | tf_op jit(solution)/shard_map/ppermute | solution.py:169
  539.3 44.4 %collective-permute-start.54 = (bf16[4,624,128]{2,1,0:T(8,128)(2,1)}, bf16[4,624,128]{2,1,0:T(8,128)(2,1)}, u32[]{:S(2)}, u32[]{:S(2)}) collective-permute-start(bf16[4,624,128]{2,1,0:T(8,128)(2,1)} %pad_maximum_fusion.10), channel_id=1, source_target_pairs={{0,16},{1,17},{2,18},{3,19},{4,20},{5,21},{6,22},{7,23},{8,24},{9,... | collective-permute-start | bytes 1916936 | tf_op jit(solution)/shard_map/ppermute | solution.py:169
  541.9 41.7 %collective-permute-start.53 = (bf16[4,624,128]{2,1,0:T(8,128)(2,1)}, bf16[4,624,128]{2,1,0:T(8,128)(2,1)}, u32[]{:S(2)}, u32[]{:S(2)}) collective-permute-start(bf16[4,624,128]{2,1,0:T(8,128)(2,1)} %pad_maximum_fusion.9), channel_id=1, source_target_pairs={{0,8},{1,9},{2,10},{3,11},{4,12},{5,13},{6,14},{7,15},{8,0},{9,1},... | collective-permute-start | bytes 1916936 | tf_op jit(solution)/shard_map/ppermute | solution.py:169
  602.6 28.6 %collective-permute-start.61 = (bf16[624,128]{1,0:T(8,128)(2,1)S(1)}, bf16[624,128]{1,0:T(8,128)(2,1)S(1)}, u32[]{:S(2)}, u32[]{:S(2)}) collective-permute-start(bf16[624,128]{1,0:T(8,128)(2,1)S(1)} %get-tuple-element.406), channel_id=1, source_target_pairs={{0,2},{1,3},{2,0},{3,1},{4,6},{5,7},{6,4},{7,5},{8,10},{9,11},{10,... | collective-permute-start | bytes 479240 | tf_op jit(solution)/shard_map/ppermute | solution.py:169
  602.6 30.3 %collective-permute-start.62 = (bf16[624,128]{1,0:T(8,128)(2,1)S(1)}, bf16[624,128]{1,0:T(8,128)(2,1)}, u32[]{:S(2)}, u32[]{:S(2)}) collective-permute-start(bf16[624,128]{1,0:T(8,128)(2,1)S(1)} %get-tuple-element.405), channel_id=1, source_target_pairs={{0,4},{1,5},{2,6},{3,7},{4,0},{5,1},{6,2},{7,3},{8,12},{9,13},{10,... | collective-permute-start | bytes 479240 | tf_op jit(solution)/shard_map/ppermute | solution.py:169
  604.6 30.1 %collective-permute-start.63 = (bf16[624,128]{1,0:T(8,128)(2,1)}, bf16[624,128]{1,0:T(8,128)(2,1)}, u32[]{:S(2)}, u32[]{:S(2)}) collective-permute-start(bf16[624,128]{1,0:T(8,128)(2,1)} %get-tuple-element.404), channel_id=1, source_target_pairs={{0,6},{1,7},{2,4},{3,5},{4,2},{5,3},{6,0},{7,1},{8,14},{9,15},{10,... | collective-permute-start | bytes 479240 | tf_op jit(solution)/shard_map/ppermute | solution.py:169
  610.0 28.5 %collective-permute-start.58 = (bf16[624,128]{1,0:T(8,128)(2,1)}, bf16[624,128]{1,0:T(8,128)(2,1)}, u32[]{:S(2)}, u32[]{:S(2)}) collective-permute-start(bf16[624,128]{1,0:T(8,128)(2,1)} %get-tuple-element.410), channel_id=1, source_target_pairs={{0,2},{1,3},{2,0},{3,1},{4,6},{5,7},{6,4},{7,5},{8,10},{9,11},{10,... | collective-permute-start | bytes 479240 | tf_op jit(solution)/shard_map/ppermute | solution.py:169
  618.9 32.2 %collective-permute-start.68 = (bf16[4,4,624,128]{3,2,1,0:T(8,128)(2,1)}, bf16[4,4,624,128]{3,2,1,0:T(8,128)(2,1)}, u32[]{:S(2)}, u32[]{:S(2)}) collective-permute-start(bf16[4,4,624,128]{3,2,1,0:T(8,128)(2,1)} %flatten.15), channel_id=1, source_target_pairs={{0,1},{1,0},{2,3},{3,2},{4,5},{5,4},{6,7},{7,6},{8,9},{9,8},{10,11... | collective-permute-start | bytes 7667720 | tf_op jit(solution)/shard_map/ppermute | solution.py:169
  660.3 21.9 %collective-permute-start.73 = (bf16[2,624,128]{2,1,0:T(8,128)(2,1)S(1)}, bf16[2,624,128]{2,1,0:T(8,128)(2,1)S(1)}, u32[]{:S(2)}, u32[]{:S(2)}) collective-permute-start(bf16[2,624,128]{2,1,0:T(8,128)(2,1)S(1)} %get-tuple-element.372), channel_id=1, source_target_pairs={{0,8},{1,9},{2,10},{3,11},{4,12},{5,13},{6,14},{7,15},{8,0},{9,1},... | collective-permute-start | bytes 958472 | tf_op jit(solution)/shard_map/ppermute | solution.py:169
  662.1 20.2 %collective-permute-start.74 = (bf16[2,624,128]{2,1,0:T(8,128)(2,1)S(1)}, bf16[2,624,128]{2,1,0:T(8,128)(2,1)S(1)}, u32[]{:S(2)}, u32[]{:S(2)}) collective-permute-start(bf16[2,624,128]{2,1,0:T(8,128)(2,1)S(1)} %get-tuple-element.371), channel_id=1, source_target_pairs={{0,16},{1,17},{2,18},{3,19},{4,20},{5,21},{6,22},{7,23},{8,24},{9,... | collective-permute-start | bytes 958472 | tf_op jit(solution)/shard_map/ppermute | solution.py:169
  (126 other events, 1557.6 us)
